TPU v7x, 32 devices: a whole 2x2x4 slice. The times are simulated.
32 devices in a mesh: seq: 8 (over z, x), head: 4 (over y, core).
Axes of the slice: x: 2, y: 2, z: 4, core: 2. Of those that a mesh axis runs over, the one named last changes fastest.
Arguments:
- lin_query: bfloat16 [2048, 4096], P('seq', 'head'), may hold values from -2 to 2
- lin_key: bfloat16 [2048, 4096], P('seq', 'head'), may hold values from -2 to 2
- lin_value: bfloat16 [2048, 4096], P('seq', 'head'), may hold values from -130 to 130
- log_decay: float32 [2048, 32], P('seq', 'head'), may hold values from -2 to 0
- gate_logits: bfloat16 [2048, 4096], P('seq', 'head'), may hold values from -6 to 6
- norm_gain: float32 [4096], P('head'), may hold values from 0.25 to 1.75
- soft_query: bfloat16 [2048, 4096], P('seq', 'head'), may hold values from -4 to 4
- soft_key: bfloat16 [2048, 4096], P('seq', 'head'), may hold values from -4 to 4
- soft_value: bfloat16 [2048, 4096], P('seq', 'head'), may hold values from -6 to 6
- doc_ids: int32 [2048], P('seq'), may hold values from 0 to 8, as said below
- doc_spans: int32 [9, 2], replicated, may hold values from 0 to 2048, as said below
Outputs:
- lin_out: bfloat16 [2048, 4096], P('seq', 'head')
- soft_out: bfloat16 [2048, 4096], P('seq', 'head')
Inputs may be any that keep to these rules, and one draw needn't show every extreme that they name: `doc_ids`: never falls; document d covers exactly the positions doc_spans[d, 0] to doc_spans[d, 1] - 1. `doc_spans`: row 0 starts at 0, each row ends where the next starts, the last ends at 2048; every document holds 1 to 768 positions, and one holds exactly that many.
All inputs are finite; a program needn't handle non-finite values.
Results may differ from a plain program's by a relative error of at most 0.0053.
Values may be sent and summed in bfloat16 or wider, within the bound.
No kernel may reach another device: no remote copies, remote signals or barrier semaphores. Data moves between devices by JAX's collectives and lax.ppermute only.
A program may use at most 128 MiB of HBM per device.

v0:
```python
import jax
import jax.numpy as jnp
from jax import lax
from jax.sharding import PartitionSpec as P

HALF_MODEL_HEADS = 32
HD = 128
SPAN = 3


def entering(part, axis, combine, identity):
    place = lax.axis_index(axis)
    gathered = jax.tree.map(lambda a: lax.all_gather(a, axis), part)
    state = jax.tree.map(lambda a, e: jnp.zeros_like(a) + jnp.asarray(e, a.dtype), part, identity)

    def one(step, state):
        return combine(
            state, jax.tree.map(lambda a: lax.dynamic_index_in_dim(a, step, 0, False), gathered)
        )

    return lax.fori_loop(0, place, one, state)


def from_behind(array, axis, by):
    devices = lax.axis_size(axis)
    pairs = [(i, i + by) for i in range(devices) if 0 <= i + by < devices]
    return lax.ppermute(array, axis, pairs)


def combine(former, latter):
    return (former[0] * latter[0], latter[0][:, None, None] * former[1] + latter[1])


def shards(
    lin_query,
    lin_key,
    lin_value,
    log_decay,
    gate_logits,
    norm_gain,
    soft_query,
    soft_key,
    soft_value,
    doc_ids,
    doc_spans,
):
    token_rows = lin_query.shape[0]
    feature_width = lin_query.shape[1]
    head_count = feature_width // HD
    block_base = lax.axis_index("seq") * token_rows
    positions = block_base + jnp.arange(token_rows, dtype=jnp.int32)
    numbers = jnp.arange(doc_spans.shape[0], dtype=jnp.int32)
    starts = jnp.sum(
        jnp.where(doc_ids[:, None] == numbers[None, :], doc_spans[None, :, 0], 0), axis=1
    )
    queries = lin_query.reshape(token_rows, head_count, HD)
    key_rows = lin_key.reshape(token_rows, head_count, HD)
    value_rows = lin_value.reshape(token_rows, head_count, HD)
    cumulative = jnp.cumsum(log_decay, axis=0)
    scores = jnp.einsum("thd,shd->hts", queries, key_rows, preferred_element_type=jnp.float32)
    spread = cumulative.T[:, :, None] - cumulative.T[:, None, :]
    allowed = (positions[None, :] <= positions[:, None]) & (positions[None, :] >= starts[:, None])
    weights = jnp.where(allowed[None], scores * jnp.exp(jnp.minimum(spread, 0.0)), 0.0).astype(
        jnp.bfloat16
    )
    inner_part = jnp.einsum("hts,shd->thd", weights, value_rows, preferred_element_type=jnp.float32)
    last_cumul = cumulative[-1]
    tail_weight = jnp.where(
        (positions >= starts[-1])[:, None],
        jnp.exp(jnp.minimum(last_cumul[None, :] - cumulative, 0.0)),
        0.0,
    )
    tail_key = (key_rows.astype(jnp.float32) * tail_weight[:, :, None]).astype(jnp.bfloat16)
    local_state = jnp.einsum(
        "shd,she->hde", tail_key, value_rows, preferred_element_type=jnp.float32
    )
    local_decay = jnp.where(starts[-1] < block_base, jnp.exp(last_cumul), 0.0)
    entry_scale = jnp.where((starts < block_base)[:, None], jnp.exp(cumulative), 0.0)
    identity = (jnp.ones_like(local_decay), jnp.zeros_like(local_state))
    carried = entering((local_decay, local_state), "seq", combine, identity)[1]
    cross_part = (
        jnp.einsum(
            "thd,hde->the",
            queries,
            carried.astype(jnp.bfloat16),
            preferred_element_type=jnp.float32,
        )
        * entry_scale[:, :, None]
    )
    mixture = inner_part + cross_part
    squares = jnp.sum(mixture * mixture, axis=(1, 2))
    norm_total = lax.psum(squares, "head")
    norm_scale = lax.rsqrt(norm_total / (HALF_MODEL_HEADS * HD) + 1e-06)
    lin_out = (
        mixture.reshape(token_rows, feature_width)
        * norm_scale[:, None]
        * norm_gain[None, :]
        * jax.nn.sigmoid(gate_logits.astype(jnp.float32))
    ).astype(jnp.bfloat16)
    key_parts = [soft_key]
    value_parts = [soft_value]
    for distance in range(1, SPAN + 1):
        earlier = from_behind((soft_key, soft_value), "seq", distance)
        key_parts.insert(0, earlier[0])
        value_parts.insert(0, earlier[1])
    all_keys = jnp.concatenate(key_parts, axis=0)
    all_values = jnp.concatenate(value_parts, axis=0)
    span_rows = all_keys.shape[0]
    key_pos = block_base + token_rows - span_rows + jnp.arange(span_rows, dtype=jnp.int32)
    soft_queries = soft_query.reshape(token_rows, head_count, HD)
    logits = jnp.einsum(
        "thd,shd->hts",
        soft_queries,
        all_keys.reshape(span_rows, head_count, HD),
        preferred_element_type=jnp.float32,
    ) * HD ** (-0.5)
    visible = (key_pos[None, :] >= starts[:, None]) & (key_pos[None, :] <= positions[:, None])
    logits = jnp.where(visible[None], logits, -jnp.inf)
    row_max = jnp.max(logits, axis=2, keepdims=True)
    soft_weights = jnp.exp(logits - row_max)
    soft_total = jnp.sum(soft_weights, axis=2)
    attended = jnp.einsum(
        "hts,shd->thd",
        soft_weights.astype(jnp.bfloat16),
        all_values.reshape(span_rows, head_count, HD),
        preferred_element_type=jnp.float32,
    )
    soft_out = (
        (attended / soft_total.T[:, :, None])
        .reshape(token_rows, feature_width)
        .astype(jnp.bfloat16)
    )
    return (lin_out, soft_out)


def solution(mesh):
    in_specs = (
        P("seq", "head"),
        P("seq", "head"),
        P("seq", "head"),
        P("seq", "head"),
        P("seq", "head"),
        P("head"),
        P("seq", "head"),
        P("seq", "head"),
        P("seq", "head"),
        P("seq"),
        P(),
    )
    out_specs = (P("seq", "head"), P("seq", "head"))
    return jax.shard_map(shards, mesh=mesh, in_specs=in_specs, out_specs=out_specs, check_vma=False)
```

profile of v0, /device:TPU:30, one launch (start us, length us, event | category | flops | bytes accessed | tf_op | source)
XLA Modules:
  0.0 212.4 jit_solution(500775631223508674)
XLA Ops:
  7.2 0.0 copy-start
  7.2 0.0 copy-start.3
  7.2 0.0 all-gather.4.cloned.1.call-start
  7.2 0.8 slice_bitcast_fusion
  8.0 0.8 select_reduce_fusion
  8.8 0.6 slice.19
  9.4 0.7 broadcast_compare_fusion
  10.7 1.3 reduce-window.6
  11.9 0.2 slice_reduce_fusion
  12.1 1.2 copy.96
  13.4 0.1 exponential_select_fusion
  13.4 0.2 slice_reduce_fusion.1
  13.6 0.1 exponential_select_fusion.1
  13.7 2.1 %fusion.22 = f32[8,128,128]{2,1,0:T(8,128)} fusion(bf16[256,8,128]{0,2,1:T(8,128)(2,1)S(1)} %bitcast.97, f32[256,8]{0,1:T(8,128)S(1)} %exponential_select_fusion.1, bf16[256,1024]{1,0:T(8,128)(2,1)} %param.15), kind=kOutput, calls=%fused_computation.30 | convolution fusion | flops 67895296 | bytes 1581056 | tf_op jit(solution)/shard_map/shd,she->hde/dot_general | solution.py:74
  15.9 0.0 all-gather.4.cloned.1.call-update
  15.9 2.1 copy.85
  17.9 1.3 collective-permute-start.3
  19.2 1.3 collective-permute-start.4
  20.5 1.3 collective-permute-start
  21.8 1.3 collective-permute-start.1
  23.1 1.3 collective-permute-start.2
  24.4 136.3 %all-gather.1 = f32[8,1,8]{2,1,0:T(1,128)S(1)} all-gather(f32[1,1,8]{2,1,0:T(1,128)S(1)} %bitcast.106), channel_id=1, replica_groups=mesh['seq'=8,'head'=4] {'seq'}, dimensions={0}, use_global_device_ids=true | all-gather | bytes 288 | tf_op jit(solution)/shard_map/all_gather | solution.py:13
  160.7 0.1 compare_and_fusion.1
  160.9 0.1 add_bitcast_fusion.1
  160.9 1.3 collective-permute-start.5
  162.2 0.3 compare_and_fusion
  162.5 0.8 copy-done.5
  163.3 1.7 pad_maximum_fusion
  165.0 2.6 %copy.84 = bf16[1024,1024]{0,1:T(8,128)(2,1)} copy(bf16[1024,1024]{1,0:T(8,128)(2,1)S(1)} %pad_maximum_fusion) | data formatting | bytes 4194304 | tf_op jit(solution)/shard_map/concatenate | solution.py:107
  167.6 6.7 %collective-permute-done.5 = bf16[256,1024]{0,1:T(8,128)(2,1)} collective-permute-done((bf16[256,1024]{0,1:T(8,128)(2,1)}, bf16[256,1024]{0,1:T(8,128)(2,1)}, u32[]{:S(2)}, u32[]{:S(2)}) %collective-permute-start.5) | collective-permute-done | bytes 524320 | tf_op jit(solution)/shard_map/ppermute | solution.py:27
  174.4 1.8 pad_maximum_fusion.1
  176.2 1.7 fusion.2
  177.9 1.7 fusion
  179.6 2.2 %divide_convert_fusion = bf16[256,8,128]{0,2,1:T(8,128)(2,1)S(1)} fusion(bf16[1024,8,128]{0,2,1:T(8,128)(2,1)S(1)} %bitcast.99, f32[8,1024,256]{2,1,0:T(8,128)S(1)} %get-tuple-element.74, f32[8,256]{1,0:T(8,128)S(1)} %get-tuple-element.73, pred[256,1024]{0,1:T(8,128)(4,1)S(1)} %compare_and_fusion, f32[256,8]{0,1:T(8,128)S(1)} %bitcast.104), kind=kOutput, calls=%fused_computation.21 | convolution fusion | flops 545783808 | bytes 11288576 | tf_op jit(solution)/shard_map/hts,shd->thd/dot_general | solution.py:122
  181.8 1.0 copy.92
  182.9 8.7 %while.12 = (s32[]{:T(128)}, f32[8,128,128]{2,1,0:T(8,128)S(1)}, s32[]{:T(128)}, f32[8,8]{1,0:T(8,128)S(1)}, f32[8,8,128,128]{3,2,1,0:T(8,128)}, /*index=5*/s32[]{:T(128)}, s32[]{:T(128)}, s32[]{:T(128)}) while((s32[]{:T(128)}, f32[8,128,128]{2,1,0:T(8,128)S(1)}, s32[]{:T(128)}, f32[8,8]{1,0:T(8,128)S(1)}, f32[8,8,128,128]{3,2,1,0:T(8,128)}, ...), condition=%wide.region_4.5_spmd, body=%wide.region_3.4_spmd.sunk | while | flops 262149 | bytes 1573087 | solution.py:21
  182.9 1.2 bitcast_add_fusion.2
  184.2 1.2 bitcast_add_fusion.2
  185.4 1.2 bitcast_add_fusion.2
  186.7 1.2 bitcast_add_fusion.2
  187.9 1.2 bitcast_add_fusion.2
  189.1 1.2 bitcast_add_fusion.2
  190.4 1.2 bitcast_add_fusion.2
  191.6 1.4 fusion.12
  193.0 2.9 %multiply_reduce_fusion = (f32[256]{0:T(256)S(1)}, f32[256,8,128]{0,2,1:T(8,128)}) fusion(f32[256,8,128]{0,2,1:T(8,128)S(1)} %fusion.12, bf16[256,8,128]{0,2,1:T(8,128)(2,1)S(1)} %bitcast.98, f32[8,256]{1,0:T(8,128)S(1)} %add_bitcast_fusion.1, pred[256,256]{1,0:T(8,128)(4,1)S(1)} %compare_and_fusion.1, bf16[256,1024]{1,0:T(8,128)(2,1)S(1)} %copy-done.2, ...), kind=kOutput, calls=%fused_computation.23 | convolution fusion | flops 271843072 | bytes 3744768 | tf_op jit(solution)/shard_map/hts,shd->thd/dot_general | solution.py:66
  195.9 1.6 copy.83
  197.5 5.9 %psum.7 = f32[256]{0:T(256)S(1)} all-reduce(f32[256]{0:T(256)S(1)} %get-tuple-element.71), channel_id=1, replica_groups=mesh['seq'=8,'head'=4] {'head'}, use_global_device_ids=true, to_apply=%region_6.7 | all-reduce | flops 256 | bytes 2048 | tf_op jit(solution)/shard_map/psum | solution.py:92
  203.4 2.2 %multiply_convert_fusion = bf16[256,1024]{1,0:T(8,128)(2,1)} fusion(bf16[256,1024]{1,0:T(8,128)(2,1)} %param.17, f32[256,1024]{1,0:T(8,128)S(1)} %copy.83, f32[1024]{0:T(1024)S(1)} %copy-done.6, f32[256]{0:T(256)S(1)} %add_rsqrt_fusion), kind=kLoop, calls=%fused_computation.22 | loop fusion | flops 2097152 | bytes 2102272 | tf_op jit(solution)/shard_map/convert_element_type | solution.py:99
  (30 shorter events, 0.2 us)
Async XLA Ops:
  7.2 169.0 %copy-start = (bf16[256,1024]{1,0:T(8,128)(2,1)S(1)}, bf16[256,1024]{1,0:T(8,128)(2,1)}, u32[]{:S(2)}) copy-start(bf16[256,1024]{1,0:T(8,128)(2,1)} %param.19) | copy-start | bytes 1572868
  7.2 13.3 %copy-start.3 = (bf16[256,1024]{1,0:T(8,128)(2,1)S(1)}, bf16[256,1024]{1,0:T(8,128)(2,1)}, u32[]{:S(2)}) copy-start(bf16[256,1024]{1,0:T(8,128)(2,1)} %param.21) | copy-start | bytes 1572868
  7.2 175.6 %all-gather.4.cloned.1.call-start = ((), (), s32[]{:S(2)}) async-start(), calls=%async_computation | async-start | bytes 4718592 | tf_op jit(solution)/shard_map/all_gather | solution.py:13
  17.9 149.7 %collective-permute-start.3 = (bf16[256,1024]{0,1:T(8,128)(2,1)}, bf16[256,1024]{0,1:T(8,128)(2,1)}, u32[]{:S(2)}, u32[]{:S(2)}) collective-permute-start(bf16[256,1024]{0,1:T(8,128)(2,1)} %copy.85), channel_id=1, source_target_pairs={{0,12},{4,16},{8,20},{12,24},{16,28},{1,13},{5,17},{9,21},{13,25},... | collective-permute-start | bytes 1572872 | tf_op jit(solution)/shard_map/ppermute | solution.py:27
  19.2 148.4 %collective-permute-start.4 = (bf16[256,1024]{0,1:T(8,128)(2,1)}, bf16[256,1024]{0,1:T(8,128)(2,1)}, u32[]{:S(2)}, u32[]{:S(2)}) collective-permute-start(bf16[256,1024]{0,1:T(8,128)(2,1)} %copy.85), channel_id=1, source_target_pairs={{0,8},{4,12},{8,16},{12,20},{16,24},{20,28},{1,9},{5,13},{9,17},{1... | collective-permute-start | bytes 1572872 | tf_op jit(solution)/shard_map/ppermute | solution.py:27
  20.5 140.4 %collective-permute-start = (bf16[256,1024]{1,0:T(8,128)(2,1)S(1)}, bf16[256,1024]{1,0:T(8,128)(2,1)S(1)}, u32[]{:S(2)}, u32[]{:S(2)}) collective-permute-start(bf16[256,1024]{1,0:T(8,128)(2,1)S(1)} %copy-done.3), channel_id=1, source_target_pairs={{0,12},{4,16},{8,20},{12,24},{16,28},{1,13},{5,17},{9,21},{13,25},... | collective-permute-start | bytes 1572872 | tf_op jit(solution)/shard_map/ppermute | solution.py:27
  21.8 140.7 %collective-permute-start.1 = (bf16[256,1024]{1,0:T(8,128)(2,1)S(1)}, bf16[256,1024]{1,0:T(8,128)(2,1)S(1)}, u32[]{:S(2)}, u32[]{:S(2)}) collective-permute-start(bf16[256,1024]{1,0:T(8,128)(2,1)S(1)} %copy-done.3), channel_id=1, source_target_pairs={{0,8},{4,12},{8,16},{12,20},{16,24},{20,28},{1,9},{5,13},{9,17},{1... | collective-permute-start | bytes 1572872 | tf_op jit(solution)/shard_map/ppermute | solution.py:27
  23.1 140.2 %collective-permute-start.2 = (bf16[256,1024]{1,0:T(8,128)(2,1)S(1)}, bf16[256,1024]{1,0:T(8,128)(2,1)}, u32[]{:S(2)}, u32[]{:S(2)}) collective-permute-start(bf16[256,1024]{1,0:T(8,128)(2,1)S(1)} %copy-done.3), channel_id=1, source_target_pairs={{0,4},{4,8},{8,12},{12,16},{16,20},{20,24},{24,28},{1,5},{5,9},{9,... | collective-permute-start | bytes 1572872 | tf_op jit(solution)/shard_map/ppermute | solution.py:27
  160.9 1.6 copy-start.4
  160.9 13.4 %collective-permute-start.5 = (bf16[256,1024]{0,1:T(8,128)(2,1)}, bf16[256,1024]{0,1:T(8,128)(2,1)}, u32[]{:S(2)}, u32[]{:S(2)}) collective-permute-start(bf16[256,1024]{0,1:T(8,128)(2,1)} %copy.85), channel_id=1, source_target_pairs={{0,4},{4,8},{8,12},{12,16},{16,20},{20,24},{24,28},{1,5},{5,9},{9,... | collective-permute-start | bytes 1572872 | tf_op jit(solution)/shard_map/ppermute | solution.py:27
  162.5 0.8 copy-start.5
  177.9 1.7 copy-start.1
  182.9 10.1 %copy-start.2 = (bf16[256,1024]{1,0:T(8,128)(2,1)S(1)}, bf16[256,1024]{1,0:T(8,128)(2,1)}, u32[]{:S(2)}) copy-start(bf16[256,1024]{1,0:T(8,128)(2,1)} %param.15) | copy-start | bytes 1572868
  193.0 10.4 %copy-start.6 = (f32[1024]{0:T(1024)S(1)}, f32[1024]{0:T(1024)}, u32[]{:S(2)}) copy-start(f32[1024]{0:T(1024)} %param.18) | copy-start | bytes 12292
Sparse Core Ops, SparseCore 0:
  16.0 114.9 all-gather.3
where the time goes:
time: 213 us; the launch traced here: 212 us
  blocking collectives  142 us (67%)
  other arithmetic  19.3 us (9%)
  between operations  14.9 us (7%)
  local copies, waits for them, and re-layouts  10.9 us (5%)
  matrix products  10.4 us (5%)
  starting transfers between devices  7.77 us (4%)
  waiting for transfers between devices  6.78 us (3%)
    all_gather x1, blocking collectives, entering(): gathered = jax.tree.map(lambda a: lax.all_gather(a, axis), part)  136 us
    add x7, other arithmetic, combine(): latter[0][:, None, None] * former[1] + latter[1]  8.38 us
    ppermute x6, starting transfers between devices, from_behind(): return lax.ppermute(array, axis, pairs)  7.73 us
    ppermute x6, waiting for transfers between devices, from_behind(): return lax.ppermute(array, axis, pairs)  6.76 us
    psum x1, blocking collectives, shards(): norm_total = lax.psum(squares, 'head')  5.89 us
  transfers between devices with their start and end apart: 7, of which 1 were waited for; matrix products, arithmetic and copies ran while one was open for 7% of the time, Pallas kernels for 0%

commit v1 on v0

v1 whole, which is shorter than its diff:
```python
import functools

import jax
import jax.numpy as jnp
from jax import lax
from jax.experimental import pallas as pl
from jax.experimental.pallas import tpu as pltpu
from jax.sharding import PartitionSpec as P

HALF_MODEL_HEADS = 32
HD = 128
NEG = -1e30
SOFT_SCALE = HD ** (-0.5) * 1.4426950408889634
F32 = jnp.float32
BF16 = jnp.bfloat16
VMEM_LIMIT = 48 * 1024 * 1024


def dot(a, b, dims, precision=None):
    return lax.dot_general(a, b, (dims, ((), ())), precision=precision, preferred_element_type=F32)


def row_starts(spans_ref, rows, base):
    positions = base + lax.broadcasted_iota(jnp.int32, (rows, 1), 0)

    def one(d, starts):
        first = spans_ref[d, 0]
        return jnp.where(positions >= first, jnp.maximum(starts, first), starts)

    docs = spans_ref.shape[0]
    return lax.fori_loop(0, docs, one, jnp.zeros((rows, 1), jnp.int32), unroll=docs <= 16), positions


def last_start(spans_ref, last):
    def one(d, start):
        first = spans_ref[d, 0]
        return jnp.where(first <= last, jnp.maximum(start, first), start)

    docs = spans_ref.shape[0]
    return lax.fori_loop(0, docs, one, jnp.int32(0), unroll=docs <= 16)


def split3(x):
    high = x.astype(BF16)
    rest = x - high.astype(F32)
    middle = rest.astype(BF16)
    return high, middle, (rest - middle.astype(F32)).astype(BF16)


def running_sums(decay):
    rows = decay.shape[0]
    r = lax.broadcasted_iota(jnp.int32, (rows, rows), 0)
    c = lax.broadcasted_iota(jnp.int32, (rows, rows), 1)
    lower = jnp.where(c <= r, 1.0, 0.0).astype(BF16)
    column = sum(dot(lower, part, ((1,), (0,))) for part in split3(decay))
    return column


def state_kernel(spans_ref, decay_ref, k_ref, v_ref, pack_ref, state_ref, cum_ref, dec_ref):
    rows, width = k_ref.shape
    heads = width // HD
    base = lax.axis_index("seq") * rows
    cumulative = running_sums(decay_ref[...])
    cum_ref[...] = cumulative
    start = last_start(spans_ref, base + rows - 1)
    positions = base + lax.broadcasted_iota(jnp.int32, (rows, 1), 0)
    inside = positions >= start
    last = cumulative[rows - 1 : rows, :]
    tail = jnp.where(inside, jnp.exp(jnp.minimum(last - cumulative, 0.0)), 0.0)
    block_decay = jnp.where(start < base, jnp.exp(last), 0.0)
    low_rows = []
    high_rows = []
    for h in range(heads):
        cols = slice(h * HD, (h + 1) * HD)
        tail_key = (k_ref[:, cols].astype(F32) * tail[:, h : h + 1]).astype(BF16)
        state = dot(tail_key, v_ref[:, cols], ((0,), (0,)))
        state_ref[cols, :] = state
        pack_ref[cols, :] = state.astype(BF16)
        one = jnp.broadcast_to(block_decay[:, h : h + 1], (1, HD))
        dec_ref[h : h + 1, :] = one
        high = one.astype(BF16)
        high_rows.append(high.astype(F32))
        low_rows.append(one - high.astype(F32))
    pad = [jnp.zeros((1, HD), F32)] * (pack_ref.shape[0] - width - 2 * heads)
    pack_ref[width:, :] = jnp.concatenate(high_rows + low_rows + pad, axis=0).astype(BF16)


def pair_kernel(state_ref, dec_ref, from_ref, out_ref):
    width = state_ref.shape[0]
    for h in range(width // HD):
        cols = slice(h * HD, (h + 1) * HD)
        out_ref[cols, :] = (
            state_ref[cols, :] + dec_ref[h : h + 1, :] * from_ref[cols, :].astype(F32)
        ).astype(BF16)


def lin_kernel(
    spans_ref, q_ref, k_ref, v_ref, gate_ref, gain_ref, cum_ref, one_ref, two_ref, y_ref, sq_ref
):
    rows, width = k_ref.shape
    heads = width // HD
    base = lax.axis_index("seq") * rows
    starts, positions = row_starts(spans_ref, rows, base)
    cumulative = cum_ref[...]
    across = jnp.transpose(cumulative)
    s_pos = base + lax.broadcasted_iota(jnp.int32, (rows, rows), 1)
    allowed = (s_pos <= positions) & (s_pos >= starts)
    entry = jnp.where(starts < base, jnp.exp(cumulative), 0.0)
    mix_gain = gain_ref[...]
    squares = jnp.zeros((rows, 1), F32)
    extra = one_ref[width:, :].astype(F32)
    for h in range(heads):
        cols = slice(h * HD, (h + 1) * HD)
        q = q_ref[:, cols]
        v = v_ref[:, cols]
        scores = dot(q, k_ref[:, cols], ((1,), (1,)))
        spread = cumulative[:, h : h + 1] - across[h : h + 1, :]
        weights = jnp.where(allowed, scores * jnp.exp(jnp.minimum(spread, 0.0)), 0.0).astype(BF16)
        before = extra[h : h + 1, :] + extra[heads + h : heads + h + 1, :]
        carried = one_ref[cols, :].astype(F32) + before * two_ref[cols, :].astype(F32)
        mixture = dot(weights, v, ((1,), (0,))) + (
            dot(q, carried.astype(BF16), ((1,), (0,))) * entry[:, h : h + 1]
        )
        squares = squares + jnp.sum(mixture * mixture, axis=1, keepdims=True)
        gate = jax.nn.sigmoid(gate_ref[:, cols].astype(F32))
        y_ref[:, cols] = mixture * mix_gain[:, cols] * gate
    sq_ref[...] = jnp.transpose(jnp.broadcast_to(squares, (rows, HD)))[:8, :]


def visible(starts, base_of_keys, rows):
    keys = base_of_keys + lax.broadcasted_iota(jnp.int32, (rows, rows), 1)
    return keys, keys >= starts


def soft_first_kernel(
    spans_ref, q_ref, k0_ref, v0_ref, k2_ref, v2_ref, ke_ref, ve_ref, acc_ref, m_ref, l_ref
):
    rows, width = q_ref.shape
    heads = width // HD
    place = lax.axis_index("seq")
    base = place * rows
    odd = lax.rem(place, 2)
    starts, positions = row_starts(spans_ref, rows, base)
    keys, seen = visible(starts, base, rows)
    bias0 = jnp.where(seen & (keys <= positions), 0.0, NEG)
    bias2 = jnp.where(visible(starts, base - 2 * rows, rows)[1], 0.0, NEG)
    biase = jnp.where(visible(starts, base - (1 + 2 * odd) * rows, rows)[1], 0.0, NEG)
    for h in range(heads):
        cols = slice(h * HD, (h + 1) * HD)
        q = q_ref[:, cols]
        s0 = dot(q, k0_ref[:, cols], ((1,), (1,))) * SOFT_SCALE + bias0
        s2 = dot(q, k2_ref[:, cols], ((1,), (1,))) * SOFT_SCALE + bias2
        se = dot(q, ke_ref[:, cols], ((1,), (1,))) * SOFT_SCALE + biase
        m = jnp.max(jnp.maximum(jnp.maximum(s0, s2), se), axis=1, keepdims=True)
        p0 = jnp.exp2(s0 - m)
        p2 = jnp.exp2(s2 - m)
        pe = jnp.exp2(se - m)
        m_ref[:, h : h + 1] = m
        l_ref[:, h : h + 1] = jnp.sum(p0 + p2 + pe, axis=1, keepdims=True)
        acc_ref[:, cols] = (
            dot(p0.astype(BF16), v0_ref[:, cols], ((1,), (0,)))
            + dot(p2.astype(BF16), v2_ref[:, cols], ((1,), (0,)))
            + dot(pe.astype(BF16), ve_ref[:, cols], ((1,), (0,)))
        )


def soft_last_kernel(
    spans_ref, q_ref, kx_ref, vx_ref, kf_ref, vf_ref, acc_ref, m_ref, l_ref, y_ref, total_ref,
    soft_ref, lin_ref,
):
    rows, width = q_ref.shape
    heads = width // HD
    place = lax.axis_index("seq")
    base = place * rows
    odd = lax.rem(place, 2)
    starts, _ = row_starts(spans_ref, rows, base)
    bias = jnp.where(visible(starts, base - (3 - 2 * odd) * rows, rows)[1], 0.0, NEG)
    total = jnp.transpose(total_ref[...])[:, 0:1]
    norm = lax.rsqrt(total / (HALF_MODEL_HEADS * HD) + 1e-06)
    m_all = m_ref[...]
    l_all = l_ref[...]
    pick = odd == 1
    for h in range(heads):
        cols = slice(h * HD, (h + 1) * HD)
        q = q_ref[:, cols]
        k = jnp.where(pick, kx_ref[:, cols], kf_ref[:, cols])
        v = jnp.where(pick, vx_ref[:, cols], vf_ref[:, cols])
        s = dot(q, k, ((1,), (1,))) * SOFT_SCALE + bias
        m_old = m_all[:, h : h + 1]
        m = jnp.maximum(m_old, jnp.max(s, axis=1, keepdims=True))
        p = jnp.exp2(s - m)
        shrink = jnp.exp2(m_old - m)
        weight = l_all[:, h : h + 1] * shrink + jnp.sum(p, axis=1, keepdims=True)
        acc = acc_ref[:, cols] * shrink + dot(p.astype(BF16), v, ((1,), (0,)))
        soft_ref[:, cols] = (acc / weight).astype(BF16)
        lin_ref[:, cols] = (y_ref[:, cols] * norm).astype(BF16)


SMEM = pl.BlockSpec(memory_space=pltpu.SMEM)
FULL = pl.BlockSpec(memory_space=pltpu.VMEM)


def call(kernel, name, out_shape, arrays, smem=1):
    return pl.pallas_call(
        kernel,
        name=name,
        out_shape=out_shape,
        in_specs=[SMEM] * smem + [FULL] * (len(arrays) - smem),
        out_specs=jax.tree.map(lambda _: FULL, out_shape),
        compiler_params=pltpu.CompilerParams(vmem_limit_bytes=VMEM_LIMIT),
    )(*arrays)


def shards(
    lin_query,
    lin_key,
    lin_value,
    log_decay,
    gate_logits,
    norm_gain,
    soft_query,
    soft_key,
    soft_value,
    doc_ids,
    doc_spans,
):
    rows, width = lin_query.shape
    heads = width // HD
    devices = lax.axis_size("seq")
    shape = jax.ShapeDtypeStruct

    def ahead(array, by, step=1):
        return lax.ppermute(
            array, "seq", [(i, i + by) for i in range(0, devices - by, step)]
        )

    def swap(array):
        return lax.ppermute(array, "seq", [(i, i ^ 1) for i in range(devices)])

    k2 = ahead(soft_key, 2)
    kx = ahead(soft_key, 1, 2)
    v2 = ahead(soft_value, 2)
    vx = ahead(soft_value, 1, 2)
    ke = swap(k2)
    ve = swap(v2)
    kf = ahead(ke, 2, 2)
    vf = ahead(ve, 2, 2)

    extra = -(-2 * heads // 16) * 16
    pack, state, cumulative, decay = call(
        state_kernel,
        "state",
        (
            shape((width + extra, HD), BF16),
            shape((width, HD), F32),
            shape((rows, heads), F32),
            shape((heads, HD), F32),
        ),
        (doc_spans, log_decay, lin_key, lin_value),
    )
    one = ahead(pack, 1)
    pair = call(pair_kernel, "pair", shape((width, HD), BF16), (state, decay, one), smem=0)
    two = ahead(pair, 2)
    y, squares = call(
        lin_kernel,
        "lin",
        (shape((rows, width), F32), shape((8, rows), F32)),
        (
            doc_spans, lin_query, lin_key, lin_value, gate_logits, norm_gain.reshape(1, width),
            cumulative, one, two,
        ),
    )
    total = lax.psum(squares, "head")
    acc, top, weight = call(
        soft_first_kernel,
        "soft_first",
        (shape((rows, width), F32), shape((rows, heads), F32), shape((rows, heads), F32)),
        (doc_spans, soft_query, soft_key, soft_value, k2, v2, ke, ve),
    )
    soft_out, lin_out = call(
        soft_last_kernel,
        "soft_last",
        (shape((rows, width), BF16), shape((rows, width), BF16)),
        (doc_spans, soft_query, kx, vx, kf, vf, acc, top, weight, y, total),
    )
    return (lin_out, soft_out)


def solution(mesh):
    in_specs = (
        P("seq", "head"),
        P("seq", "head"),
        P("seq", "head"),
        P("seq", "head"),
        P("seq", "head"),
        P("head"),
        P("seq", "head"),
        P("seq", "head"),
        P("seq", "head"),
        P("seq"),
        P(),
    )
    out_specs = (P("seq", "head"), P("seq", "head"))
    return jax.shard_map(shards, mesh=mesh, in_specs=in_specs, out_specs=out_specs, check_vma=False)
```

time: 213 us -> 99.1 us (0.47)
  the two profiles are of different devices: /device:TPU:30 before, /device:TPU:0 now
where the time goes in v1:
time: 99.1 us; the launch traced here: 98.5 us
  waiting for transfers between devices  37.9 us (38%)
  starting transfers between devices  31.8 us (32%)
  Pallas kernels  16.1 us (16%)
  local copies, waits for them, and re-layouts  6.11 us (6%)
  blocking collectives  5.74 us (6%)
    ppermute x8, waiting for transfers between devices, ahead(): lax.ppermute(array, 'seq', [(i, i + by) for i in range(0, devices - by, s...  37.9 us
    ppermute x8, starting transfers between devices, ahead(): lax.ppermute(array, 'seq', [(i, i + by) for i in range(0, devices - by, s...  28.9 us
    pallas_call x5, Pallas kernels, call(): pl.pallas_call(kernel, name=name, out_shape=out_shape, in_specs=[SMEM] *...  16.1 us
    unnamed x28, local copies, waits for them, and re-layouts  6.11 us
    psum x1, blocking collectives, shards(): total = lax.psum(squares, 'head')  5.74 us
    ppermute x2, starting transfers between devices, swap(): return lax.ppermute(array, 'seq', [(i, i ^ 1) for i in range(devices)])  2.98 us
  transfers between devices with their start and end apart: 10, of which 3 were waited for; matrix products, arithmetic and copies ran while one was open for 1% of the time, Pallas kernels for 10%

profile of v1, /device:TPU:0, one launch (start us, length us, event | category | flops | bytes accessed | tf_op | source)
XLA Modules:
  0.0 98.5 jit_solution(7082980126614641090)
XLA Ops:
  0.6 0.0 copy-start.12
  0.6 5.0 %collective-permute-start.2 = (bf16[256,1024]{1,0:T(8,128)(2,1)}, bf16[256,1024]{1,0:T(8,128)(2,1)S(1)}, u32[]{:S(2)}, u32[]{:S(2)}) collective-permute-start(bf16[256,1024]{1,0:T(8,128)(2,1)} %k0_ref.1), channel_id=1, source_target_pairs={{0,8},{4,12},{8,16},{12,20},{16,24},{20,28},{1,9},{5,13},{9,17},{1... | collective-permute-start | bytes 1572872 | tf_op jit(solution)/shard_map/ppermute | solution.py:233
  5.6 3.5 %collective-permute-start.5 = (bf16[256,1024]{1,0:T(8,128)(2,1)}, bf16[256,1024]{1,0:T(8,128)(2,1)S(1)}, u32[]{:S(2)}, u32[]{:S(2)}) collective-permute-start(bf16[256,1024]{1,0:T(8,128)(2,1)} %v0_ref.1), channel_id=1, source_target_pairs={{0,8},{4,12},{8,16},{12,20},{16,24},{20,28},{1,9},{5,13},{9,17},{1... | collective-permute-start | bytes 1572872 | tf_op jit(solution)/shard_map/ppermute | solution.py:233
  9.1 9.1 %collective-permute-done.2.k2_ref = bf16[256,1024]{1,0:T(8,128)(2,1)S(1)} collective-permute-done((bf16[256,1024]{1,0:T(8,128)(2,1)}, bf16[256,1024]{1,0:T(8,128)(2,1)S(1)}, u32[]{:S(2)}, u32[]{:S(2)}) %collective-permute-start.2) | collective-permute-done | bytes 524320 | tf_op jit(solution)/shard_map/ppermute | solution.py:233
  18.2 1.5 %collective-permute-start.3 = (bf16[256,1024]{1,0:T(8,128)(2,1)S(1)}, bf16[256,1024]{1,0:T(8,128)(2,1)}, u32[]{:S(2)}, u32[]{:S(2)}) collective-permute-start(bf16[256,1024]{1,0:T(8,128)(2,1)S(1)} %collective-permute-done.2.k2_ref), channel_id=1, source_target_pairs={{0,4},{4,0},{8,12},{12,8},{16,20},{20,16},{24,28},{28,24},{1,5},{5... | collective-permute-start | bytes 1572872 | tf_op jit(solution)/shard_map/ppermute | solution.py:238
  19.7 8.6 %collective-permute-done.5.v2_ref = bf16[256,1024]{1,0:T(8,128)(2,1)S(1)} collective-permute-done((bf16[256,1024]{1,0:T(8,128)(2,1)}, bf16[256,1024]{1,0:T(8,128)(2,1)S(1)}, u32[]{:S(2)}, u32[]{:S(2)}) %collective-permute-start.5) | collective-permute-done | bytes 524320 | tf_op jit(solution)/shard_map/ppermute | solution.py:233
  28.3 0.0 copy-start.7
  28.3 1.5 %collective-permute-start.6 = (bf16[256,1024]{1,0:T(8,128)(2,1)S(1)}, bf16[256,1024]{1,0:T(8,128)(2,1)}, u32[]{:S(2)}, u32[]{:S(2)}) collective-permute-start(bf16[256,1024]{1,0:T(8,128)(2,1)S(1)} %collective-permute-done.5.v2_ref), channel_id=1, source_target_pairs={{0,4},{4,0},{8,12},{12,8},{16,20},{20,16},{24,28},{28,24},{1,5},{5... | collective-permute-start | bytes 1572872 | tf_op jit(solution)/shard_map/ppermute | solution.py:238
  29.8 0.8 copy.16.spans_ref
  30.6 0.0 copy-done.12
  30.6 0.1 copy.14.decay_ref
  30.7 0.0 copy-start.1
  30.7 1.0 %copy-done.1 = bf16[256,1024]{1,0:T(8,128)(2,1)S(1)} copy-done((bf16[256,1024]{1,0:T(8,128)(2,1)S(1)}, bf16[256,1024]{1,0:T(8,128)(2,1)}, u32[]{:S(2)}) %copy-start.1) | copy-done | bytes 524312
  31.7 0.0 copy-start.3
  31.7 1.0 %copy-done.3 = bf16[256,1024]{1,0:T(8,128)(2,1)S(1)} copy-done((bf16[256,1024]{1,0:T(8,128)(2,1)S(1)}, bf16[256,1024]{1,0:T(8,128)(2,1)}, u32[]{:S(2)}) %copy-start.3) | copy-done | bytes 524312
  32.8 0.0 copy-start.5
  32.8 0.0 copy-start.6
  32.8 1.7 %state.1 = (bf16[1040,128]{1,0:T(8,128)(2,1)S(1)}, f32[1024,128]{1,0:T(8,128)S(1)}, f32[256,8]{1,0:T(8,128)S(1)}, f32[8,128]{1,0:T(8,128)S(1)}) custom-call(s32[9,2]{1,0:T(8,128)S(1)} %copy.16.spans_ref, f32[256,8]{1,0:T(8,128)S(1)} %copy.14.decay_ref, bf16[256,1024]{1,0:T(8,128)(2,1)S(1)} %copy-done.1, bf16[256,1024]{1,0:T(8,128)(2,1)S(1)} %copy-done.3), custom_call_target="tpu_custom_call" | custom-call | tf_op jit(solution)/shard_map/state/pallas_call | solution.py:204
  34.5 0.0 copy-done.7
  34.5 2.5 %collective-permute-start.8 = (bf16[1040,128]{1,0:T(8,128)(2,1)S(1)}, bf16[1040,128]{1,0:T(8,128)(2,1)S(1)}, u32[]{:S(2)}, u32[]{:S(2)}) collective-permute-start(bf16[1040,128]{1,0:T(8,128)(2,1)S(1)} %get-tuple-element.17), channel_id=1, source_target_pairs={{0,4},{4,8},{8,12},{12,16},{16,20},{20,24},{24,28},{1,5},{5,9},{9,... | collective-permute-start | bytes 798728 | tf_op jit(solution)/shard_map/ppermute | solution.py:233
  37.0 0.0 copy-done.5
  37.0 6.0 %collective-permute-start = (bf16[256,1024]{1,0:T(8,128)(2,1)S(1)}, bf16[256,1024]{1,0:T(8,128)(2,1)}, u32[]{:S(2)}, u32[]{:S(2)}) collective-permute-start(bf16[256,1024]{1,0:T(8,128)(2,1)S(1)} %copy-done.5), channel_id=1, source_target_pairs={{0,4},{8,12},{16,20},{24,28},{1,5},{9,13},{17,21},{25,29},{2,6},{1... | collective-permute-start | bytes 1572872 | tf_op jit(solution)/shard_map/ppermute | solution.py:233
  43.0 0.0 copy-done.6
  43.0 2.1 %collective-permute-start.1 = (bf16[256,1024]{1,0:T(8,128)(2,1)S(1)}, bf16[256,1024]{1,0:T(8,128)(2,1)}, u32[]{:S(2)}, u32[]{:S(2)}) collective-permute-start(bf16[256,1024]{1,0:T(8,128)(2,1)S(1)} %copy-done.6), channel_id=1, source_target_pairs={{0,4},{8,12},{16,20},{24,28},{1,5},{9,13},{17,21},{25,29},{2,6},{1... | collective-permute-start | bytes 1572872 | tf_op jit(solution)/shard_map/ppermute | solution.py:233
  45.1 0.0 collective-permute-done.3.ke_ref
  45.1 4.3 %collective-permute-start.4 = (bf16[256,1024]{1,0:T(8,128)(2,1)}, bf16[256,1024]{1,0:T(8,128)(2,1)}, u32[]{:S(2)}, u32[]{:S(2)}) collective-permute-start(bf16[256,1024]{1,0:T(8,128)(2,1)} %collective-permute-done.3.ke_ref), channel_id=1, source_target_pairs={{0,8},{8,16},{16,24},{1,9},{9,17},{17,25},{2,10},{10,18},{18,26},{... | collective-permute-start | bytes 1572872 | tf_op jit(solution)/shard_map/ppermute | solution.py:233
  49.4 0.0 collective-permute-done.6.ve_ref
  49.4 3.5 %collective-permute-start.7 = (bf16[256,1024]{1,0:T(8,128)(2,1)}, bf16[256,1024]{1,0:T(8,128)(2,1)}, u32[]{:S(2)}, u32[]{:S(2)}) collective-permute-start(bf16[256,1024]{1,0:T(8,128)(2,1)} %collective-permute-done.6.ve_ref), channel_id=1, source_target_pairs={{0,8},{8,16},{16,24},{1,9},{9,17},{17,25},{2,10},{10,18},{18,26},{... | collective-permute-start | bytes 1572872 | tf_op jit(solution)/shard_map/ppermute | solution.py:233
  52.9 0.0 collective-permute-done.8.from_ref.one_ref
  52.9 0.1 pair.1
  53.0 2.1 %collective-permute-start.9 = (bf16[1024,128]{1,0:T(8,128)(2,1)S(1)}, bf16[1024,128]{1,0:T(8,128)(2,1)S(1)}, u32[]{:S(2)}, u32[]{:S(2)}) collective-permute-start(bf16[1024,128]{1,0:T(8,128)(2,1)S(1)} %pair.1), channel_id=1, source_target_pairs={{0,8},{4,12},{8,16},{12,20},{16,24},{20,28},{1,9},{5,13},{9,17},{1... | collective-permute-start | bytes 786440 | tf_op jit(solution)/shard_map/ppermute | solution.py:233
  55.0 20.2 %collective-permute-done.9.two_ref = bf16[1024,128]{1,0:T(8,128)(2,1)S(1)} collective-permute-done((bf16[1024,128]{1,0:T(8,128)(2,1)S(1)}, bf16[1024,128]{1,0:T(8,128)(2,1)S(1)}, u32[]{:S(2)}, u32[]{:S(2)}) %collective-permute-start.9) | collective-permute-done | bytes 262176 | tf_op jit(solution)/shard_map/ppermute | solution.py:233
  75.2 0.0 copy-done.2
  75.2 0.0 copy-done.4
  75.2 0.0 copy-done.11
  75.2 1.0 %copy-done.9 = bf16[256,1024]{1,0:T(8,128)(2,1)S(1)} copy-done((bf16[256,1024]{1,0:T(8,128)(2,1)S(1)}, bf16[256,1024]{1,0:T(8,128)(2,1)}, u32[]{:S(2)}) %copy-start.9) | copy-done | bytes 524312
  76.2 1.0 %copy-done.10 = bf16[256,1024]{1,0:T(8,128)(2,1)S(1)} copy-done((bf16[256,1024]{1,0:T(8,128)(2,1)S(1)}, bf16[256,1024]{1,0:T(8,128)(2,1)}, u32[]{:S(2)}) %copy-start.10) | copy-done | bytes 524312
  77.3 3.3 %lin.1 = (f32[256,1024]{1,0:T(8,128)S(1)}, f32[8,256]{1,0:T(8,128)S(1)}) custom-call(s32[9,2]{1,0:T(8,128)S(1)} %copy.16.spans_ref, bf16[256,1024]{1,0:T(8,128)(2,1)S(1)} %copy-done.9, bf16[256,1024]{1,0:T(8,128)(2,1)S(1)} %copy-done.2, bf16[256,1024]{1,0:T(8,128)(2,1)S(1)} %copy-done.4, bf16[256,1024]{1,0:T(8,128)(2,1)S(1)} %copy-done.10, ...), custom_call_target="tpu_custom_call" | custom-call | tf_op jit(solution)/shard_map/lin/pallas_call | solution.py:204
  80.6 5.7 %psum.7.total_ref = f32[8,256]{1,0:T(8,128)S(1)} all-reduce(f32[8,256]{1,0:T(8,128)S(1)} %get-tuple-element.21), channel_id=1, replica_groups=mesh['seq'=8,'head'=4] {'head'}, use_global_device_ids=true, to_apply=%region_0.0 | all-reduce | flops 2048 | bytes 16384 | tf_op jit(solution)/shard_map/psum | solution.py:273
  86.4 0.0 copy-done
  86.4 0.0 copy-start.8
  86.4 1.0 %copy-done.8 = bf16[256,1024]{1,0:T(8,128)(2,1)S(1)} copy-done((bf16[256,1024]{1,0:T(8,128)(2,1)S(1)}, bf16[256,1024]{1,0:T(8,128)(2,1)}, u32[]{:S(2)}) %copy-start.8) | copy-done | bytes 524312
  87.4 4.7 %soft_first.1 = (f32[256,1024]{1,0:T(8,128)S(1)}, f32[256,8]{1,0:T(8,128)S(1)}, f32[256,8]{1,0:T(8,128)S(1)}) custom-call(s32[9,2]{1,0:T(8,128)S(1)} %copy.16.spans_ref, bf16[256,1024]{1,0:T(8,128)(2,1)S(1)} %copy-done, bf16[256,1024]{1,0:T(8,128)(2,1)S(1)} %copy-done.5, bf16[256,1024]{1,0:T(8,128)(2,1)S(1)} %copy-done.6, ...), custom_call_target="tpu_custom_call" | custom-call | tf_op jit(solution)/shard_map/soft_first/pallas_call | solution.py:204
  92.1 0.0 collective-permute-done.kx_ref
  92.2 0.0 collective-permute-done.1.vx_ref
  92.2 0.0 collective-permute-done.4.kf_ref
  92.2 0.0 collective-permute-done.7.vf_ref
  92.2 6.3 %soft_last.1 = (bf16[256,1024]{1,0:T(8,128)(2,1)}, bf16[256,1024]{1,0:T(8,128)(2,1)}) custom-call(s32[9,2]{1,0:T(8,128)S(1)} %copy.16.spans_ref, bf16[256,1024]{1,0:T(8,128)(2,1)S(1)} %copy-done, bf16[256,1024]{1,0:T(8,128)(2,1)} %collective-permute-done.kx_ref, bf16[256,1024]{1,0:T(8,128)(2,1)} %collective-permute-done.1.vx_ref, ...), custom_call_target="tpu_custom_call" | custom-call | tf_op jit(solution)/shard_map/soft_last/pallas_call | solution.py:204
  (6 shorter events, 0.0 us)
Async XLA Ops:
  0.6 29.9 %copy-start.12 = (f32[256,8]{0,1:T(8,128)S(1)}, f32[256,8]{0,1:T(8,128)}, u32[]{:S(2)}) copy-start(f32[256,8]{0,1:T(8,128)} %param.14) | copy-start | bytes 24580
  0.6 17.6 %collective-permute-start.2 = (bf16[256,1024]{1,0:T(8,128)(2,1)}, bf16[256,1024]{1,0:T(8,128)(2,1)S(1)}, u32[]{:S(2)}, u32[]{:S(2)}) collective-permute-start(bf16[256,1024]{1,0:T(8,128)(2,1)} %k0_ref.1), channel_id=1, source_target_pairs={{0,8},{4,12},{8,16},{12,20},{16,24},{20,28},{1,9},{5,13},{9,17},{1... | collective-permute-start | bytes 1572872 | tf_op jit(solution)/shard_map/ppermute | solution.py:233
  5.6 22.7 %collective-permute-start.5 = (bf16[256,1024]{1,0:T(8,128)(2,1)}, bf16[256,1024]{1,0:T(8,128)(2,1)S(1)}, u32[]{:S(2)}, u32[]{:S(2)}) collective-permute-start(bf16[256,1024]{1,0:T(8,128)(2,1)} %v0_ref.1), channel_id=1, source_target_pairs={{0,8},{4,12},{8,16},{12,20},{16,24},{20,28},{1,9},{5,13},{9,17},{1... | collective-permute-start | bytes 1572872 | tf_op jit(solution)/shard_map/ppermute | solution.py:233
  18.2 26.9 %collective-permute-start.3 = (bf16[256,1024]{1,0:T(8,128)(2,1)S(1)}, bf16[256,1024]{1,0:T(8,128)(2,1)}, u32[]{:S(2)}, u32[]{:S(2)}) collective-permute-start(bf16[256,1024]{1,0:T(8,128)(2,1)S(1)} %collective-permute-done.2.k2_ref), channel_id=1, source_target_pairs={{0,4},{4,0},{8,12},{12,8},{16,20},{20,16},{24,28},{28,24},{1,5},{5... | collective-permute-start | bytes 1572872 | tf_op jit(solution)/shard_map/ppermute | solution.py:238
  28.3 6.2 %copy-start.7 = (bf16[256,1024]{1,0:T(8,128)(2,1)}, bf16[256,1024]{1,0:T(8,128)(2,1)S(1)}, u32[]{:S(2)}) copy-start(bf16[256,1024]{1,0:T(8,128)(2,1)S(1)} %collective-permute-done.5.v2_ref) | copy-start | bytes 1572868
  28.3 21.1 %collective-permute-start.6 = (bf16[256,1024]{1,0:T(8,128)(2,1)S(1)}, bf16[256,1024]{1,0:T(8,128)(2,1)}, u32[]{:S(2)}, u32[]{:S(2)}) collective-permute-start(bf16[256,1024]{1,0:T(8,128)(2,1)S(1)} %collective-permute-done.5.v2_ref), channel_id=1, source_target_pairs={{0,4},{4,0},{8,12},{12,8},{16,20},{20,16},{24,28},{28,24},{1,5},{5... | collective-permute-start | bytes 1572872 | tf_op jit(solution)/shard_map/ppermute | solution.py:238
  30.7 1.0 %copy-start.1 = (bf16[256,1024]{1,0:T(8,128)(2,1)S(1)}, bf16[256,1024]{1,0:T(8,128)(2,1)}, u32[]{:S(2)}) copy-start(bf16[256,1024]{1,0:T(8,128)(2,1)} %k_ref.3) | copy-start | bytes 1572868
  31.7 1.0 %copy-start.3 = (bf16[256,1024]{1,0:T(8,128)(2,1)S(1)}, bf16[256,1024]{1,0:T(8,128)(2,1)}, u32[]{:S(2)}) copy-start(bf16[256,1024]{1,0:T(8,128)(2,1)} %v_ref.3) | copy-start | bytes 1572868
  32.8 4.2 %copy-start.5 = (bf16[256,1024]{1,0:T(8,128)(2,1)S(1)}, bf16[256,1024]{1,0:T(8,128)(2,1)}, u32[]{:S(2)}) copy-start(bf16[256,1024]{1,0:T(8,128)(2,1)} %k0_ref.1) | copy-start | bytes 1572868
  32.8 10.2 %copy-start.6 = (bf16[256,1024]{1,0:T(8,128)(2,1)S(1)}, bf16[256,1024]{1,0:T(8,128)(2,1)}, u32[]{:S(2)}) copy-start(bf16[256,1024]{1,0:T(8,128)(2,1)} %v0_ref.1) | copy-start | bytes 1572868
  34.5 18.4 %collective-permute-start.8 = (bf16[1040,128]{1,0:T(8,128)(2,1)S(1)}, bf16[1040,128]{1,0:T(8,128)(2,1)S(1)}, u32[]{:S(2)}, u32[]{:S(2)}) collective-permute-start(bf16[1040,128]{1,0:T(8,128)(2,1)S(1)} %get-tuple-element.17), channel_id=1, source_target_pairs={{0,4},{4,8},{8,12},{12,16},{16,20},{20,24},{24,28},{1,5},{5,9},{9,... | collective-permute-start | bytes 798728 | tf_op jit(solution)/shard_map/ppermute | solution.py:233
  37.0 55.2 %collective-permute-start = (bf16[256,1024]{1,0:T(8,128)(2,1)S(1)}, bf16[256,1024]{1,0:T(8,128)(2,1)}, u32[]{:S(2)}, u32[]{:S(2)}) collective-permute-start(bf16[256,1024]{1,0:T(8,128)(2,1)S(1)} %copy-done.5), channel_id=1, source_target_pairs={{0,4},{8,12},{16,20},{24,28},{1,5},{9,13},{17,21},{25,29},{2,6},{1... | collective-permute-start | bytes 1572872 | tf_op jit(solution)/shard_map/ppermute | solution.py:233
  43.0 49.2 %collective-permute-start.1 = (bf16[256,1024]{1,0:T(8,128)(2,1)S(1)}, bf16[256,1024]{1,0:T(8,128)(2,1)}, u32[]{:S(2)}, u32[]{:S(2)}) collective-permute-start(bf16[256,1024]{1,0:T(8,128)(2,1)S(1)} %copy-done.6), channel_id=1, source_target_pairs={{0,4},{8,12},{16,20},{24,28},{1,5},{9,13},{17,21},{25,29},{2,6},{1... | collective-permute-start | bytes 1572872 | tf_op jit(solution)/shard_map/ppermute | solution.py:233
  45.1 47.1 %collective-permute-start.4 = (bf16[256,1024]{1,0:T(8,128)(2,1)}, bf16[256,1024]{1,0:T(8,128)(2,1)}, u32[]{:S(2)}, u32[]{:S(2)}) collective-permute-start(bf16[256,1024]{1,0:T(8,128)(2,1)} %collective-permute-done.3.ke_ref), channel_id=1, source_target_pairs={{0,8},{8,16},{16,24},{1,9},{9,17},{17,25},{2,10},{10,18},{18,26},{... | collective-permute-start | bytes 1572872 | tf_op jit(solution)/shard_map/ppermute | solution.py:233
  49.4 42.8 %collective-permute-start.7 = (bf16[256,1024]{1,0:T(8,128)(2,1)}, bf16[256,1024]{1,0:T(8,128)(2,1)}, u32[]{:S(2)}, u32[]{:S(2)}) collective-permute-start(bf16[256,1024]{1,0:T(8,128)(2,1)} %collective-permute-done.6.ve_ref), channel_id=1, source_target_pairs={{0,8},{8,16},{16,24},{1,9},{9,17},{17,25},{2,10},{10,18},{18,26},{... | collective-permute-start | bytes 1572872 | tf_op jit(solution)/shard_map/ppermute | solution.py:233
  52.9 22.3 %copy-start.2 = (bf16[256,1024]{1,0:T(8,128)(2,1)S(1)}, bf16[256,1024]{1,0:T(8,128)(2,1)}, u32[]{:S(2)}) copy-start(bf16[256,1024]{1,0:T(8,128)(2,1)} %k_ref.3) | copy-start | bytes 1572868
  52.9 22.3 %copy-start.4 = (bf16[256,1024]{1,0:T(8,128)(2,1)S(1)}, bf16[256,1024]{1,0:T(8,128)(2,1)}, u32[]{:S(2)}) copy-start(bf16[256,1024]{1,0:T(8,128)(2,1)} %v_ref.3) | copy-start | bytes 1572868
  52.9 22.3 %copy-start.11 = (f32[1024]{0:T(1024)S(1)}, f32[1024]{0:T(1024)}, u32[]{:S(2)}) copy-start(f32[1024]{0:T(1024)} %param.16) | copy-start | bytes 12292
  53.0 22.2 %collective-permute-start.9 = (bf16[1024,128]{1,0:T(8,128)(2,1)S(1)}, bf16[1024,128]{1,0:T(8,128)(2,1)S(1)}, u32[]{:S(2)}, u32[]{:S(2)}) collective-permute-start(bf16[1024,128]{1,0:T(8,128)(2,1)S(1)} %pair.1), channel_id=1, source_target_pairs={{0,8},{4,12},{8,16},{12,20},{16,24},{20,28},{1,9},{5,13},{9,17},{1... | collective-permute-start | bytes 786440 | tf_op jit(solution)/shard_map/ppermute | solution.py:233
  75.2 1.0 %copy-start.9 = (bf16[256,1024]{1,0:T(8,128)(2,1)S(1)}, bf16[256,1024]{1,0:T(8,128)(2,1)}, u32[]{:S(2)}) copy-start(bf16[256,1024]{1,0:T(8,128)(2,1)} %q_ref.4) | copy-start | bytes 1572868
  76.2 1.0 %copy-start.10 = (bf16[256,1024]{1,0:T(8,128)(2,1)S(1)}, bf16[256,1024]{1,0:T(8,128)(2,1)}, u32[]{:S(2)}) copy-start(bf16[256,1024]{1,0:T(8,128)(2,1)} %gate_ref.1) | copy-start | bytes 1572868
  77.3 9.1 %copy-start = (bf16[256,1024]{1,0:T(8,128)(2,1)S(1)}, bf16[256,1024]{1,0:T(8,128)(2,1)}, u32[]{:S(2)}) copy-start(bf16[256,1024]{1,0:T(8,128)(2,1)} %q_ref.5) | copy-start | bytes 1572868
  86.4 1.0 %copy-start.8 = (bf16[256,1024]{1,0:T(8,128)(2,1)S(1)}, bf16[256,1024]{1,0:T(8,128)(2,1)}, u32[]{:S(2)}) copy-start(bf16[256,1024]{1,0:T(8,128)(2,1)} %copy-done.7) | copy-start | bytes 1572868

commit v2 on v0

v2 whole, which is shorter than its diff:
```python
import functools

import jax
import jax.numpy as jnp
from jax import lax
from jax.experimental import pallas as pl
from jax.experimental.pallas import tpu as pltpu
from jax.sharding import PartitionSpec as P

HALF_MODEL_HEADS = 32
HD = 128
LANES = 128
NEG = -1e30
SOFT_SCALE = HD ** (-0.5) * 1.4426950408889634
F32 = jnp.float32
BF16 = jnp.bfloat16
VMEM_LIMIT = 6 * 1024 * 1024


def dot(a, b, dims):
    return lax.dot_general(a, b, (dims, ((), ())), preferred_element_type=F32)


def wide(column, width):
    return jnp.concatenate([column] * (width // LANES), axis=1)


def split3(x):
    high = x.astype(BF16)
    rest = x - high.astype(F32)
    middle = rest.astype(BF16)
    return high, middle, (rest - middle.astype(F32)).astype(BF16)


def places(rows):
    base = lax.axis_index("seq") * rows
    return base, base + lax.broadcasted_iota(jnp.int32, (rows, LANES), 0)


def prep_kernel(spans_ref, decay_ref, starts_ref, last_ref, cum_ref, across_ref):
    rows, width = cum_ref.shape
    heads = width // HD
    base, positions = places(rows)
    last_position = jnp.zeros((8, LANES), jnp.int32) + (base + rows - 1)

    def one(d, starts):
        first = spans_ref[0, d]
        return tuple(
            jnp.where(at >= first, jnp.maximum(start, first), start)
            for start, at in zip(starts, (positions, last_position))
        )

    docs = spans_ref.shape[1]
    nothing = (jnp.zeros_like(positions), jnp.zeros_like(last_position))
    starts_ref[...], last_ref[...] = lax.fori_loop(0, docs, one, nothing, unroll=docs <= 16)
    r = lax.broadcasted_iota(jnp.int32, (rows, rows), 0)
    c = lax.broadcasted_iota(jnp.int32, (rows, rows), 1)
    upper = jnp.where(r <= c, 1.0, 0.0).astype(BF16)
    across = sum(dot(part, upper, ((1,), (0,))) for part in split3(decay_ref[...]))
    across_ref[...] = across
    head = lax.broadcasted_iota(jnp.int32, (heads, width), 0)
    lane = lax.broadcasted_iota(jnp.int32, (heads, width), 1)
    spread = jnp.where((lane >= head * HD) & (lane < (head + 1) * HD), 1.0, 0.0).astype(BF16)
    cum_ref[...] = sum(dot(part, spread, ((0,), (0,))) for part in split3(across))


def key_bias(starts_ref, rows, keys, behind):
    base, positions = places(rows)
    key = base - behind + lax.broadcasted_iota(jnp.int32, (rows, keys), 1)
    seen = (key >= wide(starts_ref[...], keys)) & (key <= wide(positions, keys))
    return jnp.where(seen, 0.0, NEG)


def state_kernel(last_ref, cum_ref, k_ref, v_ref, pack_ref, state_ref, dec_ref):
    rows, width = k_ref.shape
    base, positions = places(rows)
    start = last_ref[0:1, :]
    inside = positions >= start
    for h in range(width // HD):
        cols = slice(h * HD, (h + 1) * HD)
        mine = cum_ref[:, cols]
        last = mine[rows - 1 : rows, :]
        tail = jnp.where(inside, jnp.exp(jnp.minimum(last - mine, 0.0)), 0.0)
        tail_key = (k_ref[:, cols].astype(F32) * tail).astype(BF16)
        state = dot(tail_key, v_ref[:, cols], ((0,), (0,)))
        state_ref[:, cols] = state
        pack_ref[0:HD, cols] = state.astype(BF16)
        decay = jnp.broadcast_to(jnp.where(start < base, jnp.exp(last), 0.0), (8, HD))
        dec_ref[:, cols] = decay
        high = decay.astype(BF16).astype(F32)
        pack_ref[HD:, cols] = jnp.concatenate([high, decay - high], axis=0).astype(BF16)


def pick_kernel(there_ref, own_ref, out_ref):
    odd = lax.rem(lax.axis_index("seq"), 2) == 1

    @pl.when(odd)
    def _():
        out_ref[...] = there_ref[...]

    @pl.when(jnp.logical_not(odd))
    def _():
        out_ref[...] = own_ref[...]


def pair_kernel(state_ref, dec_ref, from_ref, k_ref, out_ref):
    reach = out_ref.shape[0] - HD
    out_ref[0:HD, :] = (
        state_ref[...] + dec_ref[0:1, :] * from_ref[0:HD, :].astype(F32)
    ).astype(BF16)
    out_ref[HD:, :] = k_ref[k_ref.shape[0] - reach :, :]


def nearest_kernel(v_ref, out_ref):
    out_ref[...] = v_ref[v_ref.shape[0] - out_ref.shape[0] :, :]


def lin_kernel(
    starts_ref, q_ref, k_ref, v_ref, gate_ref, gain_ref, cum_ref, across_ref, one_ref, two_ref,
    y_ref, sq_ref,
):
    rows, width = k_ref.shape
    heads = width // HD
    allowed = key_bias(starts_ref, rows, rows, 0) == 0.0
    base, _ = places(rows)
    enters = starts_ref[...] < base
    squares = jnp.zeros((rows, HD), F32)
    extra = one_ref[HD:, :].astype(F32)
    for h in range(heads):
        cols = slice(h * HD, (h + 1) * HD)
        before = extra[0:1, cols] + extra[8:9, cols]
        carried = one_ref[0:HD, cols].astype(F32) + before * two_ref[0:HD, cols].astype(F32)
        mine = cum_ref[:, cols]
        decayed = jnp.exp(jnp.minimum(wide(mine, rows) - across_ref[h : h + 1, :], 0.0))
        q = q_ref[:, cols]
        scores = dot(q, k_ref[:, cols], ((1,), (1,)))
        weights = jnp.where(allowed, scores * decayed, 0.0).astype(BF16)
        cross = dot(q, carried.astype(BF16), ((1,), (0,)))
        mixture = dot(weights, v_ref[:, cols], ((1,), (0,))) + (
            cross * jnp.where(enters, jnp.exp(mine), 0.0)
        )
        squares = squares + mixture * mixture
        gate = jax.nn.sigmoid(gate_ref[:, cols].astype(F32))
        y_ref[:, cols] = mixture * gain_ref[:, cols] * gate
    ones = jnp.ones((8, HD), BF16)
    sq_ref[...] = sum(dot(ones, part, ((1,), (1,))) for part in split3(squares))


def norm_kernel(y_ref, *refs):
    *parts, lin_ref = refs
    total = jnp.transpose(sum(part[...] for part in parts))[:, 0:1]
    norm = lax.rsqrt(total / (HALF_MODEL_HEADS * HD) + 1e-06)
    lin_ref[...] = (y_ref[...] * norm).astype(BF16)


def with_ones(v):
    return jnp.concatenate([v, jnp.ones_like(v)], axis=1)


def top_of(s):
    return jnp.broadcast_to(jnp.max(s, axis=1, keepdims=True), (s.shape[0], LANES))


def soft_own_kernel(starts_ref, q_ref, k_ref, v_ref, sums_ref, m_ref):
    rows, width = q_ref.shape
    bias = key_bias(starts_ref, rows, rows, 0)
    for h in range(width // HD):
        cols = slice(h * HD, (h + 1) * HD)
        s = dot(q_ref[:, cols], k_ref[:, cols], ((1,), (1,))) * SOFT_SCALE + bias
        m = top_of(s)
        m_ref[:, cols] = m
        p = jnp.exp2(s - wide(m, rows)).astype(BF16)
        sums_ref[:, 2 * h * HD : 2 * (h + 1) * HD] = dot(p, with_ones(v_ref[:, cols]), ((1,), (0,)))


def soft_grow_kernel(back, starts_ref, q_ref, k_ref, v_ref, sums0_ref, m0_ref, sums_ref, m_ref):
    rows, width = q_ref.shape
    keys = k_ref.shape[0]
    bias = key_bias(starts_ref, rows, keys, back * rows)
    for h in range(width // HD):
        cols = slice(h * HD, (h + 1) * HD)
        both = slice(2 * h * HD, 2 * (h + 1) * HD)
        m_old = m0_ref[:, cols]
        s = dot(q_ref[:, cols], k_ref[:, cols], ((1,), (1,))) * SOFT_SCALE + bias
        m = jnp.maximum(m_old, top_of(s))
        m_ref[:, cols] = m
        p = jnp.exp2(s - wide(m, keys)).astype(BF16)
        sums_ref[:, both] = sums0_ref[:, both] * wide(jnp.exp2(m_old - m), 2 * HD) + dot(
            p, with_ones(v_ref[:, cols]), ((1,), (0,))
        )


def soft_weigh_kernel(back, starts_ref, q_ref, k_ref, sums_ref, m_ref, p_ref, acc_ref, inv_ref):
    rows, width = q_ref.shape
    keys = k_ref.shape[0] - HD
    bias = key_bias(starts_ref, rows, keys, (back - 1) * rows + keys)
    ones = jnp.ones((keys, HD), BF16)
    for h in range(width // HD):
        cols = slice(h * HD, (h + 1) * HD)
        m_old = m_ref[:, cols]
        s = dot(q_ref[:, cols], k_ref[HD:, cols], ((1,), (1,))) * SOFT_SCALE + bias
        m = jnp.maximum(m_old, top_of(s))
        p = jnp.exp2(s - wide(m, keys)).astype(BF16)
        shrink = jnp.exp2(m_old - m)
        weight = sums_ref[:, (2 * h + 1) * HD : (2 * h + 2) * HD] * shrink + dot(
            p, ones, ((1,), (0,))
        )
        inv = 1.0 / weight
        p_ref[:, h * keys : (h + 1) * keys] = p
        acc_ref[:, cols] = sums_ref[:, 2 * h * HD : (2 * h + 1) * HD] * (shrink * inv)
        inv_ref[:, cols] = inv


def soft_last_kernel(p_ref, v_ref, acc_ref, inv_ref, soft_ref):
    keys = v_ref.shape[0]
    for h in range(acc_ref.shape[1] // HD):
        cols = slice(h * HD, (h + 1) * HD)
        more = dot(p_ref[:, h * keys : (h + 1) * keys], v_ref[:, cols], ((1,), (0,)))
        soft_ref[:, cols] = (acc_ref[:, cols] + more * inv_ref[:, cols]).astype(BF16)


SMEM = pl.BlockSpec(memory_space=pltpu.SMEM)
VMEM = pl.BlockSpec(memory_space=pltpu.VMEM)


def call(kernel, name, out_shape, *arrays, smem=0):
    return pl.pallas_call(
        kernel,
        name=name,
        out_shape=out_shape,
        in_specs=[SMEM] * smem + [VMEM] * (len(arrays) - smem),
        out_specs=jax.tree.map(lambda _: VMEM, out_shape),
        compiler_params=pltpu.CompilerParams(vmem_limit_bytes=VMEM_LIMIT),
    )(*arrays)


def program(
    reach,
    lin_query,
    lin_key,
    lin_value,
    log_decay,
    gate_logits,
    norm_gain,
    soft_query,
    soft_key,
    soft_value,
    doc_spans,
):
    rows, width = lin_query.shape
    heads = width // HD
    devices = lax.axis_size("seq")
    shape = jax.ShapeDtypeStruct

    def ahead(array, by):
        return lax.ppermute(array, "seq", [(i, i + by) for i in range(devices - by)])

    def swap(array):
        return lax.ppermute(array, "seq", [(i, i ^ 1) for i in range(devices)])

    def everywhere(array):
        count = lax.axis_size("head")
        return [array] + [
            lax.ppermute(array, "head", [(i, (i + by) % count) for i in range(count)])
            for by in range(1, count)
        ]

    together = lax.optimization_barrier
    sums = (shape((rows, 2 * width), F32), shape((rows, width), F32))
    half = shape((rows, width), BF16)

    starts, last_start, cumulative, across = call(
        prep_kernel,
        "prep",
        (
            shape((rows, LANES), jnp.int32),
            shape((8, LANES), jnp.int32),
            shape((rows, width), F32),
            shape((heads, rows), F32),
        ),
        doc_spans.T, log_decay.T, smem=1,
    )
    first_key, starts = together((soft_key, starts))
    k2 = ahead(first_key, 2)
    pack, state, decay = call(
        state_kernel,
        "state",
        (shape((HD + 16, width), BF16), shape((HD, width), F32), shape((8, width), F32)),
        last_start, cumulative, lin_key, lin_value,
    )
    own_value, pack = together((soft_value, pack))
    one = ahead(pack, 1)
    v2 = ahead(own_value, 2)
    soft = call(soft_own_kernel, "soft_own", sums, starts, soft_query, soft_key, soft_value)
    own_key, top = together((soft_key, soft[1]))
    soft = (soft[0], top)
    k1 = swap(call(pick_kernel, "pick_k", half, k2, own_key))
    v1 = swap(call(pick_kernel, "pick_v", half, v2, soft_value))
    pair = call(
        pair_kernel, "pair", shape((HD + reach, width), BF16), state, decay, one, k1
    )
    two = ahead(pair, 2)
    soft = call(
        functools.partial(soft_grow_kernel, 2), "soft_2", sums, starts, soft_query, k2, v2, *soft
    )
    v1, top = together((v1, soft[1]))
    soft = (soft[0], top)
    v3 = ahead(call(nearest_kernel, "nearest", shape((reach, width), BF16), v1), 2)
    y, squares = call(
        lin_kernel,
        "lin",
        (shape((rows, width), F32), shape((8, rows), F32)),
        starts, lin_query, lin_key, lin_value, gate_logits, norm_gain.reshape(1, width),
        cumulative, across, one, two,
    )
    parts = everywhere(squares)
    soft = call(
        functools.partial(soft_grow_kernel, 1), "soft_1", sums, starts, soft_query, k1, v1, *soft
    )
    lin_out = call(norm_kernel, "norm", half, y, *parts)
    weights, acc, inv = call(
        functools.partial(soft_weigh_kernel, 3), "soft_weigh",
        (
            shape((rows, heads * reach), BF16), shape((rows, width), F32),
            shape((rows, width), F32),
        ),
        starts, soft_query, two, *soft,
    )
    soft_out = call(soft_last_kernel, "soft_last", half, weights, v3, acc, inv)
    return (lin_out, soft_out)


def shards(
    lin_query,
    lin_key,
    lin_value,
    log_decay,
    gate_logits,
    norm_gain,
    soft_query,
    soft_key,
    soft_value,
    doc_ids,
    doc_spans,
):
    rows = lin_query.shape[0]
    blocks = rows * jnp.arange(lax.axis_size("seq"), dtype=jnp.int32)
    begun = doc_spans[None, :, 0] <= blocks[:, None]
    starts = jnp.max(jnp.where(begun, doc_spans[None, :, 0], 0), axis=1)
    farthest = jnp.max(blocks - starts)
    reach = rows // 2
    return lax.cond(
        farthest <= 2 * rows + reach,
        functools.partial(program, reach),
        functools.partial(program, rows),
        lin_query, lin_key, lin_value, log_decay, gate_logits, norm_gain, soft_query, soft_key,
        soft_value, doc_spans,
    )


def solution(mesh):
    in_specs = (
        P("seq", "head"),
        P("seq", "head"),
        P("seq", "head"),
        P("seq", "head"),
        P("seq", "head"),
        P("head"),
        P("seq", "head"),
        P("seq", "head"),
        P("seq", "head"),
        P("seq"),
        P(),
    )
    out_specs = (P("seq", "head"), P("seq", "head"))
    return jax.shard_map(shards, mesh=mesh, in_specs=in_specs, out_specs=out_specs, check_vma=False)
```

time: 213 us -> 65.2 us (0.31)
  the two profiles are of different devices: /device:TPU:30 before, /device:TPU:0 now
where the time goes in v2:
time: 65.2 us; the launch traced here: 64.8 us
  starting transfers between devices  28 us (43%)
  waiting for transfers between devices  22.1 us (34%)
  Pallas kernels  11.6 us (18%)
  between operations  1.29 us (2%)
  other arithmetic  0.83 us (1%)
  local copies, waits for them, and re-layouts  0.73 us (1%)
    ppermute x5, starting transfers between devices, ahead(): lax.ppermute(array, 'seq', [(i, i + by) for i in range(devices - by)])  20.7 us
    ppermute x5, waiting for transfers between devices, ahead(): lax.ppermute(array, 'seq', [(i, i + by) for i in range(devices - by)])  19.9 us
    pallas_call x13, Pallas kernels, call(): pl.pallas_call(kernel, name=name, out_shape=out_shape, in_specs=[SMEM] *...  11.6 us
    ppermute x2, starting transfers between devices, swap(): return lax.ppermute(array, 'seq', [(i, i ^ 1) for i in range(devices)])  4.27 us
    ppermute x3, starting transfers between devices, everywhere(): lax.ppermute(array, 'head', [(i, (i + by) % count) for i in range(count)])  3.05 us
    ppermute x2, waiting for transfers between devices, swap(): return lax.ppermute(array, 'seq', [(i, i ^ 1) for i in range(devices)])  2.25 us
  transfers between devices with their start and end apart: 10, of which 4 were waited for; matrix products, arithmetic and copies ran while one was open for 0% of the time, Pallas kernels for 13%

profile of v2, /device:TPU:0, one launch (start us, length us, event | category | flops | bytes accessed | tf_op | source)
XLA Modules:
  0.0 64.8 jit_solution(1711411339127989585)
XLA Ops:
  0.6 0.7 %slice_bitcast_fusion = s32[9]{0:T(128)S(1)} fusion(s32[9,2]{0,1:T(2,128)} %param.22), kind=kLoop, calls=%fused_computation.2 | loop fusion | bytes 72 | tf_op jit(solution)/shard_map/le | solution.py:348
  1.3 0.2 select_reduce_fusion
  1.5 0.6 subtract_reduce_fusion
  2.8 62.0 %conditional.1 = (bf16[256,1024]{1,0:T(8,128)(2,1)}, bf16[256,1024]{1,0:T(8,128)(2,1)}) conditional(s32[]{:T(128)} %convert_element_type.3, (s32[9,2]{0,1:T(2,128)}, f32[256,8]{0,1:T(8,128)}, bf16[256,1024]{1,0:T(8,128)(2,1)}, f32[1024]{0:T(1024)}, bf16[256,1024]{1,0:T(8,128)(2,1)}, /*index=5*/bf16[256,1024]{1,0:T(8,128)(2,1)}, ...), branch_computations={%region_2.3_spmd, %region_3.4_spmd} | conditional | bytes 29606528 | solution.py:352
  2.8 0.0 copy-start.5
  2.8 0.0 copy-start.1
  2.8 0.0 copy-start.3
  2.9 1.8 %prep.3 = (s32[256,128]{1,0:T(8,128)S(1)}, s32[8,128]{1,0:T(8,128)S(1)}, f32[256,1024]{1,0:T(8,128)S(1)}, f32[8,256]{1,0:T(8,128)S(1)}) custom-call(s32[2,9]{1,0:T(2,128)} %bitcast.13, f32[8,256]{1,0:T(8,128)} %bitcast.9), custom_call_target="tpu_custom_call" | custom-call | tf_op jit(solution)/shard_map/cond/branch_1_fun/prep/pallas_call | solution.py:227
  4.7 5.0 %collective-permute-start.11 = (bf16[256,1024]{1,0:T(8,128)(2,1)}, bf16[256,1024]{1,0:T(8,128)(2,1)S(1)}, u32[]{:S(2)}, u32[]{:S(2)}) collective-permute-start(bf16[256,1024]{1,0:T(8,128)(2,1)} %get-tuple-element.97.k_ref.own_ref), channel_id=1, source_target_pairs={{0,8},{4,12},{8,16},{12,20},{16,24},{20,28},{1,9},{5,13},{9,17},{1... | collective-permute-start | bytes 1572872 | tf_op jit(solution)/shard_map/cond/branch_1_fun/ppermute | solution.py:256
  9.7 1.8 %state.3 = (bf16[144,1024]{1,0:T(8,128)(2,1)S(1)}, f32[128,1024]{1,0:T(8,128)S(1)}, f32[8,1024]{1,0:T(8,128)S(1)}) custom-call(s32[8,128]{1,0:T(8,128)S(1)} %get-tuple-element.89.last_ref, f32[256,1024]{1,0:T(8,128)S(1)} %get-tuple-element.86.cum_ref, bf16[256,1024]{1,0:T(8,128)(2,1)} %get-tuple-element.82.k_ref, bf16[256,1024]{1,0:T(8,128)(2,1)} %get-tuple-element.83.v_ref), custom_call_target="tpu_custom_call" | custom-call | tf_op jit(solution)/shard_map/cond/branch_1_fun/state/pallas_call | solution.py:227
  11.4 0.0 copy-done.5
  11.4 3.5 %collective-permute-start.17 = (bf16[256,1024]{1,0:T(8,128)(2,1)S(1)}, bf16[256,1024]{1,0:T(8,128)(2,1)S(1)}, u32[]{:S(2)}, u32[]{:S(2)}) collective-permute-start(bf16[256,1024]{1,0:T(8,128)(2,1)S(1)} %copy-done.5), channel_id=1, source_target_pairs={{0,8},{4,12},{8,16},{12,20},{16,24},{20,28},{1,9},{5,13},{9,17},{1... | collective-permute-start | bytes 1572872 | tf_op jit(solution)/shard_map/cond/branch_1_fun/ppermute | solution.py:256
  14.9 0.0 copy-done.1
  14.9 0.0 copy-done.3
  14.9 0.9 %soft_own.3 = (f32[256,2048]{1,0:T(8,128)S(1)}, f32[256,1024]{1,0:T(8,128)S(1)}) custom-call(s32[256,128]{1,0:T(8,128)S(1)} %get-tuple-element.80.starts_ref, bf16[256,1024]{1,0:T(8,128)(2,1)S(1)} %copy-done.1, bf16[256,1024]{1,0:T(8,128)(2,1)S(1)} %copy-done.3, bf16[256,1024]{1,0:T(8,128)(2,1)S(1)} %copy-done.5), custom_call_target="tpu_custom_call" | custom-call | tf_op jit(solution)/shard_map/cond/branch_1_fun/soft_own/pallas_call | solution.py:227
  15.9 6.4 %collective-permute-done.11.there_ref.k_ref = bf16[256,1024]{1,0:T(8,128)(2,1)S(1)} collective-permute-done((bf16[256,1024]{1,0:T(8,128)(2,1)}, bf16[256,1024]{1,0:T(8,128)(2,1)S(1)}, u32[]{:S(2)}, u32[]{:S(2)}) %collective-permute-start.11) | collective-permute-done | bytes 524320 | tf_op jit(solution)/shard_map/cond/branch_1_fun/ppermute | solution.py:256
  22.3 1.6 %collective-permute-start.12 = (bf16[256,1024]{1,0:T(8,128)(2,1)S(1)}, bf16[256,1024]{1,0:T(8,128)(2,1)S(1)}, u32[]{:S(2)}, u32[]{:S(2)}) collective-permute-start(bf16[256,1024]{1,0:T(8,128)(2,1)S(1)} %pick_k.3), channel_id=1, source_target_pairs={{0,4},{4,0},{8,12},{12,8},{16,20},{20,16},{24,28},{28,24},{1,5},{5... | collective-permute-start | bytes 1572872 | tf_op jit(solution)/shard_map/cond/branch_1_fun/ppermute | solution.py:259
  23.8 2.4 %collective-permute-start.10 = (bf16[144,1024]{1,0:T(8,128)(2,1)S(1)}, bf16[144,1024]{1,0:T(8,128)(2,1)S(1)}, u32[]{:S(2)}, u32[]{:S(2)}) collective-permute-start(bf16[144,1024]{1,0:T(8,128)(2,1)S(1)} %get-tuple-element.91), channel_id=1, source_target_pairs={{0,4},{4,8},{8,12},{12,16},{16,20},{20,24},{24,28},{1,5},{5,9},{9,... | collective-permute-start | bytes 884744 | tf_op jit(solution)/shard_map/cond/branch_1_fun/ppermute | solution.py:256
  26.3 5.9 %collective-permute-done.17.there_ref.v_ref = bf16[256,1024]{1,0:T(8,128)(2,1)S(1)} collective-permute-done((bf16[256,1024]{1,0:T(8,128)(2,1)S(1)}, bf16[256,1024]{1,0:T(8,128)(2,1)S(1)}, u32[]{:S(2)}, u32[]{:S(2)}) %collective-permute-start.17) | collective-permute-done | bytes 524320 | tf_op jit(solution)/shard_map/cond/branch_1_fun/ppermute | solution.py:256
  32.3 2.7 %collective-permute-start.18 = (bf16[256,1024]{1,0:T(8,128)(2,1)S(1)}, bf16[256,1024]{1,0:T(8,128)(2,1)S(1)}, u32[]{:S(2)}, u32[]{:S(2)}) collective-permute-start(bf16[256,1024]{1,0:T(8,128)(2,1)S(1)} %pick_v.3), channel_id=1, source_target_pairs={{0,4},{4,0},{8,12},{12,8},{16,20},{20,16},{24,28},{28,24},{1,5},{5... | collective-permute-start | bytes 1572872 | tf_op jit(solution)/shard_map/cond/branch_1_fun/ppermute | solution.py:259
  35.0 7.6 %collective-permute-done.10.from_ref.one_ref = bf16[144,1024]{1,0:T(8,128)(2,1)S(1)} collective-permute-done((bf16[144,1024]{1,0:T(8,128)(2,1)S(1)}, bf16[144,1024]{1,0:T(8,128)(2,1)S(1)}, u32[]{:S(2)}, u32[]{:S(2)}) %collective-permute-start.10) | collective-permute-done | bytes 294944 | tf_op jit(solution)/shard_map/cond/branch_1_fun/ppermute | solution.py:256
  42.5 0.0 collective-permute-done.12.k_ref
  42.6 0.1 pair.3
  42.6 4.5 %collective-permute-start.13 = (bf16[256,1024]{1,0:T(8,128)(2,1)S(1)}, bf16[256,1024]{1,0:T(8,128)(2,1)S(1)}, u32[]{:S(2)}, u32[]{:S(2)}) collective-permute-start(bf16[256,1024]{1,0:T(8,128)(2,1)S(1)} %pair.3), channel_id=1, source_target_pairs={{0,8},{4,12},{8,16},{12,20},{16,24},{20,28},{1,9},{5,13},{9,17},{1... | collective-permute-start | bytes 1572872 | tf_op jit(solution)/shard_map/cond/branch_1_fun/ppermute | solution.py:256
  47.1 0.0 copy-start.7
  47.1 0.0 copy-start.9
  47.2 0.0 copy-start.11
  47.2 0.0 copy-start.13
  47.2 0.0 copy-start.15
  47.2 1.1 %soft_2.3 = (f32[256,2048]{1,0:T(8,128)S(1)}, f32[256,1024]{1,0:T(8,128)S(1)}) custom-call(s32[256,128]{1,0:T(8,128)S(1)} %get-tuple-element.80.starts_ref, bf16[256,1024]{1,0:T(8,128)(2,1)S(1)} %copy-done.1, bf16[256,1024]{1,0:T(8,128)(2,1)S(1)} %collective-permute-done.11.there_ref.k_ref, bf16[256,1024]{1,0:T(8,128)(2,1)S(1)} %collective-permute-done.17.there_ref.v_ref, ...), custom_call_target="tpu_custom_call" | custom-call | tf_op jit(solution)/shard_map/cond/branch_1_fun/soft_2/pallas_call | solution.py:227
  48.3 2.2 %collective-permute-done.18.v_ref = bf16[256,1024]{1,0:T(8,128)(2,1)S(1)} collective-permute-done((bf16[256,1024]{1,0:T(8,128)(2,1)S(1)}, bf16[256,1024]{1,0:T(8,128)(2,1)S(1)}, u32[]{:S(2)}, u32[]{:S(2)}) %collective-permute-start.18) | collective-permute-done | bytes 524320 | tf_op jit(solution)/shard_map/cond/branch_1_fun/ppermute | solution.py:259
  50.6 5.3 %collective-permute-start.19 = (bf16[128,1024]{1,0:T(8,128)(2,1)S(1)}, bf16[128,1024]{1,0:T(8,128)(2,1)S(1)}, u32[]{:S(2)}, u32[]{:S(2)}) collective-permute-start(bf16[128,1024]{1,0:T(8,128)(2,1)S(1)} %nearest.3), channel_id=1, source_target_pairs={{0,8},{4,12},{8,16},{12,20},{16,24},{20,28},{1,9},{5,13},{9,17},{1... | collective-permute-start | bytes 786440 | tf_op jit(solution)/shard_map/cond/branch_1_fun/ppermute | solution.py:256
  55.9 0.0 collective-permute-done.13.two_ref.k_ref
  55.9 0.0 copy-done.7
  55.9 0.0 copy-done.9
  55.9 0.0 copy-done.11
  55.9 1.5 %lin.3 = (f32[256,1024]{1,0:T(8,128)S(1)}, f32[8,256]{1,0:T(8,128)S(1)}) custom-call(s32[256,128]{1,0:T(8,128)S(1)} %get-tuple-element.80.starts_ref, bf16[256,1024]{1,0:T(8,128)(2,1)S(1)} %copy-done.11, bf16[256,1024]{1,0:T(8,128)(2,1)S(1)} %copy-done.7, bf16[256,1024]{1,0:T(8,128)(2,1)S(1)} %copy-done.9, bf16[256,1024]{1,0:T(8,128)(2,1)S(1)} %copy-done.13, ...), custom_call_target="tpu_custom_call" | custom-call | tf_op jit(solution)/shard_map/cond/branch_1_fun/lin/pallas_call | solution.py:227
  57.4 0.0 collective-permute-start.14
  57.4 1.6 %collective-permute-start.15 = (f32[8,256]{1,0:T(8,128)S(1)}, f32[8,256]{1,0:T(8,128)S(1)}, u32[]{:S(2)}, u32[]{:S(2)}) collective-permute-start(f32[8,256]{1,0:T(8,128)S(1)} %get-tuple-element.99.refs_0_), channel_id=1, source_target_pairs={{0,2},{1,3},{2,0},{3,1},{4,6},{5,7},{6,4},{7,5},{8,10},{9,11},{10,... | collective-permute-start | bytes 24584 | tf_op jit(solution)/shard_map/cond/branch_1_fun/ppermute | solution.py:264
  59.0 1.4 %collective-permute-start.16 = (f32[8,256]{1,0:T(8,128)S(1)}, f32[8,256]{1,0:T(8,128)S(1)}, u32[]{:S(2)}, u32[]{:S(2)}) collective-permute-start(f32[8,256]{1,0:T(8,128)S(1)} %get-tuple-element.99.refs_0_), channel_id=1, source_target_pairs={{0,3},{1,0},{2,1},{3,2},{4,7},{5,4},{6,5},{7,6},{8,11},{9,8},{10,9... | collective-permute-start | bytes 24584 | tf_op jit(solution)/shard_map/cond/branch_1_fun/ppermute | solution.py:264
  60.5 1.1 %soft_1.3 = (f32[256,2048]{1,0:T(8,128)S(1)}, f32[256,1024]{1,0:T(8,128)S(1)}) custom-call(s32[256,128]{1,0:T(8,128)S(1)} %get-tuple-element.80.starts_ref, bf16[256,1024]{1,0:T(8,128)(2,1)S(1)} %copy-done.1, bf16[256,1024]{1,0:T(8,128)(2,1)S(1)} %collective-permute-done.12.k_ref, bf16[256,1024]{1,0:T(8,128)(2,1)S(1)} %collective-permute-done.18.v_ref, ...), custom_call_target="tpu_custom_call" | custom-call | tf_op jit(solution)/shard_map/cond/branch_1_fun/soft_1/pallas_call | solution.py:227
  61.6 1.0 %soft_weigh.3 = (bf16[256,1024]{1,0:T(8,128)(2,1)S(1)}, f32[256,1024]{1,0:T(8,128)S(1)}, f32[256,1024]{1,0:T(8,128)S(1)}) custom-call(s32[256,128]{1,0:T(8,128)S(1)} %get-tuple-element.80.starts_ref, bf16[256,1024]{1,0:T(8,128)(2,1)S(1)} %copy-done.1, bf16[256,1024]{1,0:T(8,128)(2,1)S(1)} %collective-permute-done.13.two_ref.k_ref, ...), custom_call_target="tpu_custom_call" | custom-call | tf_op jit(solution)/shard_map/cond/branch_1_fun/soft_weigh/pallas_call | solution.py:227
  62.6 0.0 collective-permute-done.19.v_ref
  62.7 1.1 %soft_last.3 = bf16[256,1024]{1,0:T(8,128)(2,1)} custom-call(bf16[256,1024]{1,0:T(8,128)(2,1)S(1)} %get-tuple-element.109.p_ref, bf16[128,1024]{1,0:T(8,128)(2,1)S(1)} %collective-permute-done.19.v_ref, f32[256,1024]{1,0:T(8,128)S(1)} %get-tuple-element.110.acc_ref, f32[256,1024]{1,0:T(8,128)S(1)} %get-tuple-element.111.inv_ref), custom_call_target="tpu_custom_call" | custom-call | tf_op jit(solution)/shard_map/cond/branch_1_fun/soft_last/pallas_call | solution.py:227
  63.8 0.0 collective-permute-done.14.refs_1_
  63.8 0.0 collective-permute-done.15.refs_2_
  63.8 0.0 collective-permute-done.16.refs_3_
  63.8 1.1 %norm.3 = bf16[256,1024]{1,0:T(8,128)(2,1)} custom-call(f32[256,1024]{1,0:T(8,128)S(1)} %get-tuple-element.98.y_ref, f32[8,256]{1,0:T(8,128)S(1)} %get-tuple-element.99.refs_0_, f32[8,256]{1,0:T(8,128)S(1)} %collective-permute-done.14.refs_1_, f32[8,256]{1,0:T(8,128)S(1)} %collective-permute-done.15.refs_2_, f32[8,256]{1,0:T(8,128)S(1)} %collective-permute-done.16.refs_3_), custom_call_target="tpu_custom_call" | custom-call | tf_op jit(solution)/shard_map/cond/branch_1_fun/norm/pallas_call | solution.py:227
  (6 shorter events, 0.1 us)
Async XLA Ops:
  2.8 8.6 %copy-start.5 = (bf16[256,1024]{1,0:T(8,128)(2,1)S(1)}, bf16[256,1024]{1,0:T(8,128)(2,1)}, u32[]{:S(2)}) copy-start(bf16[256,1024]{1,0:T(8,128)(2,1)} %get-tuple-element.100.v_ref.own_ref) | copy-start | bytes 1572868 | tf_op jit(solution)/shard_map/cond
  2.8 12.1 %copy-start.1 = (bf16[256,1024]{1,0:T(8,128)(2,1)S(1)}, bf16[256,1024]{1,0:T(8,128)(2,1)}, u32[]{:S(2)}) copy-start(bf16[256,1024]{1,0:T(8,128)(2,1)} %get-tuple-element.95.q_ref) | copy-start | bytes 1572868 | tf_op jit(solution)/shard_map/cond
  2.8 12.1 %copy-start.3 = (bf16[256,1024]{1,0:T(8,128)(2,1)S(1)}, bf16[256,1024]{1,0:T(8,128)(2,1)}, u32[]{:S(2)}) copy-start(bf16[256,1024]{1,0:T(8,128)(2,1)} %get-tuple-element.97.k_ref.own_ref) | copy-start | bytes 1572868 | tf_op jit(solution)/shard_map/cond
  4.7 17.6 %collective-permute-start.11 = (bf16[256,1024]{1,0:T(8,128)(2,1)}, bf16[256,1024]{1,0:T(8,128)(2,1)S(1)}, u32[]{:S(2)}, u32[]{:S(2)}) collective-permute-start(bf16[256,1024]{1,0:T(8,128)(2,1)} %get-tuple-element.97.k_ref.own_ref), channel_id=1, source_target_pairs={{0,8},{4,12},{8,16},{12,20},{16,24},{20,28},{1,9},{5,13},{9,17},{1... | collective-permute-start | bytes 1572872 | tf_op jit(solution)/shard_map/cond/branch_1_fun/ppermute | solution.py:256
  11.4 20.8 %collective-permute-start.17 = (bf16[256,1024]{1,0:T(8,128)(2,1)S(1)}, bf16[256,1024]{1,0:T(8,128)(2,1)S(1)}, u32[]{:S(2)}, u32[]{:S(2)}) collective-permute-start(bf16[256,1024]{1,0:T(8,128)(2,1)S(1)} %copy-done.5), channel_id=1, source_target_pairs={{0,8},{4,12},{8,16},{12,20},{16,24},{20,28},{1,9},{5,13},{9,17},{1... | collective-permute-start | bytes 1572872 | tf_op jit(solution)/shard_map/cond/branch_1_fun/ppermute | solution.py:256
  22.3 20.3 %collective-permute-start.12 = (bf16[256,1024]{1,0:T(8,128)(2,1)S(1)}, bf16[256,1024]{1,0:T(8,128)(2,1)S(1)}, u32[]{:S(2)}, u32[]{:S(2)}) collective-permute-start(bf16[256,1024]{1,0:T(8,128)(2,1)S(1)} %pick_k.3), channel_id=1, source_target_pairs={{0,4},{4,0},{8,12},{12,8},{16,20},{20,16},{24,28},{28,24},{1,5},{5... | collective-permute-start | bytes 1572872 | tf_op jit(solution)/shard_map/cond/branch_1_fun/ppermute | solution.py:259
  23.8 18.7 %collective-permute-start.10 = (bf16[144,1024]{1,0:T(8,128)(2,1)S(1)}, bf16[144,1024]{1,0:T(8,128)(2,1)S(1)}, u32[]{:S(2)}, u32[]{:S(2)}) collective-permute-start(bf16[144,1024]{1,0:T(8,128)(2,1)S(1)} %get-tuple-element.91), channel_id=1, source_target_pairs={{0,4},{4,8},{8,12},{12,16},{16,20},{20,24},{24,28},{1,5},{5,9},{9,... | collective-permute-start | bytes 884744 | tf_op jit(solution)/shard_map/cond/branch_1_fun/ppermute | solution.py:256
  32.3 18.3 %collective-permute-start.18 = (bf16[256,1024]{1,0:T(8,128)(2,1)S(1)}, bf16[256,1024]{1,0:T(8,128)(2,1)S(1)}, u32[]{:S(2)}, u32[]{:S(2)}) collective-permute-start(bf16[256,1024]{1,0:T(8,128)(2,1)S(1)} %pick_v.3), channel_id=1, source_target_pairs={{0,4},{4,0},{8,12},{12,8},{16,20},{20,16},{24,28},{28,24},{1,5},{5... | collective-permute-start | bytes 1572872 | tf_op jit(solution)/shard_map/cond/branch_1_fun/ppermute | solution.py:259
  42.6 13.3 %collective-permute-start.13 = (bf16[256,1024]{1,0:T(8,128)(2,1)S(1)}, bf16[256,1024]{1,0:T(8,128)(2,1)S(1)}, u32[]{:S(2)}, u32[]{:S(2)}) collective-permute-start(bf16[256,1024]{1,0:T(8,128)(2,1)S(1)} %pair.3), channel_id=1, source_target_pairs={{0,8},{4,12},{8,16},{12,20},{16,24},{20,28},{1,9},{5,13},{9,17},{1... | collective-permute-start | bytes 1572872 | tf_op jit(solution)/shard_map/cond/branch_1_fun/ppermute | solution.py:256
  47.1 8.8 %copy-start.7 = (bf16[256,1024]{1,0:T(8,128)(2,1)S(1)}, bf16[256,1024]{1,0:T(8,128)(2,1)}, u32[]{:S(2)}) copy-start(bf16[256,1024]{1,0:T(8,128)(2,1)} %get-tuple-element.82.k_ref) | copy-start | bytes 1572868 | tf_op jit(solution)/shard_map/cond
  47.1 8.8 %copy-start.9 = (bf16[256,1024]{1,0:T(8,128)(2,1)S(1)}, bf16[256,1024]{1,0:T(8,128)(2,1)}, u32[]{:S(2)}) copy-start(bf16[256,1024]{1,0:T(8,128)(2,1)} %get-tuple-element.83.v_ref) | copy-start | bytes 1572868 | tf_op jit(solution)/shard_map/cond
  47.2 8.8 %copy-start.11 = (bf16[256,1024]{1,0:T(8,128)(2,1)S(1)}, bf16[256,1024]{1,0:T(8,128)(2,1)}, u32[]{:S(2)}) copy-start(bf16[256,1024]{1,0:T(8,128)(2,1)} %get-tuple-element.81.q_ref) | copy-start | bytes 1572868 | tf_op jit(solution)/shard_map/cond
  47.2 8.8 %copy-start.13 = (bf16[256,1024]{1,0:T(8,128)(2,1)S(1)}, bf16[256,1024]{1,0:T(8,128)(2,1)}, u32[]{:S(2)}) copy-start(bf16[256,1024]{1,0:T(8,128)(2,1)} %get-tuple-element.84.gate_ref) | copy-start | bytes 1572868 | tf_op jit(solution)/shard_map/cond
  47.2 8.8 %copy-start.15 = (f32[1024]{0:T(1024)S(1)}, f32[1024]{0:T(1024)}, u32[]{:S(2)}) copy-start(f32[1024]{0:T(1024)} %get-tuple-element.85) | copy-start | bytes 12292 | tf_op jit(solution)/shard_map/cond
  50.6 12.1 %collective-permute-start.19 = (bf16[128,1024]{1,0:T(8,128)(2,1)S(1)}, bf16[128,1024]{1,0:T(8,128)(2,1)S(1)}, u32[]{:S(2)}, u32[]{:S(2)}) collective-permute-start(bf16[128,1024]{1,0:T(8,128)(2,1)S(1)} %nearest.3), channel_id=1, source_target_pairs={{0,8},{4,12},{8,16},{12,20},{16,24},{20,28},{1,9},{5,13},{9,17},{1... | collective-permute-start | bytes 786440 | tf_op jit(solution)/shard_map/cond/branch_1_fun/ppermute | solution.py:256
  57.4 6.3 %collective-permute-start.14 = (f32[8,256]{1,0:T(8,128)S(1)}, f32[8,256]{1,0:T(8,128)S(1)}, u32[]{:S(2)}, u32[]{:S(2)}) collective-permute-start(f32[8,256]{1,0:T(8,128)S(1)} %get-tuple-element.99.refs_0_), channel_id=1, source_target_pairs={{0,1},{1,2},{2,3},{3,0},{4,5},{5,6},{6,7},{7,4},{8,9},{9,10},{10,1... | collective-permute-start | bytes 24584 | tf_op jit(solution)/shard_map/cond/branch_1_fun/ppermute | solution.py:264
  57.4 6.3 %collective-permute-start.15 = (f32[8,256]{1,0:T(8,128)S(1)}, f32[8,256]{1,0:T(8,128)S(1)}, u32[]{:S(2)}, u32[]{:S(2)}) collective-permute-start(f32[8,256]{1,0:T(8,128)S(1)} %get-tuple-element.99.refs_0_), channel_id=1, source_target_pairs={{0,2},{1,3},{2,0},{3,1},{4,6},{5,7},{6,4},{7,5},{8,10},{9,11},{10,... | collective-permute-start | bytes 24584 | tf_op jit(solution)/shard_map/cond/branch_1_fun/ppermute | solution.py:264
  59.0 4.7 %collective-permute-start.16 = (f32[8,256]{1,0:T(8,128)S(1)}, f32[8,256]{1,0:T(8,128)S(1)}, u32[]{:S(2)}, u32[]{:S(2)}) collective-permute-start(f32[8,256]{1,0:T(8,128)S(1)} %get-tuple-element.99.refs_0_), channel_id=1, source_target_pairs={{0,3},{1,0},{2,1},{3,2},{4,7},{5,4},{6,5},{7,6},{8,11},{9,8},{10,9... | collective-permute-start | bytes 24584 | tf_op jit(solution)/shard_map/cond/branch_1_fun/ppermute | solution.py:264

commit v3 on v2

--- a/solution.py
+++ b/solution.py
@@ -103,11 +103,25 @@
         out_ref[...] = own_ref[...]
 
 
-def pair_kernel(state_ref, dec_ref, from_ref, k_ref, out_ref):
+def decays_of(pack_ref):
+    return pack_ref[HD : HD + 1, :].astype(F32) + pack_ref[HD + 8 : HD + 9, :].astype(F32)
+
+
+def pair_kernel(state_ref, dec_ref, other_ref, far_ref, k_ref, out_ref):
     reach = out_ref.shape[0] - HD
-    out_ref[0:HD, :] = (
-        state_ref[...] + dec_ref[0:1, :] * from_ref[0:HD, :].astype(F32)
-    ).astype(BF16)
+    odd = lax.rem(lax.axis_index("seq"), 2) == 1
+    other, other_decay = other_ref[0:HD, :].astype(F32), decays_of(other_ref)
+    own, own_decay = state_ref[...], dec_ref[0:1, :]
+
+    @pl.when(odd)
+    def _():
+        out_ref[0:HD, :] = (own + own_decay * other).astype(BF16)
+
+    @pl.when(jnp.logical_not(odd))
+    def _():
+        first = own + own_decay * far_ref[0:HD, :].astype(F32)
+        out_ref[0:HD, :] = (other + other_decay * first).astype(BF16)
+
     out_ref[HD:, :] = k_ref[k_ref.shape[0] - reach :, :]
 
 
@@ -116,7 +130,7 @@
 
 
 def lin_kernel(
-    starts_ref, q_ref, k_ref, v_ref, gate_ref, gain_ref, cum_ref, across_ref, one_ref, two_ref,
+    starts_ref, q_ref, k_ref, v_ref, gate_ref, gain_ref, cum_ref, across_ref, other_ref, two_ref,
     y_ref, sq_ref,
 ):
     rows, width = k_ref.shape
@@ -125,11 +139,15 @@
     base, _ = places(rows)
     enters = starts_ref[...] < base
     squares = jnp.zeros((rows, HD), F32)
-    extra = one_ref[HD:, :].astype(F32)
+    odd = lax.rem(lax.axis_index("seq"), 2) == 1
+    kept = jnp.where(odd, 1.0, 0.0)
+    passed = jnp.where(odd, decays_of(other_ref), 1.0)
     for h in range(heads):
         cols = slice(h * HD, (h + 1) * HD)
-        before = extra[0:1, cols] + extra[8:9, cols]
-        carried = one_ref[0:HD, cols].astype(F32) + before * two_ref[0:HD, cols].astype(F32)
+        carried = (
+            kept * other_ref[0:HD, cols].astype(F32)
+            + passed[:, cols] * two_ref[0:HD, cols].astype(F32)
+        )
         mine = cum_ref[:, cols]
         decayed = jnp.exp(jnp.minimum(wide(mine, rows) - across_ref[h : h + 1, :], 0.0))
         q = q_ref[:, cols]
@@ -252,8 +270,10 @@
     devices = lax.axis_size("seq")
     shape = jax.ShapeDtypeStruct
 
-    def ahead(array, by):
-        return lax.ppermute(array, "seq", [(i, i + by) for i in range(devices - by)])
+    def ahead(array, by, step=1):
+        return lax.ppermute(
+            array, "seq", [(i, i + by) for i in range(0, devices - by, step)]
+        )
 
     def swap(array):
         return lax.ppermute(array, "seq", [(i, i ^ 1) for i in range(devices)])
@@ -280,24 +300,24 @@
         ),
         doc_spans.T, log_decay.T, smem=1,
     )
-    first_key, starts = together((soft_key, starts))
-    k2 = ahead(first_key, 2)
+    k2 = ahead(soft_key, 2)
     pack, state, decay = call(
         state_kernel,
         "state",
         (shape((HD + 16, width), BF16), shape((HD, width), F32), shape((8, width), F32)),
         last_start, cumulative, lin_key, lin_value,
     )
+    other = swap(pack)
     own_value, pack = together((soft_value, pack))
-    one = ahead(pack, 1)
     v2 = ahead(own_value, 2)
     soft = call(soft_own_kernel, "soft_own", sums, starts, soft_query, soft_key, soft_value)
     own_key, top = together((soft_key, soft[1]))
     soft = (soft[0], top)
     k1 = swap(call(pick_kernel, "pick_k", half, k2, own_key))
+    far = ahead(other, 2, 2)
     v1 = swap(call(pick_kernel, "pick_v", half, v2, soft_value))
     pair = call(
-        pair_kernel, "pair", shape((HD + reach, width), BF16), state, decay, one, k1
+        pair_kernel, "pair", shape((HD + reach, width), BF16), state, decay, other, far, k1
     )
     two = ahead(pair, 2)
     soft = call(
@@ -306,17 +326,19 @@
     v1, top = together((v1, soft[1]))
     soft = (soft[0], top)
     v3 = ahead(call(nearest_kernel, "nearest", shape((reach, width), BF16), v1), 2)
+    soft = call(
+        functools.partial(soft_grow_kernel, 1), "soft_1", sums, starts, soft_query, k1, v1, *soft
+    )
+    two, top = together((two, soft[1]))
+    soft = (soft[0], top)
     y, squares = call(
         lin_kernel,
         "lin",
         (shape((rows, width), F32), shape((8, rows), F32)),
         starts, lin_query, lin_key, lin_value, gate_logits, norm_gain.reshape(1, width),
-        cumulative, across, one, two,
+        cumulative, across, other, two,
     )
     parts = everywhere(squares)
-    soft = call(
-        functools.partial(soft_grow_kernel, 1), "soft_1", sums, starts, soft_query, k1, v1, *soft
-    )
     lin_out = call(norm_kernel, "norm", half, y, *parts)
     weights, acc, inv = call(
         functools.partial(soft_weigh_kernel, 3), "soft_weigh",

time: 65.2 us -> 62.1 us (0.952)
  starting transfers between devices: 28 us -> 26 us
  waiting for transfers between devices: 22.1 us -> 21 us
    ppermute x5, waiting for transfers between devices: 19.9 us -> 15.3 us  [ahead(): lax.ppermute(array, 'seq', [(i, i + by) for i in range(0, devices - by, s...]
    ppermute x2 -> x3, waiting for transfers between devices: 2.25 us -> 5.67 us  [swap(): return lax.ppermute(array, 'seq', [(i, i ^ 1) for i in range(devices)])]
    ppermute x5, starting transfers between devices: 20.7 us -> 19.4 us  [ahead(): lax.ppermute(array, 'seq', [(i, i + by) for i in range(0, devices - by, s...]
    ppermute x2 -> x3, starting transfers between devices: 4.27 us -> 3.53 us  [swap(): return lax.ppermute(array, 'seq', [(i, i ^ 1) for i in range(devices)])]
  transfers between devices with their start and end apart: 10 -> 11, of which waited for: 4 -> 6; matrix products, arithmetic and copies ran while one was open for 0% -> 0% of each run, Pallas kernels for 13% -> 17%
where the time goes in v3:
time: 62.1 us; the launch traced here: 61.8 us
  starting transfers between devices  26 us (42%)
  waiting for transfers between devices  21 us (34%)
  Pallas kernels  11.8 us (19%)
  between operations  1.29 us (2%)
  other arithmetic  0.83 us (1%)
  local copies, waits for them, and re-layouts  0.73 us (1%)
    ppermute x5, starting transfers between devices, ahead(): lax.ppermute(array, 'seq', [(i, i + by) for i in range(0, devices - by, s...  19.4 us
    ppermute x5, waiting for transfers between devices, ahead(): lax.ppermute(array, 'seq', [(i, i + by) for i in range(0, devices - by, s...  15.3 us
    pallas_call x13, Pallas kernels, call(): pl.pallas_call(kernel, name=name, out_shape=out_shape, in_specs=[SMEM] *...  11.8 us
    ppermute x3, waiting for transfers between devices, swap(): return lax.ppermute(array, 'seq', [(i, i ^ 1) for i in range(devices)])  5.67 us
    ppermute x3, starting transfers between devices, swap(): return lax.ppermute(array, 'seq', [(i, i ^ 1) for i in range(devices)])  3.53 us
    ppermute x3, starting transfers between devices, everywhere(): lax.ppermute(array, 'head', [(i, (i + by) % count) for i in range(count)])  3.04 us
  transfers between devices with their start and end apart: 11, of which 6 were waited for; matrix products, arithmetic and copies ran while one was open for 0% of the time, Pallas kernels for 17%

profile of v3, /device:TPU:0, one launch (start us, length us, event | category | flops | bytes accessed | tf_op | source)
XLA Modules:
  0.0 61.8 jit_solution(11770781460332614556)
XLA Ops:
  0.6 0.7 %slice_bitcast_fusion = s32[9]{0:T(128)S(1)} fusion(s32[9,2]{0,1:T(2,128)} %param.22), kind=kLoop, calls=%fused_computation.2 | loop fusion | bytes 72 | tf_op jit(solution)/shard_map/le | solution.py:370
  1.3 0.2 select_reduce_fusion
  1.5 0.6 %subtract_reduce_fusion = s32[]{:T(128)} fusion(s32[8]{0:T(128)S(1)} %select_reduce_fusion), kind=kLoop, calls=%fused_computation.1 | loop fusion | flops 23 | bytes 36 | tf_op jit(solution)/shard_map/reduce_max | solution.py:372
  2.8 59.0 %conditional.1 = (bf16[256,1024]{1,0:T(8,128)(2,1)}, bf16[256,1024]{1,0:T(8,128)(2,1)}) conditional(s32[]{:T(128)} %convert_element_type.3, (s32[9,2]{0,1:T(2,128)}, f32[256,8]{0,1:T(8,128)}, f32[1024]{0:T(1024)}, bf16[256,1024]{1,0:T(8,128)(2,1)}, bf16[256,1024]{1,0:T(8,128)(2,1)}, /*index=5*/bf16[256,1024]{1,0:T(8,128)(2,1)}, ...), branch_computations={%region_2.3_spmd, %region_3.4_spmd} | conditional | bytes 30786216 | solution.py:374
  2.8 0.0 copy-start.5
  2.8 0.0 copy-start.1
  2.8 0.0 copy-start.3
  2.9 5.1 %collective-permute-start.13 = (bf16[256,1024]{1,0:T(8,128)(2,1)}, bf16[256,1024]{1,0:T(8,128)(2,1)S(1)}, u32[]{:S(2)}, u32[]{:S(2)}) collective-permute-start(bf16[256,1024]{1,0:T(8,128)(2,1)} %get-tuple-element.93.k_ref.own_ref), channel_id=1, source_target_pairs={{0,8},{4,12},{8,16},{12,20},{16,24},{20,28},{1,9},{5,13},{9,17},{1... | collective-permute-start | bytes 1572872 | tf_op jit(solution)/shard_map/cond/branch_1_fun/ppermute | solution.py:274
  8.0 1.7 %prep.3 = (s32[256,128]{1,0:T(8,128)S(1)}, s32[8,128]{1,0:T(8,128)S(1)}, f32[256,1024]{1,0:T(8,128)S(1)}, f32[8,256]{1,0:T(8,128)S(1)}) custom-call(s32[2,9]{1,0:T(2,128)} %bitcast.13, f32[8,256]{1,0:T(8,128)} %bitcast.9), custom_call_target="tpu_custom_call" | custom-call | tf_op jit(solution)/shard_map/cond/branch_1_fun/prep/pallas_call | solution.py:245
  9.7 1.8 %state.3 = (bf16[144,1024]{1,0:T(8,128)(2,1)S(1)}, f32[128,1024]{1,0:T(8,128)S(1)}, f32[8,1024]{1,0:T(8,128)S(1)}) custom-call(s32[8,128]{1,0:T(8,128)S(1)} %get-tuple-element.85.last_ref, f32[256,1024]{1,0:T(8,128)S(1)} %get-tuple-element.83.cum_ref, bf16[256,1024]{1,0:T(8,128)(2,1)} %get-tuple-element.79.k_ref, bf16[256,1024]{1,0:T(8,128)(2,1)} %get-tuple-element.80.v_ref), custom_call_target="tpu_custom_call" | custom-call | tf_op jit(solution)/shard_map/cond/branch_1_fun/state/pallas_call | solution.py:245
  11.4 0.0 copy-done.5
  11.4 3.5 %collective-permute-start.16 = (bf16[256,1024]{1,0:T(8,128)(2,1)S(1)}, bf16[256,1024]{1,0:T(8,128)(2,1)S(1)}, u32[]{:S(2)}, u32[]{:S(2)}) collective-permute-start(bf16[256,1024]{1,0:T(8,128)(2,1)S(1)} %copy-done.5), channel_id=1, source_target_pairs={{0,8},{4,12},{8,16},{12,20},{16,24},{20,28},{1,9},{5,13},{9,17},{1... | collective-permute-start | bytes 1572872 | tf_op jit(solution)/shard_map/cond/branch_1_fun/ppermute | solution.py:274
  14.9 1.6 %collective-permute-start.11 = (bf16[144,1024]{1,0:T(8,128)(2,1)S(1)}, bf16[144,1024]{1,0:T(8,128)(2,1)S(1)}, u32[]{:S(2)}, u32[]{:S(2)}) collective-permute-start(bf16[144,1024]{1,0:T(8,128)(2,1)S(1)} %get-tuple-element.86), channel_id=1, source_target_pairs={{0,4},{4,0},{8,12},{12,8},{16,20},{20,16},{24,28},{28,24},{1,5},{5... | collective-permute-start | bytes 884744 | tf_op jit(solution)/shard_map/cond/branch_1_fun/ppermute | solution.py:279
  16.5 0.0 copy-done.1
  16.5 0.9 %soft_own.3 = (f32[256,2048]{1,0:T(8,128)S(1)}, f32[256,1024]{1,0:T(8,128)S(1)}) custom-call(s32[256,128]{1,0:T(8,128)S(1)} %get-tuple-element.77.starts_ref, bf16[256,1024]{1,0:T(8,128)(2,1)S(1)} %copy-done.1, bf16[256,1024]{1,0:T(8,128)(2,1)S(1)} %copy-done.3, bf16[256,1024]{1,0:T(8,128)(2,1)S(1)} %copy-done.5), custom_call_target="tpu_custom_call" | custom-call | tf_op jit(solution)/shard_map/cond/branch_1_fun/soft_own/pallas_call | solution.py:245
  17.4 3.1 %collective-permute-done.13.there_ref.k_ref = bf16[256,1024]{1,0:T(8,128)(2,1)S(1)} collective-permute-done((bf16[256,1024]{1,0:T(8,128)(2,1)}, bf16[256,1024]{1,0:T(8,128)(2,1)S(1)}, u32[]{:S(2)}, u32[]{:S(2)}) %collective-permute-start.13) | collective-permute-done | bytes 524320 | tf_op jit(solution)/shard_map/cond/branch_1_fun/ppermute | solution.py:274
  20.6 1.6 %collective-permute-start.14 = (bf16[256,1024]{1,0:T(8,128)(2,1)S(1)}, bf16[256,1024]{1,0:T(8,128)(2,1)S(1)}, u32[]{:S(2)}, u32[]{:S(2)}) collective-permute-start(bf16[256,1024]{1,0:T(8,128)(2,1)S(1)} %pick_k.3), channel_id=1, source_target_pairs={{0,4},{4,0},{8,12},{12,8},{16,20},{20,16},{24,28},{28,24},{1,5},{5... | collective-permute-start | bytes 1572872 | tf_op jit(solution)/shard_map/cond/branch_1_fun/ppermute | solution.py:279
  22.1 2.8 %collective-permute-done.11.other_ref = bf16[144,1024]{1,0:T(8,128)(2,1)S(1)} collective-permute-done((bf16[144,1024]{1,0:T(8,128)(2,1)S(1)}, bf16[144,1024]{1,0:T(8,128)(2,1)S(1)}, u32[]{:S(2)}, u32[]{:S(2)}) %collective-permute-start.11) | collective-permute-done | bytes 294944 | tf_op jit(solution)/shard_map/cond/branch_1_fun/ppermute | solution.py:279
  24.9 2.9 %collective-permute-start.12 = (bf16[144,1024]{1,0:T(8,128)(2,1)S(1)}, bf16[144,1024]{1,0:T(8,128)(2,1)S(1)}, u32[]{:S(2)}, u32[]{:S(2)}) collective-permute-start(bf16[144,1024]{1,0:T(8,128)(2,1)S(1)} %collective-permute-done.11.other_ref), channel_id=1, source_target_pairs={{0,8},{8,16},{16,24},{1,9},{9,17},{17,25},{2,10},{10,18},{18,26},{... | collective-permute-start | bytes 884744 | tf_op jit(solution)/shard_map/cond/branch_1_fun/ppermute | solution.py:274
  27.9 3.8 %collective-permute-done.16.there_ref.v_ref = bf16[256,1024]{1,0:T(8,128)(2,1)S(1)} collective-permute-done((bf16[256,1024]{1,0:T(8,128)(2,1)S(1)}, bf16[256,1024]{1,0:T(8,128)(2,1)S(1)}, u32[]{:S(2)}, u32[]{:S(2)}) %collective-permute-start.16) | collective-permute-done | bytes 524320 | tf_op jit(solution)/shard_map/cond/branch_1_fun/ppermute | solution.py:274
  31.7 0.4 collective-permute-start.17
  32.1 4.7 %collective-permute-done.12.far_ref = bf16[144,1024]{1,0:T(8,128)(2,1)S(1)} collective-permute-done((bf16[144,1024]{1,0:T(8,128)(2,1)S(1)}, bf16[144,1024]{1,0:T(8,128)(2,1)S(1)}, u32[]{:S(2)}, u32[]{:S(2)}) %collective-permute-start.12) | collective-permute-done | bytes 294944 | tf_op jit(solution)/shard_map/cond/branch_1_fun/ppermute | solution.py:274
  36.9 0.0 collective-permute-done.14.k_ref
  36.9 0.4 pair.3
  37.2 4.4 %collective-permute-start.15 = (bf16[256,1024]{1,0:T(8,128)(2,1)S(1)}, bf16[256,1024]{1,0:T(8,128)(2,1)S(1)}, u32[]{:S(2)}, u32[]{:S(2)}) collective-permute-start(bf16[256,1024]{1,0:T(8,128)(2,1)S(1)} %pair.3), channel_id=1, source_target_pairs={{0,8},{4,12},{8,16},{12,20},{16,24},{20,28},{1,9},{5,13},{9,17},{1... | collective-permute-start | bytes 1572872 | tf_op jit(solution)/shard_map/cond/branch_1_fun/ppermute | solution.py:274
  41.7 1.1 %soft_2.3 = (f32[256,2048]{1,0:T(8,128)S(1)}, f32[256,1024]{1,0:T(8,128)S(1)}) custom-call(s32[256,128]{1,0:T(8,128)S(1)} %get-tuple-element.77.starts_ref, bf16[256,1024]{1,0:T(8,128)(2,1)S(1)} %copy-done.1, bf16[256,1024]{1,0:T(8,128)(2,1)S(1)} %collective-permute-done.13.there_ref.k_ref, bf16[256,1024]{1,0:T(8,128)(2,1)S(1)} %collective-permute-done.16.there_ref.v_ref, ...), custom_call_target="tpu_custom_call" | custom-call | tf_op jit(solution)/shard_map/cond/branch_1_fun/soft_2/pallas_call | solution.py:245
  42.8 2.9 %collective-permute-done.17.v_ref = bf16[256,1024]{1,0:T(8,128)(2,1)S(1)} collective-permute-done((bf16[256,1024]{1,0:T(8,128)(2,1)S(1)}, bf16[256,1024]{1,0:T(8,128)(2,1)S(1)}, u32[]{:S(2)}, u32[]{:S(2)}) %collective-permute-start.17) | collective-permute-done | bytes 524320 | tf_op jit(solution)/shard_map/cond/branch_1_fun/ppermute | solution.py:279
  45.7 3.5 %collective-permute-start.21 = (bf16[128,1024]{1,0:T(8,128)(2,1)S(1)}, bf16[128,1024]{1,0:T(8,128)(2,1)S(1)}, u32[]{:S(2)}, u32[]{:S(2)}) collective-permute-start(bf16[128,1024]{1,0:T(8,128)(2,1)S(1)} %nearest.3), channel_id=1, source_target_pairs={{0,8},{4,12},{8,16},{12,20},{16,24},{20,28},{1,9},{5,13},{9,17},{1... | collective-permute-start | bytes 786440 | tf_op jit(solution)/shard_map/cond/branch_1_fun/ppermute | solution.py:274
  49.2 0.0 copy-start.7
  49.2 0.0 copy-start.9
  49.2 0.0 copy-start.11
  49.2 0.0 copy-start.13
  49.2 0.0 copy-start.15
  49.2 1.1 %soft_1.3 = (f32[256,2048]{1,0:T(8,128)S(1)}, f32[256,1024]{1,0:T(8,128)S(1)}) custom-call(s32[256,128]{1,0:T(8,128)S(1)} %get-tuple-element.77.starts_ref, bf16[256,1024]{1,0:T(8,128)(2,1)S(1)} %copy-done.1, bf16[256,1024]{1,0:T(8,128)(2,1)S(1)} %collective-permute-done.14.k_ref, bf16[256,1024]{1,0:T(8,128)(2,1)S(1)} %collective-permute-done.17.v_ref, ...), custom_call_target="tpu_custom_call" | custom-call | tf_op jit(solution)/shard_map/cond/branch_1_fun/soft_1/pallas_call | solution.py:245
  50.3 3.6 %collective-permute-done.15.two_ref.k_ref = bf16[256,1024]{1,0:T(8,128)(2,1)S(1)} collective-permute-done((bf16[256,1024]{1,0:T(8,128)(2,1)S(1)}, bf16[256,1024]{1,0:T(8,128)(2,1)S(1)}, u32[]{:S(2)}, u32[]{:S(2)}) %collective-permute-start.15) | collective-permute-done | bytes 524320 | tf_op jit(solution)/shard_map/cond/branch_1_fun/ppermute | solution.py:274
  54.0 0.0 copy-done.9
  54.0 0.0 copy-done.13
  54.0 1.5 %lin.3 = (f32[256,1024]{1,0:T(8,128)S(1)}, f32[8,256]{1,0:T(8,128)S(1)}) custom-call(s32[256,128]{1,0:T(8,128)S(1)} %get-tuple-element.77.starts_ref, bf16[256,1024]{1,0:T(8,128)(2,1)S(1)} %copy-done.11, bf16[256,1024]{1,0:T(8,128)(2,1)S(1)} %copy-done.7, bf16[256,1024]{1,0:T(8,128)(2,1)S(1)} %copy-done.9, bf16[256,1024]{1,0:T(8,128)(2,1)S(1)} %copy-done.13, ...), custom_call_target="tpu_custom_call" | custom-call | tf_op jit(solution)/shard_map/cond/branch_1_fun/lin/pallas_call | solution.py:245
  55.5 0.0 collective-permute-start.18
  55.5 1.6 %collective-permute-start.19 = (f32[8,256]{1,0:T(8,128)S(1)}, f32[8,256]{1,0:T(8,128)S(1)}, u32[]{:S(2)}, u32[]{:S(2)}) collective-permute-start(f32[8,256]{1,0:T(8,128)S(1)} %get-tuple-element.104.refs_0_), channel_id=1, source_target_pairs={{0,2},{1,3},{2,0},{3,1},{4,6},{5,7},{6,4},{7,5},{8,10},{9,11},{10,... | collective-permute-start | bytes 24584 | tf_op jit(solution)/shard_map/cond/branch_1_fun/ppermute | solution.py:284
  57.1 1.4 %collective-permute-start.20 = (f32[8,256]{1,0:T(8,128)S(1)}, f32[8,256]{1,0:T(8,128)S(1)}, u32[]{:S(2)}, u32[]{:S(2)}) collective-permute-start(f32[8,256]{1,0:T(8,128)S(1)} %get-tuple-element.104.refs_0_), channel_id=1, source_target_pairs={{0,3},{1,0},{2,1},{3,2},{4,7},{5,4},{6,5},{7,6},{8,11},{9,8},{10,9... | collective-permute-start | bytes 24584 | tf_op jit(solution)/shard_map/cond/branch_1_fun/ppermute | solution.py:284
  58.6 1.0 %soft_weigh.3 = (bf16[256,1024]{1,0:T(8,128)(2,1)S(1)}, f32[256,1024]{1,0:T(8,128)S(1)}, f32[256,1024]{1,0:T(8,128)S(1)}) custom-call(s32[256,128]{1,0:T(8,128)S(1)} %get-tuple-element.77.starts_ref, bf16[256,1024]{1,0:T(8,128)(2,1)S(1)} %copy-done.1, bf16[256,1024]{1,0:T(8,128)(2,1)S(1)} %collective-permute-done.15.two_ref.k_ref, ...), custom_call_target="tpu_custom_call" | custom-call | tf_op jit(solution)/shard_map/cond/branch_1_fun/soft_weigh/pallas_call | solution.py:245
  59.6 0.0 collective-permute-done.21.v_ref
  59.6 1.1 %soft_last.3 = bf16[256,1024]{1,0:T(8,128)(2,1)} custom-call(bf16[256,1024]{1,0:T(8,128)(2,1)S(1)} %get-tuple-element.107.p_ref, bf16[128,1024]{1,0:T(8,128)(2,1)S(1)} %collective-permute-done.21.v_ref, f32[256,1024]{1,0:T(8,128)S(1)} %get-tuple-element.108.acc_ref, f32[256,1024]{1,0:T(8,128)S(1)} %get-tuple-element.109.inv_ref), custom_call_target="tpu_custom_call" | custom-call | tf_op jit(solution)/shard_map/cond/branch_1_fun/soft_last/pallas_call | solution.py:245
  60.7 0.0 collective-permute-done.18.refs_1_
  60.7 0.0 collective-permute-done.19.refs_2_
  60.7 0.0 collective-permute-done.20.refs_3_
  60.7 1.1 %norm.3 = bf16[256,1024]{1,0:T(8,128)(2,1)} custom-call(f32[256,1024]{1,0:T(8,128)S(1)} %get-tuple-element.103.y_ref, f32[8,256]{1,0:T(8,128)S(1)} %get-tuple-element.104.refs_0_, f32[8,256]{1,0:T(8,128)S(1)} %collective-permute-done.18.refs_1_, f32[8,256]{1,0:T(8,128)S(1)} %collective-permute-done.19.refs_2_, f32[8,256]{1,0:T(8,128)S(1)} %collective-permute-done.20.refs_3_), custom_call_target="tpu_custom_call" | custom-call | tf_op jit(solution)/shard_map/cond/branch_1_fun/norm/pallas_call | solution.py:245
  (8 shorter events, 0.1 us)
Async XLA Ops:
  2.8 8.6 %copy-start.5 = (bf16[256,1024]{1,0:T(8,128)(2,1)S(1)}, bf16[256,1024]{1,0:T(8,128)(2,1)}, u32[]{:S(2)}) copy-start(bf16[256,1024]{1,0:T(8,128)(2,1)} %get-tuple-element.94.v_ref.own_ref) | copy-start | bytes 1572868 | tf_op jit(solution)/shard_map/cond
  2.8 13.7 %copy-start.1 = (bf16[256,1024]{1,0:T(8,128)(2,1)S(1)}, bf16[256,1024]{1,0:T(8,128)(2,1)}, u32[]{:S(2)}) copy-start(bf16[256,1024]{1,0:T(8,128)(2,1)} %get-tuple-element.90.q_ref) | copy-start | bytes 1572868 | tf_op jit(solution)/shard_map/cond
  2.8 13.7 %copy-start.3 = (bf16[256,1024]{1,0:T(8,128)(2,1)S(1)}, bf16[256,1024]{1,0:T(8,128)(2,1)}, u32[]{:S(2)}) copy-start(bf16[256,1024]{1,0:T(8,128)(2,1)} %get-tuple-element.93.k_ref.own_ref) | copy-start | bytes 1572868 | tf_op jit(solution)/shard_map/cond
  2.9 17.7 %collective-permute-start.13 = (bf16[256,1024]{1,0:T(8,128)(2,1)}, bf16[256,1024]{1,0:T(8,128)(2,1)S(1)}, u32[]{:S(2)}, u32[]{:S(2)}) collective-permute-start(bf16[256,1024]{1,0:T(8,128)(2,1)} %get-tuple-element.93.k_ref.own_ref), channel_id=1, source_target_pairs={{0,8},{4,12},{8,16},{12,20},{16,24},{20,28},{1,9},{5,13},{9,17},{1... | collective-permute-start | bytes 1572872 | tf_op jit(solution)/shard_map/cond/branch_1_fun/ppermute | solution.py:274
  11.4 20.2 %collective-permute-start.16 = (bf16[256,1024]{1,0:T(8,128)(2,1)S(1)}, bf16[256,1024]{1,0:T(8,128)(2,1)S(1)}, u32[]{:S(2)}, u32[]{:S(2)}) collective-permute-start(bf16[256,1024]{1,0:T(8,128)(2,1)S(1)} %copy-done.5), channel_id=1, source_target_pairs={{0,8},{4,12},{8,16},{12,20},{16,24},{20,28},{1,9},{5,13},{9,17},{1... | collective-permute-start | bytes 1572872 | tf_op jit(solution)/shard_map/cond/branch_1_fun/ppermute | solution.py:274
  14.9 10.0 %collective-permute-start.11 = (bf16[144,1024]{1,0:T(8,128)(2,1)S(1)}, bf16[144,1024]{1,0:T(8,128)(2,1)S(1)}, u32[]{:S(2)}, u32[]{:S(2)}) collective-permute-start(bf16[144,1024]{1,0:T(8,128)(2,1)S(1)} %get-tuple-element.86), channel_id=1, source_target_pairs={{0,4},{4,0},{8,12},{12,8},{16,20},{20,16},{24,28},{28,24},{1,5},{5... | collective-permute-start | bytes 884744 | tf_op jit(solution)/shard_map/cond/branch_1_fun/ppermute | solution.py:279
  20.6 16.3 %collective-permute-start.14 = (bf16[256,1024]{1,0:T(8,128)(2,1)S(1)}, bf16[256,1024]{1,0:T(8,128)(2,1)S(1)}, u32[]{:S(2)}, u32[]{:S(2)}) collective-permute-start(bf16[256,1024]{1,0:T(8,128)(2,1)S(1)} %pick_k.3), channel_id=1, source_target_pairs={{0,4},{4,0},{8,12},{12,8},{16,20},{20,16},{24,28},{28,24},{1,5},{5... | collective-permute-start | bytes 1572872 | tf_op jit(solution)/shard_map/cond/branch_1_fun/ppermute | solution.py:279
  24.9 11.9 %collective-permute-start.12 = (bf16[144,1024]{1,0:T(8,128)(2,1)S(1)}, bf16[144,1024]{1,0:T(8,128)(2,1)S(1)}, u32[]{:S(2)}, u32[]{:S(2)}) collective-permute-start(bf16[144,1024]{1,0:T(8,128)(2,1)S(1)} %collective-permute-done.11.other_ref), channel_id=1, source_target_pairs={{0,8},{8,16},{16,24},{1,9},{9,17},{17,25},{2,10},{10,18},{18,26},{... | collective-permute-start | bytes 884744 | tf_op jit(solution)/shard_map/cond/branch_1_fun/ppermute | solution.py:274
  31.7 13.9 %collective-permute-start.17 = (bf16[256,1024]{1,0:T(8,128)(2,1)S(1)}, bf16[256,1024]{1,0:T(8,128)(2,1)S(1)}, u32[]{:S(2)}, u32[]{:S(2)}) collective-permute-start(bf16[256,1024]{1,0:T(8,128)(2,1)S(1)} %pick_v.3), channel_id=1, source_target_pairs={{0,4},{4,0},{8,12},{12,8},{16,20},{20,16},{24,28},{28,24},{1,5},{5... | collective-permute-start | bytes 1572872 | tf_op jit(solution)/shard_map/cond/branch_1_fun/ppermute | solution.py:279
  37.2 16.8 %collective-permute-start.15 = (bf16[256,1024]{1,0:T(8,128)(2,1)S(1)}, bf16[256,1024]{1,0:T(8,128)(2,1)S(1)}, u32[]{:S(2)}, u32[]{:S(2)}) collective-permute-start(bf16[256,1024]{1,0:T(8,128)(2,1)S(1)} %pair.3), channel_id=1, source_target_pairs={{0,8},{4,12},{8,16},{12,20},{16,24},{20,28},{1,9},{5,13},{9,17},{1... | collective-permute-start | bytes 1572872 | tf_op jit(solution)/shard_map/cond/branch_1_fun/ppermute | solution.py:274
  45.7 13.9 %collective-permute-start.21 = (bf16[128,1024]{1,0:T(8,128)(2,1)S(1)}, bf16[128,1024]{1,0:T(8,128)(2,1)S(1)}, u32[]{:S(2)}, u32[]{:S(2)}) collective-permute-start(bf16[128,1024]{1,0:T(8,128)(2,1)S(1)} %nearest.3), channel_id=1, source_target_pairs={{0,8},{4,12},{8,16},{12,20},{16,24},{20,28},{1,9},{5,13},{9,17},{1... | collective-permute-start | bytes 786440 | tf_op jit(solution)/shard_map/cond/branch_1_fun/ppermute | solution.py:274
  49.2 4.8 %copy-start.7 = (bf16[256,1024]{1,0:T(8,128)(2,1)S(1)}, bf16[256,1024]{1,0:T(8,128)(2,1)}, u32[]{:S(2)}) copy-start(bf16[256,1024]{1,0:T(8,128)(2,1)} %get-tuple-element.79.k_ref) | copy-start | bytes 1572868 | tf_op jit(solution)/shard_map/cond
  49.2 4.8 %copy-start.9 = (bf16[256,1024]{1,0:T(8,128)(2,1)S(1)}, bf16[256,1024]{1,0:T(8,128)(2,1)}, u32[]{:S(2)}) copy-start(bf16[256,1024]{1,0:T(8,128)(2,1)} %get-tuple-element.80.v_ref) | copy-start | bytes 1572868 | tf_op jit(solution)/shard_map/cond
  49.2 4.8 %copy-start.11 = (bf16[256,1024]{1,0:T(8,128)(2,1)S(1)}, bf16[256,1024]{1,0:T(8,128)(2,1)}, u32[]{:S(2)}) copy-start(bf16[256,1024]{1,0:T(8,128)(2,1)} %get-tuple-element.78.q_ref) | copy-start | bytes 1572868 | tf_op jit(solution)/shard_map/cond
  49.2 4.8 %copy-start.13 = (bf16[256,1024]{1,0:T(8,128)(2,1)S(1)}, bf16[256,1024]{1,0:T(8,128)(2,1)}, u32[]{:S(2)}) copy-start(bf16[256,1024]{1,0:T(8,128)(2,1)} %get-tuple-element.81.gate_ref) | copy-start | bytes 1572868 | tf_op jit(solution)/shard_map/cond
  49.2 4.8 %copy-start.15 = (f32[1024]{0:T(1024)S(1)}, f32[1024]{0:T(1024)}, u32[]{:S(2)}) copy-start(f32[1024]{0:T(1024)} %get-tuple-element.82) | copy-start | bytes 12292 | tf_op jit(solution)/shard_map/cond
  55.5 5.2 %collective-permute-start.18 = (f32[8,256]{1,0:T(8,128)S(1)}, f32[8,256]{1,0:T(8,128)S(1)}, u32[]{:S(2)}, u32[]{:S(2)}) collective-permute-start(f32[8,256]{1,0:T(8,128)S(1)} %get-tuple-element.104.refs_0_), channel_id=1, source_target_pairs={{0,1},{1,2},{2,3},{3,0},{4,5},{5,6},{6,7},{7,4},{8,9},{9,10},{10,1... | collective-permute-start | bytes 24584 | tf_op jit(solution)/shard_map/cond/branch_1_fun/ppermute | solution.py:284
  55.5 5.2 %collective-permute-start.19 = (f32[8,256]{1,0:T(8,128)S(1)}, f32[8,256]{1,0:T(8,128)S(1)}, u32[]{:S(2)}, u32[]{:S(2)}) collective-permute-start(f32[8,256]{1,0:T(8,128)S(1)} %get-tuple-element.104.refs_0_), channel_id=1, source_target_pairs={{0,2},{1,3},{2,0},{3,1},{4,6},{5,7},{6,4},{7,5},{8,10},{9,11},{10,... | collective-permute-start | bytes 24584 | tf_op jit(solution)/shard_map/cond/branch_1_fun/ppermute | solution.py:284
  57.1 3.6 %collective-permute-start.20 = (f32[8,256]{1,0:T(8,128)S(1)}, f32[8,256]{1,0:T(8,128)S(1)}, u32[]{:S(2)}, u32[]{:S(2)}) collective-permute-start(f32[8,256]{1,0:T(8,128)S(1)} %get-tuple-element.104.refs_0_), channel_id=1, source_target_pairs={{0,3},{1,0},{2,1},{3,2},{4,7},{5,4},{6,5},{7,6},{8,11},{9,8},{10,9... | collective-permute-start | bytes 24584 | tf_op jit(solution)/shard_map/cond/branch_1_fun/ppermute | solution.py:284

commit v4 on v3

--- a/solution.py
+++ b/solution.py
@@ -9,6 +9,7 @@
 
 HALF_MODEL_HEADS = 32
 HD = 128
+SPAN = 3
 LANES = 128
 NEG = -1e30
 SOFT_SCALE = HD ** (-0.5) * 1.4426950408889634
@@ -129,46 +130,42 @@
     out_ref[...] = v_ref[v_ref.shape[0] - out_ref.shape[0] :, :]
 
 
-def lin_kernel(
-    starts_ref, q_ref, k_ref, v_ref, gate_ref, gain_ref, cum_ref, across_ref, other_ref, two_ref,
-    y_ref, sq_ref,
+def inner_kernel(
+    starts_ref, q_ref, k_ref, v_ref, gate_ref, gain_ref, cum_ref, across_ref, inner_ref, scale_ref
 ):
     rows, width = k_ref.shape
-    heads = width // HD
     allowed = key_bias(starts_ref, rows, rows, 0) == 0.0
+    for h in range(width // HD):
+        cols = slice(h * HD, (h + 1) * HD)
+        decayed = jnp.exp(jnp.minimum(wide(cum_ref[:, cols], rows) - across_ref[h : h + 1, :], 0.0))
+        scores = dot(q_ref[:, cols], k_ref[:, cols], ((1,), (1,)))
+        weights = jnp.where(allowed, scores * decayed, 0.0).astype(BF16)
+        inner_ref[:, cols] = dot(weights, v_ref[:, cols], ((1,), (0,)))
+        scale_ref[:, cols] = gain_ref[:, cols] * jax.nn.sigmoid(gate_ref[:, cols].astype(F32))
+
+
+def cross_kernel(
+    starts_ref, q_ref, cum_ref, inner_ref, other_ref, two_ref, mixture_ref, sq_ref
+):
+    rows, width = q_ref.shape
     base, _ = places(rows)
     enters = starts_ref[...] < base
-    squares = jnp.zeros((rows, HD), F32)
     odd = lax.rem(lax.axis_index("seq"), 2) == 1
     kept = jnp.where(odd, 1.0, 0.0)
     passed = jnp.where(odd, decays_of(other_ref), 1.0)
-    for h in range(heads):
+    squares = jnp.zeros((rows, HD), F32)
+    for h in range(width // HD):
         cols = slice(h * HD, (h + 1) * HD)
         carried = (
             kept * other_ref[0:HD, cols].astype(F32)
             + passed[:, cols] * two_ref[0:HD, cols].astype(F32)
         )
-        mine = cum_ref[:, cols]
-        decayed = jnp.exp(jnp.minimum(wide(mine, rows) - across_ref[h : h + 1, :], 0.0))
-        q = q_ref[:, cols]
-        scores = dot(q, k_ref[:, cols], ((1,), (1,)))
-        weights = jnp.where(allowed, scores * decayed, 0.0).astype(BF16)
-        cross = dot(q, carried.astype(BF16), ((1,), (0,)))
-        mixture = dot(weights, v_ref[:, cols], ((1,), (0,))) + (
-            cross * jnp.where(enters, jnp.exp(mine), 0.0)
-        )
+        cross = dot(q_ref[:, cols], carried.astype(BF16), ((1,), (0,)))
+        mixture = inner_ref[:, cols] + cross * jnp.where(enters, jnp.exp(cum_ref[:, cols]), 0.0)
         squares = squares + mixture * mixture
-        gate = jax.nn.sigmoid(gate_ref[:, cols].astype(F32))
-        y_ref[:, cols] = mixture * gain_ref[:, cols] * gate
+        mixture_ref[:, cols] = mixture
     ones = jnp.ones((8, HD), BF16)
     sq_ref[...] = sum(dot(ones, part, ((1,), (1,))) for part in split3(squares))
-
-
-def norm_kernel(y_ref, *refs):
-    *parts, lin_ref = refs
-    total = jnp.transpose(sum(part[...] for part in parts))[:, 0:1]
-    norm = lax.rsqrt(total / (HALF_MODEL_HEADS * HD) + 1e-06)
-    lin_ref[...] = (y_ref[...] * norm).astype(BF16)
 
 
 def with_ones(v):
@@ -229,12 +226,18 @@
         inv_ref[:, cols] = inv
 
 
-def soft_last_kernel(p_ref, v_ref, acc_ref, inv_ref, soft_ref):
+def last_kernel(p_ref, v_ref, acc_ref, inv_ref, mixture_ref, scale_ref, *refs):
+    *parts, lin_ref, soft_ref = refs
     keys = v_ref.shape[0]
+    total = jnp.transpose(sum(part[...] for part in parts))[:, 0:1]
+    norm = jnp.broadcast_to(
+        lax.rsqrt(total / (HALF_MODEL_HEADS * HD) + 1e-06), (acc_ref.shape[0], HD)
+    )
     for h in range(acc_ref.shape[1] // HD):
         cols = slice(h * HD, (h + 1) * HD)
         more = dot(p_ref[:, h * keys : (h + 1) * keys], v_ref[:, cols], ((1,), (0,)))
         soft_ref[:, cols] = (acc_ref[:, cols] + more * inv_ref[:, cols]).astype(BF16)
+        lin_ref[:, cols] = (mixture_ref[:, cols] * norm * scale_ref[:, cols]).astype(BF16)
 
 
 SMEM = pl.BlockSpec(memory_space=pltpu.SMEM)
@@ -323,7 +326,12 @@
     soft = call(
         functools.partial(soft_grow_kernel, 2), "soft_2", sums, starts, soft_query, k2, v2, *soft
     )
-    v1, top = together((v1, soft[1]))
+    inner, scale = call(
+        inner_kernel, "inner", (shape((rows, width), F32), shape((rows, width), F32)),
+        starts, lin_query, lin_key, lin_value, gate_logits, norm_gain.reshape(1, width),
+        cumulative, across,
+    )
+    v1, top, inner = together((v1, soft[1], inner))
     soft = (soft[0], top)
     v3 = ahead(call(nearest_kernel, "nearest", shape((reach, width), BF16), v1), 2)
     soft = call(
@@ -331,25 +339,22 @@
     )
     two, top = together((two, soft[1]))
     soft = (soft[0], top)
-    y, squares = call(
-        lin_kernel,
-        "lin",
-        (shape((rows, width), F32), shape((8, rows), F32)),
-        starts, lin_query, lin_key, lin_value, gate_logits, norm_gain.reshape(1, width),
-        cumulative, across, other, two,
+    mixture, squares = call(
+        cross_kernel, "cross", (shape((rows, width), F32), shape((8, rows), F32)),
+        starts, lin_query, cumulative, inner, other, two,
     )
     parts = everywhere(squares)
-    lin_out = call(norm_kernel, "norm", half, y, *parts)
     weights, acc, inv = call(
-        functools.partial(soft_weigh_kernel, 3), "soft_weigh",
+        functools.partial(soft_weigh_kernel, SPAN), "soft_weigh",
         (
             shape((rows, heads * reach), BF16), shape((rows, width), F32),
             shape((rows, width), F32),
         ),
         starts, soft_query, two, *soft,
     )
-    soft_out = call(soft_last_kernel, "soft_last", half, weights, v3, acc, inv)
-    return (lin_out, soft_out)
+    return call(
+        last_kernel, "last", (half, half), weights, v3, acc, inv, mixture, scale, *parts
+    )
 
 
 def shards(
@@ -366,13 +371,11 @@
     doc_spans,
 ):
     rows = lin_query.shape[0]
-    blocks = rows * jnp.arange(lax.axis_size("seq"), dtype=jnp.int32)
-    begun = doc_spans[None, :, 0] <= blocks[:, None]
-    starts = jnp.max(jnp.where(begun, doc_spans[None, :, 0], 0), axis=1)
-    farthest = jnp.max(blocks - starts)
     reach = rows // 2
+    firsts, ends = doc_spans[:, 0], doc_spans[:, 1]
+    farthest = jnp.max((ends - 1) // rows * rows - firsts)
     return lax.cond(
-        farthest <= 2 * rows + reach,
+        farthest <= (SPAN - 1) * rows + reach,
         functools.partial(program, reach),
         functools.partial(program, rows),
         lin_query, lin_key, lin_value, log_decay, gate_logits, norm_gain, soft_query, soft_key,

time: 62.1 us -> 60.8 us (0.979)
  waiting for transfers between devices: 21 us -> 20 us
  local copies, waits for them, and re-layouts: 0.73 us -> 0.05 us
    ppermute x3, waiting for transfers between devices: 5.67 us -> 4.73 us  [swap(): return lax.ppermute(array, 'seq', [(i, i ^ 1) for i in range(devices)])]
    le x1 -> x0, local copies, waits for them, and re-layouts: 0.68 us -> none  [shards(): begun = doc_spans[None, :, 0] <= blocks[:, None]]
    reduce_max x2 -> x1, other arithmetic: 0.82 us -> 1.4 us  [shards(): farthest = jnp.max((ends - 1) // rows * rows - firsts)]
  transfers between devices with their start and end apart: 11 -> 11, of which waited for: 6 -> 7; matrix products, arithmetic and copies ran while one was open for 0% -> 0% of each run, Pallas kernels for 17% -> 16%
where the time goes in v4:
time: 60.8 us; the launch traced here: 60.2 us
  starting transfers between devices  25.9 us (43%)
  waiting for transfers between devices  20 us (33%)
  Pallas kernels  11.3 us (19%)
  other arithmetic  1.4 us (2%)
  between operations  1.28 us (2%)
    ppermute x5, starting transfers between devices, ahead(): lax.ppermute(array, 'seq', [(i, i + by) for i in range(0, devices - by, s...  19.3 us
    ppermute x5, waiting for transfers between devices, ahead(): lax.ppermute(array, 'seq', [(i, i + by) for i in range(0, devices - by, s...  15 us
    pallas_call x13, Pallas kernels, call(): pl.pallas_call(kernel, name=name, out_shape=out_shape, in_specs=[SMEM] *...  11.3 us
    ppermute x3, waiting for transfers between devices, swap(): return lax.ppermute(array, 'seq', [(i, i ^ 1) for i in range(devices)])  4.73 us
    ppermute x3, starting transfers between devices, swap(): return lax.ppermute(array, 'seq', [(i, i ^ 1) for i in range(devices)])  3.53 us
    ppermute x3, starting transfers between devices, everywhere(): lax.ppermute(array, 'head', [(i, (i + by) % count) for i in range(count)])  3.02 us
    reduce_max x1, other arithmetic, shards(): farthest = jnp.max((ends - 1) // rows * rows - firsts)  1.4 us
  transfers between devices with their start and end apart: 11, of which 7 were waited for; matrix products, arithmetic and copies ran while one was open for 0% of the time, Pallas kernels for 16%

profile of v4, /device:TPU:0, one launch (start us, length us, event | category | flops | bytes accessed | tf_op | source)
XLA Modules:
  0.0 60.2 jit_solution(5878483469866176714)
XLA Ops:
  0.6 1.4 %fusion = s32[]{:T(128)} fusion(s32[9,2]{0,1:T(2,128)} %param.22), kind=kLoop, calls=%fused_computation.5 | loop fusion | flops 170 | bytes 76 | tf_op jit(solution)/shard_map/reduce_max | solution.py:376
  2.7 57.6 %conditional.1 = ((bf16[256,1024]{1,0:T(8,128)(2,1)}, bf16[256,1024]{1,0:T(8,128)(2,1)})) conditional(s32[]{:T(128)} %convert_element_type.3, (s32[9,2]{0,1:T(2,128)}, f32[256,8]{0,1:T(8,128)}, bf16[256,1024]{1,0:T(8,128)(2,1)}, bf16[256,1024]{1,0:T(8,128)(2,1)}, bf16[256,1024]{1,0:T(8,128)(2,1)}, /*index=5*/bf16[256,1024]{1,0:T(8,128)(2,1)}, ...), branch_computations={%region_1.2_spmd, %region_2.3_spmd} | conditional | bytes 30786208 | solution.py:377
  2.7 0.0 copy-start.5
  2.7 0.0 copy-start.1
  2.7 0.0 copy-start.3
  2.7 5.1 %collective-permute-start.13 = (bf16[256,1024]{1,0:T(8,128)(2,1)}, bf16[256,1024]{1,0:T(8,128)(2,1)S(1)}, u32[]{:S(2)}, u32[]{:S(2)}) collective-permute-start(bf16[256,1024]{1,0:T(8,128)(2,1)} %get-tuple-element.92.k_ref.own_ref), channel_id=1, source_target_pairs={{0,8},{4,12},{8,16},{12,20},{16,24},{20,28},{1,9},{5,13},{9,17},{1... | collective-permute-start | bytes 1572872 | tf_op jit(solution)/shard_map/cond/branch_1_fun/ppermute | solution.py:277
  7.8 1.7 %prep.3 = (s32[256,128]{1,0:T(8,128)S(1)}, s32[8,128]{1,0:T(8,128)S(1)}, f32[256,1024]{1,0:T(8,128)S(1)}, f32[8,256]{1,0:T(8,128)S(1)}) custom-call(s32[2,9]{1,0:T(2,128)} %bitcast.25, f32[8,256]{1,0:T(8,128)} %bitcast.21), custom_call_target="tpu_custom_call" | custom-call | tf_op jit(solution)/shard_map/cond/branch_1_fun/prep/pallas_call | solution.py:248
  9.6 1.8 %state.3 = (bf16[144,1024]{1,0:T(8,128)(2,1)S(1)}, f32[128,1024]{1,0:T(8,128)S(1)}, f32[8,1024]{1,0:T(8,128)S(1)}) custom-call(s32[8,128]{1,0:T(8,128)S(1)} %get-tuple-element.82.last_ref, f32[256,1024]{1,0:T(8,128)S(1)} %get-tuple-element.83.cum_ref, bf16[256,1024]{1,0:T(8,128)(2,1)} %get-tuple-element.84.k_ref, bf16[256,1024]{1,0:T(8,128)(2,1)} %get-tuple-element.85.v_ref), custom_call_target="tpu_custom_call" | custom-call | tf_op jit(solution)/shard_map/cond/branch_1_fun/state/pallas_call | solution.py:248
  11.3 0.0 copy-done.5
  11.3 3.5 %collective-permute-start.16 = (bf16[256,1024]{1,0:T(8,128)(2,1)S(1)}, bf16[256,1024]{1,0:T(8,128)(2,1)S(1)}, u32[]{:S(2)}, u32[]{:S(2)}) collective-permute-start(bf16[256,1024]{1,0:T(8,128)(2,1)S(1)} %copy-done.5), channel_id=1, source_target_pairs={{0,8},{4,12},{8,16},{12,20},{16,24},{20,28},{1,9},{5,13},{9,17},{1... | collective-permute-start | bytes 1572872 | tf_op jit(solution)/shard_map/cond/branch_1_fun/ppermute | solution.py:277
  14.8 1.6 %collective-permute-start.11 = (bf16[144,1024]{1,0:T(8,128)(2,1)S(1)}, bf16[144,1024]{1,0:T(8,128)(2,1)S(1)}, u32[]{:S(2)}, u32[]{:S(2)}) collective-permute-start(bf16[144,1024]{1,0:T(8,128)(2,1)S(1)} %get-tuple-element.88), channel_id=1, source_target_pairs={{0,4},{4,0},{8,12},{12,8},{16,20},{20,16},{24,28},{28,24},{1,5},{5... | collective-permute-start | bytes 884744 | tf_op jit(solution)/shard_map/cond/branch_1_fun/ppermute | solution.py:282
  16.4 0.0 copy-done.1
  16.4 0.0 copy-done.3
  16.4 0.9 %soft_own.3 = (f32[256,2048]{1,0:T(8,128)S(1)}, f32[256,1024]{1,0:T(8,128)S(1)}) custom-call(s32[256,128]{1,0:T(8,128)S(1)} %get-tuple-element.80.starts_ref, bf16[256,1024]{1,0:T(8,128)(2,1)S(1)} %copy-done.1, bf16[256,1024]{1,0:T(8,128)(2,1)S(1)} %copy-done.3, bf16[256,1024]{1,0:T(8,128)(2,1)S(1)} %copy-done.5), custom_call_target="tpu_custom_call" | custom-call | tf_op jit(solution)/shard_map/cond/branch_1_fun/soft_own/pallas_call | solution.py:248
  17.3 3.1 %collective-permute-done.13.there_ref.k_ref = bf16[256,1024]{1,0:T(8,128)(2,1)S(1)} collective-permute-done((bf16[256,1024]{1,0:T(8,128)(2,1)}, bf16[256,1024]{1,0:T(8,128)(2,1)S(1)}, u32[]{:S(2)}, u32[]{:S(2)}) %collective-permute-start.13) | collective-permute-done | bytes 524320 | tf_op jit(solution)/shard_map/cond/branch_1_fun/ppermute | solution.py:277
  20.5 0.0 copy-start.7
  20.5 0.0 copy-start.9
  20.5 0.0 copy-start.11
  20.5 0.0 copy-start.13
  20.5 0.0 copy-start.15
  20.5 1.6 %collective-permute-start.14 = (bf16[256,1024]{1,0:T(8,128)(2,1)S(1)}, bf16[256,1024]{1,0:T(8,128)(2,1)S(1)}, u32[]{:S(2)}, u32[]{:S(2)}) collective-permute-start(bf16[256,1024]{1,0:T(8,128)(2,1)S(1)} %pick_k.3), channel_id=1, source_target_pairs={{0,4},{4,0},{8,12},{12,8},{16,20},{20,16},{24,28},{28,24},{1,5},{5... | collective-permute-start | bytes 1572872 | tf_op jit(solution)/shard_map/cond/branch_1_fun/ppermute | solution.py:282
  22.1 2.7 %collective-permute-done.11.other_ref = bf16[144,1024]{1,0:T(8,128)(2,1)S(1)} collective-permute-done((bf16[144,1024]{1,0:T(8,128)(2,1)S(1)}, bf16[144,1024]{1,0:T(8,128)(2,1)S(1)}, u32[]{:S(2)}, u32[]{:S(2)}) %collective-permute-start.11) | collective-permute-done | bytes 294944 | tf_op jit(solution)/shard_map/cond/branch_1_fun/ppermute | solution.py:282
  24.8 2.9 %collective-permute-start.12 = (bf16[144,1024]{1,0:T(8,128)(2,1)S(1)}, bf16[144,1024]{1,0:T(8,128)(2,1)S(1)}, u32[]{:S(2)}, u32[]{:S(2)}) collective-permute-start(bf16[144,1024]{1,0:T(8,128)(2,1)S(1)} %collective-permute-done.11.other_ref), channel_id=1, source_target_pairs={{0,8},{8,16},{16,24},{1,9},{9,17},{17,25},{2,10},{10,18},{18,26},{... | collective-permute-start | bytes 884744 | tf_op jit(solution)/shard_map/cond/branch_1_fun/ppermute | solution.py:277
  27.7 3.8 %collective-permute-done.16.there_ref.v_ref = bf16[256,1024]{1,0:T(8,128)(2,1)S(1)} collective-permute-done((bf16[256,1024]{1,0:T(8,128)(2,1)S(1)}, bf16[256,1024]{1,0:T(8,128)(2,1)S(1)}, u32[]{:S(2)}, u32[]{:S(2)}) %collective-permute-start.16) | collective-permute-done | bytes 524320 | tf_op jit(solution)/shard_map/cond/branch_1_fun/ppermute | solution.py:277
  31.6 0.2 pick_v.3
  31.8 0.4 collective-permute-start.17
  32.2 4.5 %collective-permute-done.12.far_ref = bf16[144,1024]{1,0:T(8,128)(2,1)S(1)} collective-permute-done((bf16[144,1024]{1,0:T(8,128)(2,1)S(1)}, bf16[144,1024]{1,0:T(8,128)(2,1)S(1)}, u32[]{:S(2)}, u32[]{:S(2)}) %collective-permute-start.12) | collective-permute-done | bytes 294944 | tf_op jit(solution)/shard_map/cond/branch_1_fun/ppermute | solution.py:277
  36.7 0.0 collective-permute-done.14.k_ref
  36.7 0.2 pair.3
  36.9 4.4 %collective-permute-start.15 = (bf16[256,1024]{1,0:T(8,128)(2,1)S(1)}, bf16[256,1024]{1,0:T(8,128)(2,1)S(1)}, u32[]{:S(2)}, u32[]{:S(2)}) collective-permute-start(bf16[256,1024]{1,0:T(8,128)(2,1)S(1)} %pair.3), channel_id=1, source_target_pairs={{0,8},{4,12},{8,16},{12,20},{16,24},{20,28},{1,9},{5,13},{9,17},{1... | collective-permute-start | bytes 1572872 | tf_op jit(solution)/shard_map/cond/branch_1_fun/ppermute | solution.py:277
  41.4 0.0 copy-done.7
  41.4 0.0 copy-done.9
  41.4 1.0 %inner.3 = (f32[256,1024]{1,0:T(8,128)S(1)}, f32[256,1024]{1,0:T(8,128)S(1)}) custom-call(s32[256,128]{1,0:T(8,128)S(1)} %get-tuple-element.80.starts_ref, bf16[256,1024]{1,0:T(8,128)(2,1)S(1)} %copy-done.11, bf16[256,1024]{1,0:T(8,128)(2,1)S(1)} %copy-done.7, bf16[256,1024]{1,0:T(8,128)(2,1)S(1)} %copy-done.9, bf16[256,1024]{1,0:T(8,128)(2,1)S(1)} %copy-done.13, ...), custom_call_target="tpu_custom_call" | custom-call | tf_op jit(solution)/shard_map/cond/branch_1_fun/inner/pallas_call | solution.py:248
  42.4 1.1 %soft_2.3 = (f32[256,2048]{1,0:T(8,128)S(1)}, f32[256,1024]{1,0:T(8,128)S(1)}) custom-call(s32[256,128]{1,0:T(8,128)S(1)} %get-tuple-element.80.starts_ref, bf16[256,1024]{1,0:T(8,128)(2,1)S(1)} %copy-done.1, bf16[256,1024]{1,0:T(8,128)(2,1)S(1)} %collective-permute-done.13.there_ref.k_ref, bf16[256,1024]{1,0:T(8,128)(2,1)S(1)} %collective-permute-done.16.there_ref.v_ref, ...), custom_call_target="tpu_custom_call" | custom-call | tf_op jit(solution)/shard_map/cond/branch_1_fun/soft_2/pallas_call | solution.py:248
  43.6 2.0 %collective-permute-done.17.v_ref = bf16[256,1024]{1,0:T(8,128)(2,1)S(1)} collective-permute-done((bf16[256,1024]{1,0:T(8,128)(2,1)S(1)}, bf16[256,1024]{1,0:T(8,128)(2,1)S(1)}, u32[]{:S(2)}, u32[]{:S(2)}) %collective-permute-start.17) | collective-permute-done | bytes 524320 | tf_op jit(solution)/shard_map/cond/branch_1_fun/ppermute | solution.py:282
  45.6 3.5 %collective-permute-start.18 = (bf16[128,1024]{1,0:T(8,128)(2,1)S(1)}, bf16[128,1024]{1,0:T(8,128)(2,1)S(1)}, u32[]{:S(2)}, u32[]{:S(2)}) collective-permute-start(bf16[128,1024]{1,0:T(8,128)(2,1)S(1)} %nearest.3), channel_id=1, source_target_pairs={{0,8},{4,12},{8,16},{12,20},{16,24},{20,28},{1,9},{5,13},{9,17},{1... | collective-permute-start | bytes 786440 | tf_op jit(solution)/shard_map/cond/branch_1_fun/ppermute | solution.py:277
  49.1 1.1 %soft_1.3 = (f32[256,2048]{1,0:T(8,128)S(1)}, f32[256,1024]{1,0:T(8,128)S(1)}) custom-call(s32[256,128]{1,0:T(8,128)S(1)} %get-tuple-element.80.starts_ref, bf16[256,1024]{1,0:T(8,128)(2,1)S(1)} %copy-done.1, bf16[256,1024]{1,0:T(8,128)(2,1)S(1)} %collective-permute-done.14.k_ref, bf16[256,1024]{1,0:T(8,128)(2,1)S(1)} %collective-permute-done.17.v_ref, ...), custom_call_target="tpu_custom_call" | custom-call | tf_op jit(solution)/shard_map/cond/branch_1_fun/soft_1/pallas_call | solution.py:248
  50.2 3.5 %collective-permute-done.15.k_ref.two_ref = bf16[256,1024]{1,0:T(8,128)(2,1)S(1)} collective-permute-done((bf16[256,1024]{1,0:T(8,128)(2,1)S(1)}, bf16[256,1024]{1,0:T(8,128)(2,1)S(1)}, u32[]{:S(2)}, u32[]{:S(2)}) %collective-permute-start.15) | collective-permute-done | bytes 524320 | tf_op jit(solution)/shard_map/cond/branch_1_fun/ppermute | solution.py:277
  53.7 0.7 %cross.3 = (f32[256,1024]{1,0:T(8,128)S(1)}, f32[8,256]{1,0:T(8,128)S(1)}) custom-call(s32[256,128]{1,0:T(8,128)S(1)} %get-tuple-element.80.starts_ref, bf16[256,1024]{1,0:T(8,128)(2,1)S(1)} %copy-done.11, f32[256,1024]{1,0:T(8,128)S(1)} %get-tuple-element.83.cum_ref, f32[256,1024]{1,0:T(8,128)S(1)} %get-tuple-element.112.inner_ref, ...), custom_call_target="tpu_custom_call" | custom-call | tf_op jit(solution)/shard_map/cond/branch_1_fun/cross/pallas_call | solution.py:248
  54.4 0.0 collective-permute-start.19
  54.4 1.6 %collective-permute-start.20 = (f32[8,256]{1,0:T(8,128)S(1)}, f32[8,256]{1,0:T(8,128)S(1)}, u32[]{:S(2)}, u32[]{:S(2)}) collective-permute-start(f32[8,256]{1,0:T(8,128)S(1)} %get-tuple-element.115.refs_0_), channel_id=1, source_target_pairs={{0,2},{1,3},{2,0},{3,1},{4,6},{5,7},{6,4},{7,5},{8,10},{9,11},{10,... | collective-permute-start | bytes 24584 | tf_op jit(solution)/shard_map/cond/branch_1_fun/ppermute | solution.py:287
  56.0 1.4 %collective-permute-start.21 = (f32[8,256]{1,0:T(8,128)S(1)}, f32[8,256]{1,0:T(8,128)S(1)}, u32[]{:S(2)}, u32[]{:S(2)}) collective-permute-start(f32[8,256]{1,0:T(8,128)S(1)} %get-tuple-element.115.refs_0_), channel_id=1, source_target_pairs={{0,3},{1,0},{2,1},{3,2},{4,7},{5,4},{6,5},{7,6},{8,11},{9,8},{10,9... | collective-permute-start | bytes 24584 | tf_op jit(solution)/shard_map/cond/branch_1_fun/ppermute | solution.py:287
  57.4 1.0 %soft_weigh.3 = (bf16[256,1024]{1,0:T(8,128)(2,1)S(1)}, f32[256,1024]{1,0:T(8,128)S(1)}, f32[256,1024]{1,0:T(8,128)S(1)}) custom-call(s32[256,128]{1,0:T(8,128)S(1)} %get-tuple-element.80.starts_ref, bf16[256,1024]{1,0:T(8,128)(2,1)S(1)} %copy-done.1, bf16[256,1024]{1,0:T(8,128)(2,1)S(1)} %collective-permute-done.15.k_ref.two_ref, ...), custom_call_target="tpu_custom_call" | custom-call | tf_op jit(solution)/shard_map/cond/branch_1_fun/soft_weigh/pallas_call | solution.py:248
  58.5 0.0 collective-permute-done.18.v_ref
  58.5 0.0 collective-permute-done.19.refs_1_
  58.5 0.0 collective-permute-done.20.refs_2_
  58.5 0.3 collective-permute-done.21.refs_3_
  58.8 1.4 %last.3 = (bf16[256,1024]{1,0:T(8,128)(2,1)}, bf16[256,1024]{1,0:T(8,128)(2,1)}) custom-call(bf16[256,1024]{1,0:T(8,128)(2,1)S(1)} %get-tuple-element.109.p_ref, bf16[128,1024]{1,0:T(8,128)(2,1)S(1)} %collective-permute-done.18.v_ref, f32[256,1024]{1,0:T(8,128)S(1)} %get-tuple-element.110.acc_ref, f32[256,1024]{1,0:T(8,128)S(1)} %get-tuple-element.111.inv_ref, ...), custom_call_target="tpu_custom_call" | custom-call | tf_op jit(solution)/shard_map/cond/branch_1_fun/last/pallas_call | solution.py:248
  (5 shorter events, 0.1 us)
Async XLA Ops:
  2.7 8.6 %copy-start.5 = (bf16[256,1024]{1,0:T(8,128)(2,1)S(1)}, bf16[256,1024]{1,0:T(8,128)(2,1)}, u32[]{:S(2)}) copy-start(bf16[256,1024]{1,0:T(8,128)(2,1)} %get-tuple-element.93.v_ref.own_ref) | copy-start | bytes 1572868 | tf_op jit(solution)/shard_map/cond
  2.7 13.7 %copy-start.1 = (bf16[256,1024]{1,0:T(8,128)(2,1)S(1)}, bf16[256,1024]{1,0:T(8,128)(2,1)}, u32[]{:S(2)}) copy-start(bf16[256,1024]{1,0:T(8,128)(2,1)} %get-tuple-element.81.q_ref) | copy-start | bytes 1572868 | tf_op jit(solution)/shard_map/cond
  2.7 13.7 %copy-start.3 = (bf16[256,1024]{1,0:T(8,128)(2,1)S(1)}, bf16[256,1024]{1,0:T(8,128)(2,1)}, u32[]{:S(2)}) copy-start(bf16[256,1024]{1,0:T(8,128)(2,1)} %get-tuple-element.92.k_ref.own_ref) | copy-start | bytes 1572868 | tf_op jit(solution)/shard_map/cond
  2.7 17.7 %collective-permute-start.13 = (bf16[256,1024]{1,0:T(8,128)(2,1)}, bf16[256,1024]{1,0:T(8,128)(2,1)S(1)}, u32[]{:S(2)}, u32[]{:S(2)}) collective-permute-start(bf16[256,1024]{1,0:T(8,128)(2,1)} %get-tuple-element.92.k_ref.own_ref), channel_id=1, source_target_pairs={{0,8},{4,12},{8,16},{12,20},{16,24},{20,28},{1,9},{5,13},{9,17},{1... | collective-permute-start | bytes 1572872 | tf_op jit(solution)/shard_map/cond/branch_1_fun/ppermute | solution.py:277
  11.3 20.2 %collective-permute-start.16 = (bf16[256,1024]{1,0:T(8,128)(2,1)S(1)}, bf16[256,1024]{1,0:T(8,128)(2,1)S(1)}, u32[]{:S(2)}, u32[]{:S(2)}) collective-permute-start(bf16[256,1024]{1,0:T(8,128)(2,1)S(1)} %copy-done.5), channel_id=1, source_target_pairs={{0,8},{4,12},{8,16},{12,20},{16,24},{20,28},{1,9},{5,13},{9,17},{1... | collective-permute-start | bytes 1572872 | tf_op jit(solution)/shard_map/cond/branch_1_fun/ppermute | solution.py:277
  14.8 10.0 %collective-permute-start.11 = (bf16[144,1024]{1,0:T(8,128)(2,1)S(1)}, bf16[144,1024]{1,0:T(8,128)(2,1)S(1)}, u32[]{:S(2)}, u32[]{:S(2)}) collective-permute-start(bf16[144,1024]{1,0:T(8,128)(2,1)S(1)} %get-tuple-element.88), channel_id=1, source_target_pairs={{0,4},{4,0},{8,12},{12,8},{16,20},{20,16},{24,28},{28,24},{1,5},{5... | collective-permute-start | bytes 884744 | tf_op jit(solution)/shard_map/cond/branch_1_fun/ppermute | solution.py:282
  20.5 20.9 %copy-start.7 = (bf16[256,1024]{1,0:T(8,128)(2,1)S(1)}, bf16[256,1024]{1,0:T(8,128)(2,1)}, u32[]{:S(2)}) copy-start(bf16[256,1024]{1,0:T(8,128)(2,1)} %get-tuple-element.84.k_ref) | copy-start | bytes 1572868 | tf_op jit(solution)/shard_map/cond
  20.5 20.9 %copy-start.9 = (bf16[256,1024]{1,0:T(8,128)(2,1)S(1)}, bf16[256,1024]{1,0:T(8,128)(2,1)}, u32[]{:S(2)}) copy-start(bf16[256,1024]{1,0:T(8,128)(2,1)} %get-tuple-element.85.v_ref) | copy-start | bytes 1572868 | tf_op jit(solution)/shard_map/cond
  20.5 20.9 %copy-start.11 = (bf16[256,1024]{1,0:T(8,128)(2,1)S(1)}, bf16[256,1024]{1,0:T(8,128)(2,1)}, u32[]{:S(2)}) copy-start(bf16[256,1024]{1,0:T(8,128)(2,1)} %get-tuple-element.97.q_ref) | copy-start | bytes 1572868 | tf_op jit(solution)/shard_map/cond
  20.5 20.9 %copy-start.13 = (bf16[256,1024]{1,0:T(8,128)(2,1)S(1)}, bf16[256,1024]{1,0:T(8,128)(2,1)}, u32[]{:S(2)}) copy-start(bf16[256,1024]{1,0:T(8,128)(2,1)} %get-tuple-element.98.gate_ref) | copy-start | bytes 1572868 | tf_op jit(solution)/shard_map/cond
  20.5 20.9 %copy-start.15 = (f32[1024]{0:T(1024)S(1)}, f32[1024]{0:T(1024)}, u32[]{:S(2)}) copy-start(f32[1024]{0:T(1024)} %get-tuple-element.99) | copy-start | bytes 12292 | tf_op jit(solution)/shard_map/cond
  20.5 16.2 %collective-permute-start.14 = (bf16[256,1024]{1,0:T(8,128)(2,1)S(1)}, bf16[256,1024]{1,0:T(8,128)(2,1)S(1)}, u32[]{:S(2)}, u32[]{:S(2)}) collective-permute-start(bf16[256,1024]{1,0:T(8,128)(2,1)S(1)} %pick_k.3), channel_id=1, source_target_pairs={{0,4},{4,0},{8,12},{12,8},{16,20},{20,16},{24,28},{28,24},{1,5},{5... | collective-permute-start | bytes 1572872 | tf_op jit(solution)/shard_map/cond/branch_1_fun/ppermute | solution.py:282
  24.8 11.9 %collective-permute-start.12 = (bf16[144,1024]{1,0:T(8,128)(2,1)S(1)}, bf16[144,1024]{1,0:T(8,128)(2,1)S(1)}, u32[]{:S(2)}, u32[]{:S(2)}) collective-permute-start(bf16[144,1024]{1,0:T(8,128)(2,1)S(1)} %collective-permute-done.11.other_ref), channel_id=1, source_target_pairs={{0,8},{8,16},{16,24},{1,9},{9,17},{17,25},{2,10},{10,18},{18,26},{... | collective-permute-start | bytes 884744 | tf_op jit(solution)/shard_map/cond/branch_1_fun/ppermute | solution.py:277
  31.8 13.8 %collective-permute-start.17 = (bf16[256,1024]{1,0:T(8,128)(2,1)S(1)}, bf16[256,1024]{1,0:T(8,128)(2,1)S(1)}, u32[]{:S(2)}, u32[]{:S(2)}) collective-permute-start(bf16[256,1024]{1,0:T(8,128)(2,1)S(1)} %pick_v.3), channel_id=1, source_target_pairs={{0,4},{4,0},{8,12},{12,8},{16,20},{20,16},{24,28},{28,24},{1,5},{5... | collective-permute-start | bytes 1572872 | tf_op jit(solution)/shard_map/cond/branch_1_fun/ppermute | solution.py:282
  36.9 16.8 %collective-permute-start.15 = (bf16[256,1024]{1,0:T(8,128)(2,1)S(1)}, bf16[256,1024]{1,0:T(8,128)(2,1)S(1)}, u32[]{:S(2)}, u32[]{:S(2)}) collective-permute-start(bf16[256,1024]{1,0:T(8,128)(2,1)S(1)} %pair.3), channel_id=1, source_target_pairs={{0,8},{4,12},{8,16},{12,20},{16,24},{20,28},{1,9},{5,13},{9,17},{1... | collective-permute-start | bytes 1572872 | tf_op jit(solution)/shard_map/cond/branch_1_fun/ppermute | solution.py:277
  45.6 12.9 %collective-permute-start.18 = (bf16[128,1024]{1,0:T(8,128)(2,1)S(1)}, bf16[128,1024]{1,0:T(8,128)(2,1)S(1)}, u32[]{:S(2)}, u32[]{:S(2)}) collective-permute-start(bf16[128,1024]{1,0:T(8,128)(2,1)S(1)} %nearest.3), channel_id=1, source_target_pairs={{0,8},{4,12},{8,16},{12,20},{16,24},{20,28},{1,9},{5,13},{9,17},{1... | collective-permute-start | bytes 786440 | tf_op jit(solution)/shard_map/cond/branch_1_fun/ppermute | solution.py:277
  54.4 4.1 %collective-permute-start.19 = (f32[8,256]{1,0:T(8,128)S(1)}, f32[8,256]{1,0:T(8,128)S(1)}, u32[]{:S(2)}, u32[]{:S(2)}) collective-permute-start(f32[8,256]{1,0:T(8,128)S(1)} %get-tuple-element.115.refs_0_), channel_id=1, source_target_pairs={{0,1},{1,2},{2,3},{3,0},{4,5},{5,6},{6,7},{7,4},{8,9},{9,10},{10,1... | collective-permute-start | bytes 24584 | tf_op jit(solution)/shard_map/cond/branch_1_fun/ppermute | solution.py:287
  54.4 4.1 %collective-permute-start.20 = (f32[8,256]{1,0:T(8,128)S(1)}, f32[8,256]{1,0:T(8,128)S(1)}, u32[]{:S(2)}, u32[]{:S(2)}) collective-permute-start(f32[8,256]{1,0:T(8,128)S(1)} %get-tuple-element.115.refs_0_), channel_id=1, source_target_pairs={{0,2},{1,3},{2,0},{3,1},{4,6},{5,7},{6,4},{7,5},{8,10},{9,11},{10,... | collective-permute-start | bytes 24584 | tf_op jit(solution)/shard_map/cond/branch_1_fun/ppermute | solution.py:287
  56.0 2.8 %collective-permute-start.21 = (f32[8,256]{1,0:T(8,128)S(1)}, f32[8,256]{1,0:T(8,128)S(1)}, u32[]{:S(2)}, u32[]{:S(2)}) collective-permute-start(f32[8,256]{1,0:T(8,128)S(1)} %get-tuple-element.115.refs_0_), channel_id=1, source_target_pairs={{0,3},{1,0},{2,1},{3,2},{4,7},{5,4},{6,5},{7,6},{8,11},{9,8},{10,9... | collective-permute-start | bytes 24584 | tf_op jit(solution)/shard_map/cond/branch_1_fun/ppermute | solution.py:287

commit v5 on v4

--- a/solution.py
+++ b/solution.py
@@ -120,10 +120,14 @@
 
     @pl.when(jnp.logical_not(odd))
     def _():
-        first = own + own_decay * far_ref[0:HD, :].astype(F32)
+        first = own + own_decay * far_ref[...].astype(F32)
         out_ref[0:HD, :] = (other + other_decay * first).astype(BF16)
 
     out_ref[HD:, :] = k_ref[k_ref.shape[0] - reach :, :]
+
+
+def first_kernel(a_ref, out_ref):
+    out_ref[...] = a_ref[0 : out_ref.shape[0], :]
 
 
 def nearest_kernel(v_ref, out_ref):
@@ -317,7 +321,7 @@
     own_key, top = together((soft_key, soft[1]))
     soft = (soft[0], top)
     k1 = swap(call(pick_kernel, "pick_k", half, k2, own_key))
-    far = ahead(other, 2, 2)
+    far = ahead(call(first_kernel, "states", shape((HD, width), BF16), other), 2, 2)
     v1 = swap(call(pick_kernel, "pick_v", half, v2, soft_value))
     pair = call(
         pair_kernel, "pair", shape((HD + reach, width), BF16), state, decay, other, far, k1
@@ -372,8 +376,8 @@
 ):
     rows = lin_query.shape[0]
     reach = rows // 2
-    firsts, ends = doc_spans[:, 0], doc_spans[:, 1]
-    farthest = jnp.max((ends - 1) // rows * rows - firsts)
+    firsts, lasts = doc_spans[:, 0], doc_spans[:, 1] - 1
+    farthest = jnp.max(lasts - lax.rem(lasts, jnp.int32(rows)) - firsts)
     return lax.cond(
         farthest <= (SPAN - 1) * rows + reach,
         functools.partial(program, reach),

time: 60.8 us -> 60.1 us (0.988)
    ppermute x5, waiting for transfers between devices: 15 us -> 13.6 us  [ahead(): lax.ppermute(array, 'seq', [(i, i + by) for i in range(0, devices - by, s...]
    ppermute x3, waiting for transfers between devices: 4.73 us -> 5.47 us  [swap(): return lax.ppermute(array, 'seq', [(i, i ^ 1) for i in range(devices)])]
    pallas_call x13 -> x14, Pallas kernels: 11.3 us -> 11.3 us  [call(): pl.pallas_call(kernel, name=name, out_shape=out_shape, in_specs=[SMEM] *...]
  transfers between devices with their start and end apart: 11 -> 11, of which waited for: 7 -> 7; matrix products, arithmetic and copies ran while one was open for 0% -> 0% of each run, Pallas kernels for 16% -> 17%
where the time goes in v5:
time: 60.1 us; the launch traced here: 59.5 us
  starting transfers between devices  25.9 us (43%)
  waiting for transfers between devices  19.4 us (32%)
  Pallas kernels  11.3 us (19%)
  other arithmetic  1.4 us (2%)
  between operations  1.28 us (2%)
    ppermute x5, starting transfers between devices, ahead(): lax.ppermute(array, 'seq', [(i, i + by) for i in range(0, devices - by, s...  19.3 us
    ppermute x5, waiting for transfers between devices, ahead(): lax.ppermute(array, 'seq', [(i, i + by) for i in range(0, devices - by, s...  13.6 us
    pallas_call x14, Pallas kernels, call(): pl.pallas_call(kernel, name=name, out_shape=out_shape, in_specs=[SMEM] *...  11.3 us
    ppermute x3, waiting for transfers between devices, swap(): return lax.ppermute(array, 'seq', [(i, i ^ 1) for i in range(devices)])  5.47 us
    ppermute x3, starting transfers between devices, swap(): return lax.ppermute(array, 'seq', [(i, i ^ 1) for i in range(devices)])  3.53 us
    ppermute x3, starting transfers between devices, everywhere(): lax.ppermute(array, 'head', [(i, (i + by) % count) for i in range(count)])  3.02 us
    reduce_max x1, other arithmetic, shards(): farthest = jnp.max(lasts - lax.rem(lasts, jnp.int32(rows)) - firsts)  1.4 us
  transfers between devices with their start and end apart: 11, of which 7 were waited for; matrix products, arithmetic and copies ran while one was open for 0% of the time, Pallas kernels for 17%

profile of v5, /device:TPU:0, one launch (start us, length us, event | category | flops | bytes accessed | tf_op | source)
XLA Modules:
  0.0 59.5 jit_solution(7448157518989172082)
XLA Ops:
  0.6 1.4 %fusion.3 = s32[]{:T(128)} fusion(s32[9,2]{0,1:T(2,128)} %param.22), kind=kLoop, calls=%fused_computation.5 | loop fusion | flops 89 | bytes 76 | tf_op jit(solution)/shard_map/reduce_max | solution.py:380
  2.7 56.9 %conditional.1 = ((bf16[256,1024]{1,0:T(8,128)(2,1)}, bf16[256,1024]{1,0:T(8,128)(2,1)})) conditional(s32[]{:T(128)} %convert_element_type.3, (s32[9,2]{0,1:T(2,128)}, f32[256,8]{0,1:T(8,128)}, bf16[256,1024]{1,0:T(8,128)(2,1)}, bf16[256,1024]{1,0:T(8,128)(2,1)}, bf16[256,1024]{1,0:T(8,128)(2,1)}, /*index=5*/bf16[256,1024]{1,0:T(8,128)(2,1)}, ...), branch_computations={%region_1.0_spmd, %region_2.0_spmd} | conditional | bytes 30655136 | solution.py:381
  2.7 0.0 copy-start.5
  2.7 0.0 copy-start.1
  2.7 0.0 copy-start.3
  2.7 5.1 %collective-permute-start.13 = (bf16[256,1024]{1,0:T(8,128)(2,1)}, bf16[256,1024]{1,0:T(8,128)(2,1)S(1)}, u32[]{:S(2)}, u32[]{:S(2)}) collective-permute-start(bf16[256,1024]{1,0:T(8,128)(2,1)} %get-tuple-element.92.k_ref.own_ref), channel_id=1, source_target_pairs={{0,8},{4,12},{8,16},{12,20},{16,24},{20,28},{1,9},{5,13},{9,17},{1... | collective-permute-start | bytes 1572872 | tf_op jit(solution)/shard_map/cond/branch_1_fun/ppermute | solution.py:281
  7.8 1.7 %prep.3 = (s32[256,128]{1,0:T(8,128)S(1)}, s32[8,128]{1,0:T(8,128)S(1)}, f32[256,1024]{1,0:T(8,128)S(1)}, f32[8,256]{1,0:T(8,128)S(1)}) custom-call(s32[2,9]{1,0:T(2,128)} %bitcast.19, f32[8,256]{1,0:T(8,128)} %bitcast.15), custom_call_target="tpu_custom_call" | custom-call | tf_op jit(solution)/shard_map/cond/branch_1_fun/prep/pallas_call | solution.py:252
  9.6 1.8 %state.3 = (bf16[144,1024]{1,0:T(8,128)(2,1)S(1)}, f32[128,1024]{1,0:T(8,128)S(1)}, f32[8,1024]{1,0:T(8,128)S(1)}) custom-call(s32[8,128]{1,0:T(8,128)S(1)} %get-tuple-element.82.last_ref, f32[256,1024]{1,0:T(8,128)S(1)} %get-tuple-element.83.cum_ref, bf16[256,1024]{1,0:T(8,128)(2,1)} %get-tuple-element.84.k_ref, bf16[256,1024]{1,0:T(8,128)(2,1)} %get-tuple-element.85.v_ref), custom_call_target="tpu_custom_call" | custom-call | tf_op jit(solution)/shard_map/cond/branch_1_fun/state/pallas_call | solution.py:252
  11.3 0.0 copy-done.5
  11.3 3.5 %collective-permute-start.16 = (bf16[256,1024]{1,0:T(8,128)(2,1)S(1)}, bf16[256,1024]{1,0:T(8,128)(2,1)S(1)}, u32[]{:S(2)}, u32[]{:S(2)}) collective-permute-start(bf16[256,1024]{1,0:T(8,128)(2,1)S(1)} %copy-done.5), channel_id=1, source_target_pairs={{0,8},{4,12},{8,16},{12,20},{16,24},{20,28},{1,9},{5,13},{9,17},{1... | collective-permute-start | bytes 1572872 | tf_op jit(solution)/shard_map/cond/branch_1_fun/ppermute | solution.py:281
  14.8 1.6 %collective-permute-start.11 = (bf16[144,1024]{1,0:T(8,128)(2,1)S(1)}, bf16[144,1024]{1,0:T(8,128)(2,1)S(1)}, u32[]{:S(2)}, u32[]{:S(2)}) collective-permute-start(bf16[144,1024]{1,0:T(8,128)(2,1)S(1)} %get-tuple-element.88), channel_id=1, source_target_pairs={{0,4},{4,0},{8,12},{12,8},{16,20},{20,16},{24,28},{28,24},{1,5},{5... | collective-permute-start | bytes 884744 | tf_op jit(solution)/shard_map/cond/branch_1_fun/ppermute | solution.py:286
  16.4 0.0 copy-done.1
  16.4 0.0 copy-done.3
  16.4 0.9 %soft_own.3 = (f32[256,2048]{1,0:T(8,128)S(1)}, f32[256,1024]{1,0:T(8,128)S(1)}) custom-call(s32[256,128]{1,0:T(8,128)S(1)} %get-tuple-element.80.starts_ref, bf16[256,1024]{1,0:T(8,128)(2,1)S(1)} %copy-done.1, bf16[256,1024]{1,0:T(8,128)(2,1)S(1)} %copy-done.3, bf16[256,1024]{1,0:T(8,128)(2,1)S(1)} %copy-done.5), custom_call_target="tpu_custom_call" | custom-call | tf_op jit(solution)/shard_map/cond/branch_1_fun/soft_own/pallas_call | solution.py:252
  17.3 3.1 %collective-permute-done.13.there_ref.k_ref = bf16[256,1024]{1,0:T(8,128)(2,1)S(1)} collective-permute-done((bf16[256,1024]{1,0:T(8,128)(2,1)}, bf16[256,1024]{1,0:T(8,128)(2,1)S(1)}, u32[]{:S(2)}, u32[]{:S(2)}) %collective-permute-start.13) | collective-permute-done | bytes 524320 | tf_op jit(solution)/shard_map/cond/branch_1_fun/ppermute | solution.py:281
  20.5 0.0 copy-start.7
  20.5 0.0 copy-start.9
  20.5 0.0 copy-start.11
  20.5 0.0 copy-start.13
  20.5 0.0 copy-start.15
  20.5 1.6 %collective-permute-start.14 = (bf16[256,1024]{1,0:T(8,128)(2,1)S(1)}, bf16[256,1024]{1,0:T(8,128)(2,1)S(1)}, u32[]{:S(2)}, u32[]{:S(2)}) collective-permute-start(bf16[256,1024]{1,0:T(8,128)(2,1)S(1)} %pick_k.3), channel_id=1, source_target_pairs={{0,4},{4,0},{8,12},{12,8},{16,20},{20,16},{24,28},{28,24},{1,5},{5... | collective-permute-start | bytes 1572872 | tf_op jit(solution)/shard_map/cond/branch_1_fun/ppermute | solution.py:286
  22.1 2.7 %collective-permute-done.11.a_ref.other_ref = bf16[144,1024]{1,0:T(8,128)(2,1)S(1)} collective-permute-done((bf16[144,1024]{1,0:T(8,128)(2,1)S(1)}, bf16[144,1024]{1,0:T(8,128)(2,1)S(1)}, u32[]{:S(2)}, u32[]{:S(2)}) %collective-permute-start.11) | collective-permute-done | bytes 294944 | tf_op jit(solution)/shard_map/cond/branch_1_fun/ppermute | solution.py:286
  24.9 2.9 %collective-permute-start.12 = (bf16[128,1024]{1,0:T(8,128)(2,1)S(1)}, bf16[128,1024]{1,0:T(8,128)(2,1)S(1)}, u32[]{:S(2)}, u32[]{:S(2)}) collective-permute-start(bf16[128,1024]{1,0:T(8,128)(2,1)S(1)} %states.3), channel_id=1, source_target_pairs={{0,8},{8,16},{16,24},{1,9},{9,17},{17,25},{2,10},{10,18},{18,26},{... | collective-permute-start | bytes 786440 | tf_op jit(solution)/shard_map/cond/branch_1_fun/ppermute | solution.py:281
  27.7 3.8 %collective-permute-done.16.there_ref.v_ref = bf16[256,1024]{1,0:T(8,128)(2,1)S(1)} collective-permute-done((bf16[256,1024]{1,0:T(8,128)(2,1)S(1)}, bf16[256,1024]{1,0:T(8,128)(2,1)S(1)}, u32[]{:S(2)}, u32[]{:S(2)}) %collective-permute-start.16) | collective-permute-done | bytes 524320 | tf_op jit(solution)/shard_map/cond/branch_1_fun/ppermute | solution.py:281
  31.6 0.2 pick_v.3
  31.8 0.4 collective-permute-start.17
  32.2 3.8 %collective-permute-done.12.far_ref = bf16[128,1024]{1,0:T(8,128)(2,1)S(1)} collective-permute-done((bf16[128,1024]{1,0:T(8,128)(2,1)S(1)}, bf16[128,1024]{1,0:T(8,128)(2,1)S(1)}, u32[]{:S(2)}, u32[]{:S(2)}) %collective-permute-start.12) | collective-permute-done | bytes 262176 | tf_op jit(solution)/shard_map/cond/branch_1_fun/ppermute | solution.py:281
  36.0 0.0 collective-permute-done.14.k_ref
  36.1 0.2 pair.3
  36.3 4.4 %collective-permute-start.15 = (bf16[256,1024]{1,0:T(8,128)(2,1)S(1)}, bf16[256,1024]{1,0:T(8,128)(2,1)S(1)}, u32[]{:S(2)}, u32[]{:S(2)}) collective-permute-start(bf16[256,1024]{1,0:T(8,128)(2,1)S(1)} %pair.3), channel_id=1, source_target_pairs={{0,8},{4,12},{8,16},{12,20},{16,24},{20,28},{1,9},{5,13},{9,17},{1... | collective-permute-start | bytes 1572872 | tf_op jit(solution)/shard_map/cond/branch_1_fun/ppermute | solution.py:281
  40.7 0.0 copy-done.7
  40.7 0.0 copy-done.9
  40.7 1.0 %inner.3 = (f32[256,1024]{1,0:T(8,128)S(1)}, f32[256,1024]{1,0:T(8,128)S(1)}) custom-call(s32[256,128]{1,0:T(8,128)S(1)} %get-tuple-element.80.starts_ref, bf16[256,1024]{1,0:T(8,128)(2,1)S(1)} %copy-done.11, bf16[256,1024]{1,0:T(8,128)(2,1)S(1)} %copy-done.7, bf16[256,1024]{1,0:T(8,128)(2,1)S(1)} %copy-done.9, bf16[256,1024]{1,0:T(8,128)(2,1)S(1)} %copy-done.13, ...), custom_call_target="tpu_custom_call" | custom-call | tf_op jit(solution)/shard_map/cond/branch_1_fun/inner/pallas_call | solution.py:252
  41.7 1.1 %soft_2.3 = (f32[256,2048]{1,0:T(8,128)S(1)}, f32[256,1024]{1,0:T(8,128)S(1)}) custom-call(s32[256,128]{1,0:T(8,128)S(1)} %get-tuple-element.80.starts_ref, bf16[256,1024]{1,0:T(8,128)(2,1)S(1)} %copy-done.1, bf16[256,1024]{1,0:T(8,128)(2,1)S(1)} %collective-permute-done.13.there_ref.k_ref, bf16[256,1024]{1,0:T(8,128)(2,1)S(1)} %collective-permute-done.16.there_ref.v_ref, ...), custom_call_target="tpu_custom_call" | custom-call | tf_op jit(solution)/shard_map/cond/branch_1_fun/soft_2/pallas_call | solution.py:252
  42.9 2.7 %collective-permute-done.17.v_ref = bf16[256,1024]{1,0:T(8,128)(2,1)S(1)} collective-permute-done((bf16[256,1024]{1,0:T(8,128)(2,1)S(1)}, bf16[256,1024]{1,0:T(8,128)(2,1)S(1)}, u32[]{:S(2)}, u32[]{:S(2)}) %collective-permute-start.17) | collective-permute-done | bytes 524320 | tf_op jit(solution)/shard_map/cond/branch_1_fun/ppermute | solution.py:286
  45.6 3.5 %collective-permute-start.18 = (bf16[128,1024]{1,0:T(8,128)(2,1)S(1)}, bf16[128,1024]{1,0:T(8,128)(2,1)S(1)}, u32[]{:S(2)}, u32[]{:S(2)}) collective-permute-start(bf16[128,1024]{1,0:T(8,128)(2,1)S(1)} %nearest.3), channel_id=1, source_target_pairs={{0,8},{4,12},{8,16},{12,20},{16,24},{20,28},{1,9},{5,13},{9,17},{1... | collective-permute-start | bytes 786440 | tf_op jit(solution)/shard_map/cond/branch_1_fun/ppermute | solution.py:281
  49.0 1.1 %soft_1.3 = (f32[256,2048]{1,0:T(8,128)S(1)}, f32[256,1024]{1,0:T(8,128)S(1)}) custom-call(s32[256,128]{1,0:T(8,128)S(1)} %get-tuple-element.80.starts_ref, bf16[256,1024]{1,0:T(8,128)(2,1)S(1)} %copy-done.1, bf16[256,1024]{1,0:T(8,128)(2,1)S(1)} %collective-permute-done.14.k_ref, bf16[256,1024]{1,0:T(8,128)(2,1)S(1)} %collective-permute-done.17.v_ref, ...), custom_call_target="tpu_custom_call" | custom-call | tf_op jit(solution)/shard_map/cond/branch_1_fun/soft_1/pallas_call | solution.py:252
  50.2 2.8 %collective-permute-done.15.k_ref.two_ref = bf16[256,1024]{1,0:T(8,128)(2,1)S(1)} collective-permute-done((bf16[256,1024]{1,0:T(8,128)(2,1)S(1)}, bf16[256,1024]{1,0:T(8,128)(2,1)S(1)}, u32[]{:S(2)}, u32[]{:S(2)}) %collective-permute-start.15) | collective-permute-done | bytes 524320 | tf_op jit(solution)/shard_map/cond/branch_1_fun/ppermute | solution.py:281
  53.0 0.7 %cross.3 = (f32[256,1024]{1,0:T(8,128)S(1)}, f32[8,256]{1,0:T(8,128)S(1)}) custom-call(s32[256,128]{1,0:T(8,128)S(1)} %get-tuple-element.80.starts_ref, bf16[256,1024]{1,0:T(8,128)(2,1)S(1)} %copy-done.11, f32[256,1024]{1,0:T(8,128)S(1)} %get-tuple-element.83.cum_ref, f32[256,1024]{1,0:T(8,128)S(1)} %get-tuple-element.112.inner_ref, ...), custom_call_target="tpu_custom_call" | custom-call | tf_op jit(solution)/shard_map/cond/branch_1_fun/cross/pallas_call | solution.py:252
  53.7 0.0 collective-permute-start.19
  53.7 1.6 %collective-permute-start.20 = (f32[8,256]{1,0:T(8,128)S(1)}, f32[8,256]{1,0:T(8,128)S(1)}, u32[]{:S(2)}, u32[]{:S(2)}) collective-permute-start(f32[8,256]{1,0:T(8,128)S(1)} %get-tuple-element.115.refs_0_), channel_id=1, source_target_pairs={{0,2},{1,3},{2,0},{3,1},{4,6},{5,7},{6,4},{7,5},{8,10},{9,11},{10,... | collective-permute-start | bytes 24584 | tf_op jit(solution)/shard_map/cond/branch_1_fun/ppermute | solution.py:291
  55.3 1.4 %collective-permute-start.21 = (f32[8,256]{1,0:T(8,128)S(1)}, f32[8,256]{1,0:T(8,128)S(1)}, u32[]{:S(2)}, u32[]{:S(2)}) collective-permute-start(f32[8,256]{1,0:T(8,128)S(1)} %get-tuple-element.115.refs_0_), channel_id=1, source_target_pairs={{0,3},{1,0},{2,1},{3,2},{4,7},{5,4},{6,5},{7,6},{8,11},{9,8},{10,9... | collective-permute-start | bytes 24584 | tf_op jit(solution)/shard_map/cond/branch_1_fun/ppermute | solution.py:291
  56.7 1.0 %soft_weigh.3 = (bf16[256,1024]{1,0:T(8,128)(2,1)S(1)}, f32[256,1024]{1,0:T(8,128)S(1)}, f32[256,1024]{1,0:T(8,128)S(1)}) custom-call(s32[256,128]{1,0:T(8,128)S(1)} %get-tuple-element.80.starts_ref, bf16[256,1024]{1,0:T(8,128)(2,1)S(1)} %copy-done.1, bf16[256,1024]{1,0:T(8,128)(2,1)S(1)} %collective-permute-done.15.k_ref.two_ref, ...), custom_call_target="tpu_custom_call" | custom-call | tf_op jit(solution)/shard_map/cond/branch_1_fun/soft_weigh/pallas_call | solution.py:252
  57.8 0.0 collective-permute-done.18.v_ref
  57.8 0.0 collective-permute-done.19.refs_1_
  57.8 0.0 collective-permute-done.20.refs_2_
  57.8 0.3 collective-permute-done.21.refs_3_
  58.1 1.4 %last.3 = (bf16[256,1024]{1,0:T(8,128)(2,1)}, bf16[256,1024]{1,0:T(8,128)(2,1)}) custom-call(bf16[256,1024]{1,0:T(8,128)(2,1)S(1)} %get-tuple-element.109.p_ref, bf16[128,1024]{1,0:T(8,128)(2,1)S(1)} %collective-permute-done.18.v_ref, f32[256,1024]{1,0:T(8,128)S(1)} %get-tuple-element.110.acc_ref, f32[256,1024]{1,0:T(8,128)S(1)} %get-tuple-element.111.inv_ref, ...), custom_call_target="tpu_custom_call" | custom-call | tf_op jit(solution)/shard_map/cond/branch_1_fun/last/pallas_call | solution.py:252
  (6 shorter events, 0.1 us)
Async XLA Ops:
  2.7 8.6 %copy-start.5 = (bf16[256,1024]{1,0:T(8,128)(2,1)S(1)}, bf16[256,1024]{1,0:T(8,128)(2,1)}, u32[]{:S(2)}) copy-start(bf16[256,1024]{1,0:T(8,128)(2,1)} %get-tuple-element.93.v_ref.own_ref) | copy-start | bytes 1572868 | tf_op jit(solution)/shard_map/cond
  2.7 13.7 %copy-start.1 = (bf16[256,1024]{1,0:T(8,128)(2,1)S(1)}, bf16[256,1024]{1,0:T(8,128)(2,1)}, u32[]{:S(2)}) copy-start(bf16[256,1024]{1,0:T(8,128)(2,1)} %get-tuple-element.81.q_ref) | copy-start | bytes 1572868 | tf_op jit(solution)/shard_map/cond
  2.7 13.7 %copy-start.3 = (bf16[256,1024]{1,0:T(8,128)(2,1)S(1)}, bf16[256,1024]{1,0:T(8,128)(2,1)}, u32[]{:S(2)}) copy-start(bf16[256,1024]{1,0:T(8,128)(2,1)} %get-tuple-element.92.k_ref.own_ref) | copy-start | bytes 1572868 | tf_op jit(solution)/shard_map/cond
  2.7 17.7 %collective-permute-start.13 = (bf16[256,1024]{1,0:T(8,128)(2,1)}, bf16[256,1024]{1,0:T(8,128)(2,1)S(1)}, u32[]{:S(2)}, u32[]{:S(2)}) collective-permute-start(bf16[256,1024]{1,0:T(8,128)(2,1)} %get-tuple-element.92.k_ref.own_ref), channel_id=1, source_target_pairs={{0,8},{4,12},{8,16},{12,20},{16,24},{20,28},{1,9},{5,13},{9,17},{1... | collective-permute-start | bytes 1572872 | tf_op jit(solution)/shard_map/cond/branch_1_fun/ppermute | solution.py:281
  11.3 20.2 %collective-permute-start.16 = (bf16[256,1024]{1,0:T(8,128)(2,1)S(1)}, bf16[256,1024]{1,0:T(8,128)(2,1)S(1)}, u32[]{:S(2)}, u32[]{:S(2)}) collective-permute-start(bf16[256,1024]{1,0:T(8,128)(2,1)S(1)} %copy-done.5), channel_id=1, source_target_pairs={{0,8},{4,12},{8,16},{12,20},{16,24},{20,28},{1,9},{5,13},{9,17},{1... | collective-permute-start | bytes 1572872 | tf_op jit(solution)/shard_map/cond/branch_1_fun/ppermute | solution.py:281
  14.8 10.0 %collective-permute-start.11 = (bf16[144,1024]{1,0:T(8,128)(2,1)S(1)}, bf16[144,1024]{1,0:T(8,128)(2,1)S(1)}, u32[]{:S(2)}, u32[]{:S(2)}) collective-permute-start(bf16[144,1024]{1,0:T(8,128)(2,1)S(1)} %get-tuple-element.88), channel_id=1, source_target_pairs={{0,4},{4,0},{8,12},{12,8},{16,20},{20,16},{24,28},{28,24},{1,5},{5... | collective-permute-start | bytes 884744 | tf_op jit(solution)/shard_map/cond/branch_1_fun/ppermute | solution.py:286
  20.5 20.2 %copy-start.7 = (bf16[256,1024]{1,0:T(8,128)(2,1)S(1)}, bf16[256,1024]{1,0:T(8,128)(2,1)}, u32[]{:S(2)}) copy-start(bf16[256,1024]{1,0:T(8,128)(2,1)} %get-tuple-element.84.k_ref) | copy-start | bytes 1572868 | tf_op jit(solution)/shard_map/cond
  20.5 20.2 %copy-start.9 = (bf16[256,1024]{1,0:T(8,128)(2,1)S(1)}, bf16[256,1024]{1,0:T(8,128)(2,1)}, u32[]{:S(2)}) copy-start(bf16[256,1024]{1,0:T(8,128)(2,1)} %get-tuple-element.85.v_ref) | copy-start | bytes 1572868 | tf_op jit(solution)/shard_map/cond
  20.5 20.2 %copy-start.11 = (bf16[256,1024]{1,0:T(8,128)(2,1)S(1)}, bf16[256,1024]{1,0:T(8,128)(2,1)}, u32[]{:S(2)}) copy-start(bf16[256,1024]{1,0:T(8,128)(2,1)} %get-tuple-element.97.q_ref) | copy-start | bytes 1572868 | tf_op jit(solution)/shard_map/cond
  20.5 20.2 %copy-start.13 = (bf16[256,1024]{1,0:T(8,128)(2,1)S(1)}, bf16[256,1024]{1,0:T(8,128)(2,1)}, u32[]{:S(2)}) copy-start(bf16[256,1024]{1,0:T(8,128)(2,1)} %get-tuple-element.98.gate_ref) | copy-start | bytes 1572868 | tf_op jit(solution)/shard_map/cond
  20.5 20.2 %copy-start.15 = (f32[1024]{0:T(1024)S(1)}, f32[1024]{0:T(1024)}, u32[]{:S(2)}) copy-start(f32[1024]{0:T(1024)} %get-tuple-element.99) | copy-start | bytes 12292 | tf_op jit(solution)/shard_map/cond
  20.5 15.5 %collective-permute-start.14 = (bf16[256,1024]{1,0:T(8,128)(2,1)S(1)}, bf16[256,1024]{1,0:T(8,128)(2,1)S(1)}, u32[]{:S(2)}, u32[]{:S(2)}) collective-permute-start(bf16[256,1024]{1,0:T(8,128)(2,1)S(1)} %pick_k.3), channel_id=1, source_target_pairs={{0,4},{4,0},{8,12},{12,8},{16,20},{20,16},{24,28},{28,24},{1,5},{5... | collective-permute-start | bytes 1572872 | tf_op jit(solution)/shard_map/cond/branch_1_fun/ppermute | solution.py:286
  24.9 11.2 %collective-permute-start.12 = (bf16[128,1024]{1,0:T(8,128)(2,1)S(1)}, bf16[128,1024]{1,0:T(8,128)(2,1)S(1)}, u32[]{:S(2)}, u32[]{:S(2)}) collective-permute-start(bf16[128,1024]{1,0:T(8,128)(2,1)S(1)} %states.3), channel_id=1, source_target_pairs={{0,8},{8,16},{16,24},{1,9},{9,17},{17,25},{2,10},{10,18},{18,26},{... | collective-permute-start | bytes 786440 | tf_op jit(solution)/shard_map/cond/branch_1_fun/ppermute | solution.py:281
  31.8 13.8 %collective-permute-start.17 = (bf16[256,1024]{1,0:T(8,128)(2,1)S(1)}, bf16[256,1024]{1,0:T(8,128)(2,1)S(1)}, u32[]{:S(2)}, u32[]{:S(2)}) collective-permute-start(bf16[256,1024]{1,0:T(8,128)(2,1)S(1)} %pick_v.3), channel_id=1, source_target_pairs={{0,4},{4,0},{8,12},{12,8},{16,20},{20,16},{24,28},{28,24},{1,5},{5... | collective-permute-start | bytes 1572872 | tf_op jit(solution)/shard_map/cond/branch_1_fun/ppermute | solution.py:286
  36.3 16.7 %collective-permute-start.15 = (bf16[256,1024]{1,0:T(8,128)(2,1)S(1)}, bf16[256,1024]{1,0:T(8,128)(2,1)S(1)}, u32[]{:S(2)}, u32[]{:S(2)}) collective-permute-start(bf16[256,1024]{1,0:T(8,128)(2,1)S(1)} %pair.3), channel_id=1, source_target_pairs={{0,8},{4,12},{8,16},{12,20},{16,24},{20,28},{1,9},{5,13},{9,17},{1... | collective-permute-start | bytes 1572872 | tf_op jit(solution)/shard_map/cond/branch_1_fun/ppermute | solution.py:281
  45.6 12.2 %collective-permute-start.18 = (bf16[128,1024]{1,0:T(8,128)(2,1)S(1)}, bf16[128,1024]{1,0:T(8,128)(2,1)S(1)}, u32[]{:S(2)}, u32[]{:S(2)}) collective-permute-start(bf16[128,1024]{1,0:T(8,128)(2,1)S(1)} %nearest.3), channel_id=1, source_target_pairs={{0,8},{4,12},{8,16},{12,20},{16,24},{20,28},{1,9},{5,13},{9,17},{1... | collective-permute-start | bytes 786440 | tf_op jit(solution)/shard_map/cond/branch_1_fun/ppermute | solution.py:281
  53.7 4.1 %collective-permute-start.19 = (f32[8,256]{1,0:T(8,128)S(1)}, f32[8,256]{1,0:T(8,128)S(1)}, u32[]{:S(2)}, u32[]{:S(2)}) collective-permute-start(f32[8,256]{1,0:T(8,128)S(1)} %get-tuple-element.115.refs_0_), channel_id=1, source_target_pairs={{0,1},{1,2},{2,3},{3,0},{4,5},{5,6},{6,7},{7,4},{8,9},{9,10},{10,1... | collective-permute-start | bytes 24584 | tf_op jit(solution)/shard_map/cond/branch_1_fun/ppermute | solution.py:291
  53.7 4.1 %collective-permute-start.20 = (f32[8,256]{1,0:T(8,128)S(1)}, f32[8,256]{1,0:T(8,128)S(1)}, u32[]{:S(2)}, u32[]{:S(2)}) collective-permute-start(f32[8,256]{1,0:T(8,128)S(1)} %get-tuple-element.115.refs_0_), channel_id=1, source_target_pairs={{0,2},{1,3},{2,0},{3,1},{4,6},{5,7},{6,4},{7,5},{8,10},{9,11},{10,... | collective-permute-start | bytes 24584 | tf_op jit(solution)/shard_map/cond/branch_1_fun/ppermute | solution.py:291
  55.3 2.8 %collective-permute-start.21 = (f32[8,256]{1,0:T(8,128)S(1)}, f32[8,256]{1,0:T(8,128)S(1)}, u32[]{:S(2)}, u32[]{:S(2)}) collective-permute-start(f32[8,256]{1,0:T(8,128)S(1)} %get-tuple-element.115.refs_0_), channel_id=1, source_target_pairs={{0,3},{1,0},{2,1},{3,2},{4,7},{5,4},{6,5},{7,6},{8,11},{9,8},{10,9... | collective-permute-start | bytes 24584 | tf_op jit(solution)/shard_map/cond/branch_1_fun/ppermute | solution.py:291

commit v6 on v5

--- a/solution.py
+++ b/solution.py
@@ -230,17 +230,21 @@
         inv_ref[:, cols] = inv
 
 
-def last_kernel(p_ref, v_ref, acc_ref, inv_ref, mixture_ref, scale_ref, *refs):
-    *parts, lin_ref, soft_ref = refs
+def soft_last_kernel(p_ref, v_ref, acc_ref, inv_ref, soft_ref):
     keys = v_ref.shape[0]
-    total = jnp.transpose(sum(part[...] for part in parts))[:, 0:1]
-    norm = jnp.broadcast_to(
-        lax.rsqrt(total / (HALF_MODEL_HEADS * HD) + 1e-06), (acc_ref.shape[0], HD)
-    )
     for h in range(acc_ref.shape[1] // HD):
         cols = slice(h * HD, (h + 1) * HD)
         more = dot(p_ref[:, h * keys : (h + 1) * keys], v_ref[:, cols], ((1,), (0,)))
         soft_ref[:, cols] = (acc_ref[:, cols] + more * inv_ref[:, cols]).astype(BF16)
+
+
+def norm_kernel(mixture_ref, scale_ref, *refs):
+    *parts, lin_ref = refs
+    rows, width = lin_ref.shape
+    total = jnp.transpose(sum(part[...] for part in parts))[:, 0:1]
+    norm = jnp.broadcast_to(lax.rsqrt(total / (HALF_MODEL_HEADS * HD) + 1e-06), (rows, HD))
+    for h in range(width // HD):
+        cols = slice(h * HD, (h + 1) * HD)
         lin_ref[:, cols] = (mixture_ref[:, cols] * norm * scale_ref[:, cols]).astype(BF16)
 
 
@@ -287,8 +291,11 @@
 
     def everywhere(array):
         count = lax.axis_size("head")
+        paired = count & (count - 1) == 0
         return [array] + [
-            lax.ppermute(array, "head", [(i, (i + by) % count) for i in range(count)])
+            lax.ppermute(
+                array, "head", [(i, i ^ by if paired else (i + by) % count) for i in range(count)]
+            )
             for by in range(1, count)
         ]
 
@@ -356,9 +363,9 @@
         ),
         starts, soft_query, two, *soft,
     )
-    return call(
-        last_kernel, "last", (half, half), weights, v3, acc, inv, mixture, scale, *parts
-    )
+    soft_out = call(soft_last_kernel, "soft_last", half, weights, v3, acc, inv)
+    lin_out = call(norm_kernel, "norm", half, mixture, scale, *parts)
+    return (lin_out, soft_out)
 
 
 def shards(

time: 60.1 us -> 59.8 us (level)
  starting transfers between devices: 25.9 us -> 24.9 us
    ppermute x3, starting transfers between devices: 3.02 us -> 1.89 us  [everywhere(): lax.ppermute(array, 'head', [(i, i ^ by if paired else (i + by) % count)...]
    pallas_call x14 -> x15, Pallas kernels: 11.3 us -> 11.9 us  [call(): pl.pallas_call(kernel, name=name, out_shape=out_shape, in_specs=[SMEM] *...]
  transfers between devices with their start and end apart: 11 -> 11, of which waited for: 7 -> 7; matrix products, arithmetic and copies ran while one was open for 0% -> 0% of each run, Pallas kernels for 17% -> 18%
where the time goes in v6:
time: 59.8 us; the launch traced here: 59.5 us
  starting transfers between devices  24.9 us (42%)
  waiting for transfers between devices  19.6 us (33%)
  Pallas kernels  11.9 us (20%)
  other arithmetic  1.4 us (2%)
  between operations  1.28 us (2%)
    ppermute x5, starting transfers between devices, ahead(): lax.ppermute(array, 'seq', [(i, i + by) for i in range(0, devices - by, s...  19.3 us
    ppermute x5, waiting for transfers between devices, ahead(): lax.ppermute(array, 'seq', [(i, i + by) for i in range(0, devices - by, s...  13.6 us
    pallas_call x15, Pallas kernels, call(): pl.pallas_call(kernel, name=name, out_shape=out_shape, in_specs=[SMEM] *...  11.9 us
    ppermute x3, waiting for transfers between devices, swap(): return lax.ppermute(array, 'seq', [(i, i ^ 1) for i in range(devices)])  5.47 us
    ppermute x3, starting transfers between devices, swap(): return lax.ppermute(array, 'seq', [(i, i ^ 1) for i in range(devices)])  3.71 us
    ppermute x3, starting transfers between devices, everywhere(): lax.ppermute(array, 'head', [(i, i ^ by if paired else (i + by) % count)...  1.89 us
    reduce_max x1, other arithmetic, shards(): farthest = jnp.max(lasts - lax.rem(lasts, jnp.int32(rows)) - firsts)  1.4 us
  transfers between devices with their start and end apart: 11, of which 7 were waited for; matrix products, arithmetic and copies ran while one was open for 0% of the time, Pallas kernels for 18%

profile of v6, /device:TPU:0, one launch (start us, length us, event | category | flops | bytes accessed | tf_op | source)
XLA Modules:
  0.0 59.5 jit_solution(10723341417753735769)
XLA Ops:
  0.6 1.4 %fusion.3 = s32[]{:T(128)} fusion(s32[9,2]{0,1:T(2,128)} %param.22), kind=kLoop, calls=%fused_computation.5 | loop fusion | flops 89 | bytes 76 | tf_op jit(solution)/shard_map/reduce_max | solution.py:387
  2.7 56.8 %conditional.1 = (bf16[256,1024]{1,0:T(8,128)(2,1)}, bf16[256,1024]{1,0:T(8,128)(2,1)}) conditional(s32[]{:T(128)} %convert_element_type.3, (s32[9,2]{0,1:T(2,128)}, f32[256,8]{0,1:T(8,128)}, bf16[256,1024]{1,0:T(8,128)(2,1)}, bf16[256,1024]{1,0:T(8,128)(2,1)}, bf16[256,1024]{1,0:T(8,128)(2,1)}, /*index=5*/bf16[256,1024]{1,0:T(8,128)(2,1)}, ...), branch_computations={%region_1.0_spmd, %region_2.0_spmd} | conditional | bytes 30655144 | solution.py:388
  2.7 0.0 copy-start.3
  2.7 0.0 copy-start.1
  2.7 0.0 copy-start.5
  2.7 5.1 %collective-permute-start.13 = (bf16[256,1024]{1,0:T(8,128)(2,1)}, bf16[256,1024]{1,0:T(8,128)(2,1)S(1)}, u32[]{:S(2)}, u32[]{:S(2)}) collective-permute-start(bf16[256,1024]{1,0:T(8,128)(2,1)} %get-tuple-element.102.k_ref.own_ref), channel_id=1, source_target_pairs={{0,8},{4,12},{8,16},{12,20},{16,24},{20,28},{1,9},{5,13},{9,17},{1... | collective-permute-start | bytes 1572872 | tf_op jit(solution)/shard_map/cond/branch_1_fun/ppermute | solution.py:285
  7.8 1.7 %prep.3 = (s32[256,128]{1,0:T(8,128)S(1)}, s32[8,128]{1,0:T(8,128)S(1)}, f32[256,1024]{1,0:T(8,128)S(1)}, f32[8,256]{1,0:T(8,128)S(1)}) custom-call(s32[2,9]{1,0:T(2,128)} %bitcast.19, f32[8,256]{1,0:T(8,128)} %bitcast.15), custom_call_target="tpu_custom_call" | custom-call | tf_op jit(solution)/shard_map/cond/branch_1_fun/prep/pallas_call | solution.py:256
  9.6 1.8 %state.3 = (bf16[144,1024]{1,0:T(8,128)(2,1)S(1)}, f32[128,1024]{1,0:T(8,128)S(1)}, f32[8,1024]{1,0:T(8,128)S(1)}) custom-call(s32[8,128]{1,0:T(8,128)S(1)} %get-tuple-element.84.last_ref, f32[256,1024]{1,0:T(8,128)S(1)} %get-tuple-element.82.cum_ref, bf16[256,1024]{1,0:T(8,128)(2,1)} %get-tuple-element.85.k_ref, bf16[256,1024]{1,0:T(8,128)(2,1)} %get-tuple-element.86.v_ref), custom_call_target="tpu_custom_call" | custom-call | tf_op jit(solution)/shard_map/cond/branch_1_fun/state/pallas_call | solution.py:256
  11.3 0.0 copy-done.3
  11.3 3.5 %collective-permute-start.11 = (bf16[256,1024]{1,0:T(8,128)(2,1)S(1)}, bf16[256,1024]{1,0:T(8,128)(2,1)S(1)}, u32[]{:S(2)}, u32[]{:S(2)}) collective-permute-start(bf16[256,1024]{1,0:T(8,128)(2,1)S(1)} %copy-done.3), channel_id=1, source_target_pairs={{0,8},{4,12},{8,16},{12,20},{16,24},{20,28},{1,9},{5,13},{9,17},{1... | collective-permute-start | bytes 1572872 | tf_op jit(solution)/shard_map/cond/branch_1_fun/ppermute | solution.py:285
  14.8 1.6 %collective-permute-start.14 = (bf16[144,1024]{1,0:T(8,128)(2,1)S(1)}, bf16[144,1024]{1,0:T(8,128)(2,1)S(1)}, u32[]{:S(2)}, u32[]{:S(2)}) collective-permute-start(bf16[144,1024]{1,0:T(8,128)(2,1)S(1)} %get-tuple-element.87), channel_id=1, source_target_pairs={{0,4},{4,0},{8,12},{12,8},{16,20},{20,16},{24,28},{28,24},{1,5},{5... | collective-permute-start | bytes 884744 | tf_op jit(solution)/shard_map/cond/branch_1_fun/ppermute | solution.py:290
  16.4 0.0 copy-done.1
  16.4 0.0 copy-done.5
  16.4 0.9 %soft_own.3 = (f32[256,2048]{1,0:T(8,128)S(1)}, f32[256,1024]{1,0:T(8,128)S(1)}) custom-call(s32[256,128]{1,0:T(8,128)S(1)} %get-tuple-element.80.starts_ref, bf16[256,1024]{1,0:T(8,128)(2,1)S(1)} %copy-done.1, bf16[256,1024]{1,0:T(8,128)(2,1)S(1)} %copy-done.5, bf16[256,1024]{1,0:T(8,128)(2,1)S(1)} %copy-done.3), custom_call_target="tpu_custom_call" | custom-call | tf_op jit(solution)/shard_map/cond/branch_1_fun/soft_own/pallas_call | solution.py:256
  17.3 3.1 %collective-permute-done.13.k_ref.there_ref = bf16[256,1024]{1,0:T(8,128)(2,1)S(1)} collective-permute-done((bf16[256,1024]{1,0:T(8,128)(2,1)}, bf16[256,1024]{1,0:T(8,128)(2,1)S(1)}, u32[]{:S(2)}, u32[]{:S(2)}) %collective-permute-start.13) | collective-permute-done | bytes 524320 | tf_op jit(solution)/shard_map/cond/branch_1_fun/ppermute | solution.py:285
  20.5 0.0 copy-start.7
  20.5 0.0 copy-start.9
  20.5 0.0 copy-start.11
  20.5 0.0 copy-start.13
  20.5 0.0 copy-start.15
  20.5 1.6 %collective-permute-start.16 = (bf16[256,1024]{1,0:T(8,128)(2,1)S(1)}, bf16[256,1024]{1,0:T(8,128)(2,1)S(1)}, u32[]{:S(2)}, u32[]{:S(2)}) collective-permute-start(bf16[256,1024]{1,0:T(8,128)(2,1)S(1)} %pick_k.3), channel_id=1, source_target_pairs={{0,4},{4,0},{8,12},{12,8},{16,20},{20,16},{24,28},{28,24},{1,5},{5... | collective-permute-start | bytes 1572872 | tf_op jit(solution)/shard_map/cond/branch_1_fun/ppermute | solution.py:290
  22.1 2.7 %collective-permute-done.14.a_ref.other_ref = bf16[144,1024]{1,0:T(8,128)(2,1)S(1)} collective-permute-done((bf16[144,1024]{1,0:T(8,128)(2,1)S(1)}, bf16[144,1024]{1,0:T(8,128)(2,1)S(1)}, u32[]{:S(2)}, u32[]{:S(2)}) %collective-permute-start.14) | collective-permute-done | bytes 294944 | tf_op jit(solution)/shard_map/cond/branch_1_fun/ppermute | solution.py:290
  24.9 2.9 %collective-permute-start.15 = (bf16[128,1024]{1,0:T(8,128)(2,1)S(1)}, bf16[128,1024]{1,0:T(8,128)(2,1)S(1)}, u32[]{:S(2)}, u32[]{:S(2)}) collective-permute-start(bf16[128,1024]{1,0:T(8,128)(2,1)S(1)} %states.3), channel_id=1, source_target_pairs={{0,8},{8,16},{16,24},{1,9},{9,17},{17,25},{2,10},{10,18},{18,26},{... | collective-permute-start | bytes 786440 | tf_op jit(solution)/shard_map/cond/branch_1_fun/ppermute | solution.py:285
  27.7 3.8 %collective-permute-done.11.there_ref.v_ref = bf16[256,1024]{1,0:T(8,128)(2,1)S(1)} collective-permute-done((bf16[256,1024]{1,0:T(8,128)(2,1)S(1)}, bf16[256,1024]{1,0:T(8,128)(2,1)S(1)}, u32[]{:S(2)}, u32[]{:S(2)}) %collective-permute-start.11) | collective-permute-done | bytes 524320 | tf_op jit(solution)/shard_map/cond/branch_1_fun/ppermute | solution.py:285
  31.6 0.6 collective-permute-start.12
  32.2 3.8 %collective-permute-done.15.far_ref = bf16[128,1024]{1,0:T(8,128)(2,1)S(1)} collective-permute-done((bf16[128,1024]{1,0:T(8,128)(2,1)S(1)}, bf16[128,1024]{1,0:T(8,128)(2,1)S(1)}, u32[]{:S(2)}, u32[]{:S(2)}) %collective-permute-start.15) | collective-permute-done | bytes 262176 | tf_op jit(solution)/shard_map/cond/branch_1_fun/ppermute | solution.py:285
  36.0 0.0 collective-permute-done.16.k_ref
  36.1 0.2 pair.3
  36.3 4.4 %collective-permute-start.17 = (bf16[256,1024]{1,0:T(8,128)(2,1)S(1)}, bf16[256,1024]{1,0:T(8,128)(2,1)S(1)}, u32[]{:S(2)}, u32[]{:S(2)}) collective-permute-start(bf16[256,1024]{1,0:T(8,128)(2,1)S(1)} %pair.3), channel_id=1, source_target_pairs={{0,8},{4,12},{8,16},{12,20},{16,24},{20,28},{1,9},{5,13},{9,17},{1... | collective-permute-start | bytes 1572872 | tf_op jit(solution)/shard_map/cond/branch_1_fun/ppermute | solution.py:285
  40.7 0.0 copy-done.7
  40.7 0.0 copy-done.9
  40.7 1.0 %inner.3 = (f32[256,1024]{1,0:T(8,128)S(1)}, f32[256,1024]{1,0:T(8,128)S(1)}) custom-call(s32[256,128]{1,0:T(8,128)S(1)} %get-tuple-element.80.starts_ref, bf16[256,1024]{1,0:T(8,128)(2,1)S(1)} %copy-done.11, bf16[256,1024]{1,0:T(8,128)(2,1)S(1)} %copy-done.7, bf16[256,1024]{1,0:T(8,128)(2,1)S(1)} %copy-done.9, bf16[256,1024]{1,0:T(8,128)(2,1)S(1)} %copy-done.13, ...), custom_call_target="tpu_custom_call" | custom-call | tf_op jit(solution)/shard_map/cond/branch_1_fun/inner/pallas_call | solution.py:256
  41.7 1.1 %soft_2.3 = (f32[256,2048]{1,0:T(8,128)S(1)}, f32[256,1024]{1,0:T(8,128)S(1)}) custom-call(s32[256,128]{1,0:T(8,128)S(1)} %get-tuple-element.80.starts_ref, bf16[256,1024]{1,0:T(8,128)(2,1)S(1)} %copy-done.1, bf16[256,1024]{1,0:T(8,128)(2,1)S(1)} %collective-permute-done.13.k_ref.there_ref, bf16[256,1024]{1,0:T(8,128)(2,1)S(1)} %collective-permute-done.11.there_ref.v_ref, ...), custom_call_target="tpu_custom_call" | custom-call | tf_op jit(solution)/shard_map/cond/branch_1_fun/soft_2/pallas_call | solution.py:256
  42.9 2.7 %collective-permute-done.12.v_ref = bf16[256,1024]{1,0:T(8,128)(2,1)S(1)} collective-permute-done((bf16[256,1024]{1,0:T(8,128)(2,1)S(1)}, bf16[256,1024]{1,0:T(8,128)(2,1)S(1)}, u32[]{:S(2)}, u32[]{:S(2)}) %collective-permute-start.12) | collective-permute-done | bytes 524320 | tf_op jit(solution)/shard_map/cond/branch_1_fun/ppermute | solution.py:290
  45.6 3.5 %collective-permute-start.21 = (bf16[128,1024]{1,0:T(8,128)(2,1)S(1)}, bf16[128,1024]{1,0:T(8,128)(2,1)S(1)}, u32[]{:S(2)}, u32[]{:S(2)}) collective-permute-start(bf16[128,1024]{1,0:T(8,128)(2,1)S(1)} %nearest.3), channel_id=1, source_target_pairs={{0,8},{4,12},{8,16},{12,20},{16,24},{20,28},{1,9},{5,13},{9,17},{1... | collective-permute-start | bytes 786440 | tf_op jit(solution)/shard_map/cond/branch_1_fun/ppermute | solution.py:285
  49.0 1.1 %soft_1.3 = (f32[256,2048]{1,0:T(8,128)S(1)}, f32[256,1024]{1,0:T(8,128)S(1)}) custom-call(s32[256,128]{1,0:T(8,128)S(1)} %get-tuple-element.80.starts_ref, bf16[256,1024]{1,0:T(8,128)(2,1)S(1)} %copy-done.1, bf16[256,1024]{1,0:T(8,128)(2,1)S(1)} %collective-permute-done.16.k_ref, bf16[256,1024]{1,0:T(8,128)(2,1)S(1)} %collective-permute-done.12.v_ref, ...), custom_call_target="tpu_custom_call" | custom-call | tf_op jit(solution)/shard_map/cond/branch_1_fun/soft_1/pallas_call | solution.py:256
  50.2 2.8 %collective-permute-done.17.two_ref.k_ref = bf16[256,1024]{1,0:T(8,128)(2,1)S(1)} collective-permute-done((bf16[256,1024]{1,0:T(8,128)(2,1)S(1)}, bf16[256,1024]{1,0:T(8,128)(2,1)S(1)}, u32[]{:S(2)}, u32[]{:S(2)}) %collective-permute-start.17) | collective-permute-done | bytes 524320 | tf_op jit(solution)/shard_map/cond/branch_1_fun/ppermute | solution.py:285
  53.0 0.7 %cross.3 = (f32[256,1024]{1,0:T(8,128)S(1)}, f32[8,256]{1,0:T(8,128)S(1)}) custom-call(s32[256,128]{1,0:T(8,128)S(1)} %get-tuple-element.80.starts_ref, bf16[256,1024]{1,0:T(8,128)(2,1)S(1)} %copy-done.11, f32[256,1024]{1,0:T(8,128)S(1)} %get-tuple-element.82.cum_ref, f32[256,1024]{1,0:T(8,128)S(1)} %get-tuple-element.99.inner_ref, ...), custom_call_target="tpu_custom_call" | custom-call | tf_op jit(solution)/shard_map/cond/branch_1_fun/cross/pallas_call | solution.py:256
  53.7 0.0 collective-permute-start.18
  53.7 1.6 %collective-permute-start.19 = (f32[8,256]{1,0:T(8,128)S(1)}, f32[8,256]{1,0:T(8,128)S(1)}, u32[]{:S(2)}, u32[]{:S(2)}) collective-permute-start(f32[8,256]{1,0:T(8,128)S(1)} %get-tuple-element.110.refs_0_), channel_id=1, source_target_pairs={{0,2},{1,3},{2,0},{3,1},{4,6},{5,7},{6,4},{7,5},{8,10},{9,11},{10,... | collective-permute-start | bytes 24584 | tf_op jit(solution)/shard_map/cond/branch_1_fun/ppermute | solution.py:296
  55.3 0.3 collective-permute-start.20
  55.6 1.0 %soft_weigh.3 = (bf16[256,1024]{1,0:T(8,128)(2,1)S(1)}, f32[256,1024]{1,0:T(8,128)S(1)}, f32[256,1024]{1,0:T(8,128)S(1)}) custom-call(s32[256,128]{1,0:T(8,128)S(1)} %get-tuple-element.80.starts_ref, bf16[256,1024]{1,0:T(8,128)(2,1)S(1)} %copy-done.1, bf16[256,1024]{1,0:T(8,128)(2,1)S(1)} %collective-permute-done.17.two_ref.k_ref, ...), custom_call_target="tpu_custom_call" | custom-call | tf_op jit(solution)/shard_map/cond/branch_1_fun/soft_weigh/pallas_call | solution.py:256
  56.7 0.0 collective-permute-done.21.v_ref
  56.7 1.1 %soft_last.3 = bf16[256,1024]{1,0:T(8,128)(2,1)} custom-call(bf16[256,1024]{1,0:T(8,128)(2,1)S(1)} %get-tuple-element.113.p_ref, bf16[128,1024]{1,0:T(8,128)(2,1)S(1)} %collective-permute-done.21.v_ref, f32[256,1024]{1,0:T(8,128)S(1)} %get-tuple-element.114.acc_ref, f32[256,1024]{1,0:T(8,128)S(1)} %get-tuple-element.115.inv_ref), custom_call_target="tpu_custom_call" | custom-call | tf_op jit(solution)/shard_map/cond/branch_1_fun/soft_last/pallas_call | solution.py:256
  57.8 0.0 collective-permute-done.18.refs_1_
  57.8 0.0 collective-permute-done.19.refs_2_
  57.8 0.6 collective-permute-done.20.refs_3_
  58.4 1.1 %norm.3 = bf16[256,1024]{1,0:T(8,128)(2,1)} custom-call(f32[256,1024]{1,0:T(8,128)S(1)} %get-tuple-element.108.mixture_ref, f32[256,1024]{1,0:T(8,128)S(1)} %get-tuple-element.109.scale_ref, f32[8,256]{1,0:T(8,128)S(1)} %get-tuple-element.110.refs_0_, f32[8,256]{1,0:T(8,128)S(1)} %collective-permute-done.18.refs_1_, ...), custom_call_target="tpu_custom_call" | custom-call | tf_op jit(solution)/shard_map/cond/branch_1_fun/norm/pallas_call | solution.py:256
  (7 shorter events, 0.1 us)
Async XLA Ops:
  2.7 8.6 %copy-start.3 = (bf16[256,1024]{1,0:T(8,128)(2,1)S(1)}, bf16[256,1024]{1,0:T(8,128)(2,1)}, u32[]{:S(2)}) copy-start(bf16[256,1024]{1,0:T(8,128)(2,1)} %get-tuple-element.88.own_ref.v_ref) | copy-start | bytes 1572868 | tf_op jit(solution)/shard_map/cond
  2.7 13.7 %copy-start.1 = (bf16[256,1024]{1,0:T(8,128)(2,1)S(1)}, bf16[256,1024]{1,0:T(8,128)(2,1)}, u32[]{:S(2)}) copy-start(bf16[256,1024]{1,0:T(8,128)(2,1)} %get-tuple-element.89.q_ref) | copy-start | bytes 1572868 | tf_op jit(solution)/shard_map/cond
  2.7 13.7 %copy-start.5 = (bf16[256,1024]{1,0:T(8,128)(2,1)S(1)}, bf16[256,1024]{1,0:T(8,128)(2,1)}, u32[]{:S(2)}) copy-start(bf16[256,1024]{1,0:T(8,128)(2,1)} %get-tuple-element.102.k_ref.own_ref) | copy-start | bytes 1572868 | tf_op jit(solution)/shard_map/cond
  2.7 17.7 %collective-permute-start.13 = (bf16[256,1024]{1,0:T(8,128)(2,1)}, bf16[256,1024]{1,0:T(8,128)(2,1)S(1)}, u32[]{:S(2)}, u32[]{:S(2)}) collective-permute-start(bf16[256,1024]{1,0:T(8,128)(2,1)} %get-tuple-element.102.k_ref.own_ref), channel_id=1, source_target_pairs={{0,8},{4,12},{8,16},{12,20},{16,24},{20,28},{1,9},{5,13},{9,17},{1... | collective-permute-start | bytes 1572872 | tf_op jit(solution)/shard_map/cond/branch_1_fun/ppermute | solution.py:285
  11.3 20.2 %collective-permute-start.11 = (bf16[256,1024]{1,0:T(8,128)(2,1)S(1)}, bf16[256,1024]{1,0:T(8,128)(2,1)S(1)}, u32[]{:S(2)}, u32[]{:S(2)}) collective-permute-start(bf16[256,1024]{1,0:T(8,128)(2,1)S(1)} %copy-done.3), channel_id=1, source_target_pairs={{0,8},{4,12},{8,16},{12,20},{16,24},{20,28},{1,9},{5,13},{9,17},{1... | collective-permute-start | bytes 1572872 | tf_op jit(solution)/shard_map/cond/branch_1_fun/ppermute | solution.py:285
  14.8 10.0 %collective-permute-start.14 = (bf16[144,1024]{1,0:T(8,128)(2,1)S(1)}, bf16[144,1024]{1,0:T(8,128)(2,1)S(1)}, u32[]{:S(2)}, u32[]{:S(2)}) collective-permute-start(bf16[144,1024]{1,0:T(8,128)(2,1)S(1)} %get-tuple-element.87), channel_id=1, source_target_pairs={{0,4},{4,0},{8,12},{12,8},{16,20},{20,16},{24,28},{28,24},{1,5},{5... | collective-permute-start | bytes 884744 | tf_op jit(solution)/shard_map/cond/branch_1_fun/ppermute | solution.py:290
  20.5 20.2 %copy-start.7 = (bf16[256,1024]{1,0:T(8,128)(2,1)S(1)}, bf16[256,1024]{1,0:T(8,128)(2,1)}, u32[]{:S(2)}) copy-start(bf16[256,1024]{1,0:T(8,128)(2,1)} %get-tuple-element.85.k_ref) | copy-start | bytes 1572868 | tf_op jit(solution)/shard_map/cond
  20.5 20.2 %copy-start.9 = (bf16[256,1024]{1,0:T(8,128)(2,1)S(1)}, bf16[256,1024]{1,0:T(8,128)(2,1)}, u32[]{:S(2)}) copy-start(bf16[256,1024]{1,0:T(8,128)(2,1)} %get-tuple-element.86.v_ref) | copy-start | bytes 1572868 | tf_op jit(solution)/shard_map/cond
  20.5 20.2 %copy-start.11 = (bf16[256,1024]{1,0:T(8,128)(2,1)S(1)}, bf16[256,1024]{1,0:T(8,128)(2,1)}, u32[]{:S(2)}) copy-start(bf16[256,1024]{1,0:T(8,128)(2,1)} %get-tuple-element.81.q_ref) | copy-start | bytes 1572868 | tf_op jit(solution)/shard_map/cond
  20.5 20.2 %copy-start.13 = (bf16[256,1024]{1,0:T(8,128)(2,1)S(1)}, bf16[256,1024]{1,0:T(8,128)(2,1)}, u32[]{:S(2)}) copy-start(bf16[256,1024]{1,0:T(8,128)(2,1)} %get-tuple-element.95.gate_ref) | copy-start | bytes 1572868 | tf_op jit(solution)/shard_map/cond
  20.5 20.2 %copy-start.15 = (f32[1024]{0:T(1024)S(1)}, f32[1024]{0:T(1024)}, u32[]{:S(2)}) copy-start(f32[1024]{0:T(1024)} %get-tuple-element.96) | copy-start | bytes 12292 | tf_op jit(solution)/shard_map/cond
  20.5 15.5 %collective-permute-start.16 = (bf16[256,1024]{1,0:T(8,128)(2,1)S(1)}, bf16[256,1024]{1,0:T(8,128)(2,1)S(1)}, u32[]{:S(2)}, u32[]{:S(2)}) collective-permute-start(bf16[256,1024]{1,0:T(8,128)(2,1)S(1)} %pick_k.3), channel_id=1, source_target_pairs={{0,4},{4,0},{8,12},{12,8},{16,20},{20,16},{24,28},{28,24},{1,5},{5... | collective-permute-start | bytes 1572872 | tf_op jit(solution)/shard_map/cond/branch_1_fun/ppermute | solution.py:290
  24.9 11.2 %collective-permute-start.15 = (bf16[128,1024]{1,0:T(8,128)(2,1)S(1)}, bf16[128,1024]{1,0:T(8,128)(2,1)S(1)}, u32[]{:S(2)}, u32[]{:S(2)}) collective-permute-start(bf16[128,1024]{1,0:T(8,128)(2,1)S(1)} %states.3), channel_id=1, source_target_pairs={{0,8},{8,16},{16,24},{1,9},{9,17},{17,25},{2,10},{10,18},{18,26},{... | collective-permute-start | bytes 786440 | tf_op jit(solution)/shard_map/cond/branch_1_fun/ppermute | solution.py:285
  31.6 14.0 %collective-permute-start.12 = (bf16[256,1024]{1,0:T(8,128)(2,1)S(1)}, bf16[256,1024]{1,0:T(8,128)(2,1)S(1)}, u32[]{:S(2)}, u32[]{:S(2)}) collective-permute-start(bf16[256,1024]{1,0:T(8,128)(2,1)S(1)} %pick_v.3), channel_id=1, source_target_pairs={{0,4},{4,0},{8,12},{12,8},{16,20},{20,16},{24,28},{28,24},{1,5},{5... | collective-permute-start | bytes 1572872 | tf_op jit(solution)/shard_map/cond/branch_1_fun/ppermute | solution.py:290
  36.3 16.7 %collective-permute-start.17 = (bf16[256,1024]{1,0:T(8,128)(2,1)S(1)}, bf16[256,1024]{1,0:T(8,128)(2,1)S(1)}, u32[]{:S(2)}, u32[]{:S(2)}) collective-permute-start(bf16[256,1024]{1,0:T(8,128)(2,1)S(1)} %pair.3), channel_id=1, source_target_pairs={{0,8},{4,12},{8,16},{12,20},{16,24},{20,28},{1,9},{5,13},{9,17},{1... | collective-permute-start | bytes 1572872 | tf_op jit(solution)/shard_map/cond/branch_1_fun/ppermute | solution.py:285
  45.6 11.1 %collective-permute-start.21 = (bf16[128,1024]{1,0:T(8,128)(2,1)S(1)}, bf16[128,1024]{1,0:T(8,128)(2,1)S(1)}, u32[]{:S(2)}, u32[]{:S(2)}) collective-permute-start(bf16[128,1024]{1,0:T(8,128)(2,1)S(1)} %nearest.3), channel_id=1, source_target_pairs={{0,8},{4,12},{8,16},{12,20},{16,24},{20,28},{1,9},{5,13},{9,17},{1... | collective-permute-start | bytes 786440 | tf_op jit(solution)/shard_map/cond/branch_1_fun/ppermute | solution.py:285
  53.7 4.1 %collective-permute-start.18 = (f32[8,256]{1,0:T(8,128)S(1)}, f32[8,256]{1,0:T(8,128)S(1)}, u32[]{:S(2)}, u32[]{:S(2)}) collective-permute-start(f32[8,256]{1,0:T(8,128)S(1)} %get-tuple-element.110.refs_0_), channel_id=1, source_target_pairs={{0,1},{1,0},{2,3},{3,2},{4,5},{5,4},{6,7},{7,6},{8,9},{9,8},{10,11... | collective-permute-start | bytes 24584 | tf_op jit(solution)/shard_map/cond/branch_1_fun/ppermute | solution.py:296
  53.7 4.1 %collective-permute-start.19 = (f32[8,256]{1,0:T(8,128)S(1)}, f32[8,256]{1,0:T(8,128)S(1)}, u32[]{:S(2)}, u32[]{:S(2)}) collective-permute-start(f32[8,256]{1,0:T(8,128)S(1)} %get-tuple-element.110.refs_0_), channel_id=1, source_target_pairs={{0,2},{1,3},{2,0},{3,1},{4,6},{5,7},{6,4},{7,5},{8,10},{9,11},{10,... | collective-permute-start | bytes 24584 | tf_op jit(solution)/shard_map/cond/branch_1_fun/ppermute | solution.py:296
  55.3 3.1 %collective-permute-start.20 = (f32[8,256]{1,0:T(8,128)S(1)}, f32[8,256]{1,0:T(8,128)S(1)}, u32[]{:S(2)}, u32[]{:S(2)}) collective-permute-start(f32[8,256]{1,0:T(8,128)S(1)} %get-tuple-element.110.refs_0_), channel_id=1, source_target_pairs={{0,3},{1,2},{2,1},{3,0},{4,7},{5,6},{6,5},{7,4},{8,11},{9,10},{10,... | collective-permute-start | bytes 24584 | tf_op jit(solution)/shard_map/cond/branch_1_fun/ppermute | solution.py:296

commit v7 on v6

--- a/solution.py
+++ b/solution.py
@@ -209,33 +209,21 @@
         )
 
 
-def soft_weigh_kernel(back, starts_ref, q_ref, k_ref, sums_ref, m_ref, p_ref, acc_ref, inv_ref):
+def soft_end_kernel(starts_ref, q_ref, k_ref, v_ref, sums_ref, m_ref, soft_ref):
     rows, width = q_ref.shape
-    keys = k_ref.shape[0] - HD
-    bias = key_bias(starts_ref, rows, keys, (back - 1) * rows + keys)
-    ones = jnp.ones((keys, HD), BF16)
-    for h in range(width // HD):
-        cols = slice(h * HD, (h + 1) * HD)
+    keys = v_ref.shape[0]
+    bias = key_bias(starts_ref, rows, keys, (SPAN - 1) * rows + keys)
+    for h in range(width // HD):
+        cols = slice(h * HD, (h + 1) * HD)
+        both = slice(2 * h * HD, 2 * (h + 1) * HD)
         m_old = m_ref[:, cols]
         s = dot(q_ref[:, cols], k_ref[HD:, cols], ((1,), (1,))) * SOFT_SCALE + bias
         m = jnp.maximum(m_old, top_of(s))
         p = jnp.exp2(s - wide(m, keys)).astype(BF16)
-        shrink = jnp.exp2(m_old - m)
-        weight = sums_ref[:, (2 * h + 1) * HD : (2 * h + 2) * HD] * shrink + dot(
-            p, ones, ((1,), (0,))
-        )
-        inv = 1.0 / weight
-        p_ref[:, h * keys : (h + 1) * keys] = p
-        acc_ref[:, cols] = sums_ref[:, 2 * h * HD : (2 * h + 1) * HD] * (shrink * inv)
-        inv_ref[:, cols] = inv
-
-
-def soft_last_kernel(p_ref, v_ref, acc_ref, inv_ref, soft_ref):
-    keys = v_ref.shape[0]
-    for h in range(acc_ref.shape[1] // HD):
-        cols = slice(h * HD, (h + 1) * HD)
-        more = dot(p_ref[:, h * keys : (h + 1) * keys], v_ref[:, cols], ((1,), (0,)))
-        soft_ref[:, cols] = (acc_ref[:, cols] + more * inv_ref[:, cols]).astype(BF16)
+        total = sums_ref[:, both] * wide(jnp.exp2(m_old - m), 2 * HD) + dot(
+            p, with_ones(v_ref[:, cols]), ((1,), (0,))
+        )
+        soft_ref[:, cols] = (total[:, :HD] / total[:, HD:]).astype(BF16)
 
 
 def norm_kernel(mixture_ref, scale_ref, *refs):
@@ -355,15 +343,7 @@
         starts, lin_query, cumulative, inner, other, two,
     )
     parts = everywhere(squares)
-    weights, acc, inv = call(
-        functools.partial(soft_weigh_kernel, SPAN), "soft_weigh",
-        (
-            shape((rows, heads * reach), BF16), shape((rows, width), F32),
-            shape((rows, width), F32),
-        ),
-        starts, soft_query, two, *soft,
-    )
-    soft_out = call(soft_last_kernel, "soft_last", half, weights, v3, acc, inv)
+    soft_out = call(soft_end_kernel, "soft_end", half, starts, soft_query, two, v3, *soft)
     lin_out = call(norm_kernel, "norm", half, mixture, scale, *parts)
     return (lin_out, soft_out)
 

time: 59.8 us -> 60.2 us (level)
    ppermute x5, waiting for transfers between devices: 13.6 us -> 14.7 us  [ahead(): lax.ppermute(array, 'seq', [(i, i + by) for i in range(0, devices - by, s...]
    pallas_call x15 -> x14, Pallas kernels: 11.9 us -> 12 us  [call(): pl.pallas_call(kernel, name=name, out_shape=out_shape, in_specs=[SMEM] *...]
where the time goes in v7:
time: 60.2 us; the launch traced here: 59.8 us
  starting transfers between devices  24.9 us (41%)
  waiting for transfers between devices  20 us (33%)
  Pallas kernels  12 us (20%)
  other arithmetic  1.4 us (2%)
  between operations  1.28 us (2%)
    ppermute x5, starting transfers between devices, ahead(): lax.ppermute(array, 'seq', [(i, i + by) for i in range(0, devices - by, s...  19.5 us
    ppermute x5, waiting for transfers between devices, ahead(): lax.ppermute(array, 'seq', [(i, i + by) for i in range(0, devices - by, s...  14.7 us
    pallas_call x14, Pallas kernels, call(): pl.pallas_call(kernel, name=name, out_shape=out_shape, in_specs=[SMEM] *...  12 us
    ppermute x3, waiting for transfers between devices, swap(): return lax.ppermute(array, 'seq', [(i, i ^ 1) for i in range(devices)])  5.29 us
    ppermute x3, starting transfers between devices, swap(): return lax.ppermute(array, 'seq', [(i, i ^ 1) for i in range(devices)])  3.53 us
    ppermute x3, starting transfers between devices, everywhere(): lax.ppermute(array, 'head', [(i, i ^ by if paired else (i + by) % count)...  1.89 us
    reduce_max x1, other arithmetic, shards(): farthest = jnp.max(lasts - lax.rem(lasts, jnp.int32(rows)) - firsts)  1.4 us
  transfers between devices with their start and end apart: 11, of which 7 were waited for; matrix products, arithmetic and copies ran while one was open for 0% of the time, Pallas kernels for 18%

profile of v7, /device:TPU:0, one launch (start us, length us, event | category | flops | bytes accessed | tf_op | source)
XLA Modules:
  0.0 59.8 jit_solution(13528951057075145833)
XLA Ops:
  0.6 1.4 %fusion.3 = s32[]{:T(128)} fusion(s32[9,2]{0,1:T(2,128)} %param.22), kind=kLoop, calls=%fused_computation.5 | loop fusion | flops 89 | bytes 76 | tf_op jit(solution)/shard_map/reduce_max | solution.py:367
  2.7 57.1 %conditional.1 = (bf16[256,1024]{1,0:T(8,128)(2,1)}, bf16[256,1024]{1,0:T(8,128)(2,1)}) conditional(s32[]{:T(128)} %convert_element_type.3, (s32[9,2]{0,1:T(2,128)}, f32[256,8]{0,1:T(8,128)}, bf16[256,1024]{1,0:T(8,128)(2,1)}, bf16[256,1024]{1,0:T(8,128)(2,1)}, bf16[256,1024]{1,0:T(8,128)(2,1)}, /*index=5*/bf16[256,1024]{1,0:T(8,128)(2,1)}, ...), branch_computations={%region_1.0_spmd, %region_2.0_spmd} | conditional | bytes 30655144 | solution.py:368
  2.7 0.0 copy-start.3
  2.7 0.0 copy-start.1
  2.7 0.0 copy-start.5
  2.7 5.1 %collective-permute-start.13 = (bf16[256,1024]{1,0:T(8,128)(2,1)}, bf16[256,1024]{1,0:T(8,128)(2,1)S(1)}, u32[]{:S(2)}, u32[]{:S(2)}) collective-permute-start(bf16[256,1024]{1,0:T(8,128)(2,1)} %get-tuple-element.99.k_ref.own_ref), channel_id=1, source_target_pairs={{0,8},{4,12},{8,16},{12,20},{16,24},{20,28},{1,9},{5,13},{9,17},{1... | collective-permute-start | bytes 1572872 | tf_op jit(solution)/shard_map/cond/branch_1_fun/ppermute | solution.py:273
  7.8 1.7 %prep.3 = (s32[256,128]{1,0:T(8,128)S(1)}, s32[8,128]{1,0:T(8,128)S(1)}, f32[256,1024]{1,0:T(8,128)S(1)}, f32[8,256]{1,0:T(8,128)S(1)}) custom-call(s32[2,9]{1,0:T(2,128)} %bitcast.19, f32[8,256]{1,0:T(8,128)} %bitcast.15), custom_call_target="tpu_custom_call" | custom-call | tf_op jit(solution)/shard_map/cond/branch_1_fun/prep/pallas_call | solution.py:244
  9.6 1.8 %state.3 = (bf16[144,1024]{1,0:T(8,128)(2,1)S(1)}, f32[128,1024]{1,0:T(8,128)S(1)}, f32[8,1024]{1,0:T(8,128)S(1)}) custom-call(s32[8,128]{1,0:T(8,128)S(1)} %get-tuple-element.81.last_ref, f32[256,1024]{1,0:T(8,128)S(1)} %get-tuple-element.79.cum_ref, bf16[256,1024]{1,0:T(8,128)(2,1)} %get-tuple-element.82.k_ref, bf16[256,1024]{1,0:T(8,128)(2,1)} %get-tuple-element.83.v_ref), custom_call_target="tpu_custom_call" | custom-call | tf_op jit(solution)/shard_map/cond/branch_1_fun/state/pallas_call | solution.py:244
  11.3 0.0 copy-done.3
  11.3 3.5 %collective-permute-start.11 = (bf16[256,1024]{1,0:T(8,128)(2,1)S(1)}, bf16[256,1024]{1,0:T(8,128)(2,1)S(1)}, u32[]{:S(2)}, u32[]{:S(2)}) collective-permute-start(bf16[256,1024]{1,0:T(8,128)(2,1)S(1)} %copy-done.3), channel_id=1, source_target_pairs={{0,8},{4,12},{8,16},{12,20},{16,24},{20,28},{1,9},{5,13},{9,17},{1... | collective-permute-start | bytes 1572872 | tf_op jit(solution)/shard_map/cond/branch_1_fun/ppermute | solution.py:273
  14.8 1.6 %collective-permute-start.14 = (bf16[144,1024]{1,0:T(8,128)(2,1)S(1)}, bf16[144,1024]{1,0:T(8,128)(2,1)S(1)}, u32[]{:S(2)}, u32[]{:S(2)}) collective-permute-start(bf16[144,1024]{1,0:T(8,128)(2,1)S(1)} %get-tuple-element.84), channel_id=1, source_target_pairs={{0,4},{4,0},{8,12},{12,8},{16,20},{20,16},{24,28},{28,24},{1,5},{5... | collective-permute-start | bytes 884744 | tf_op jit(solution)/shard_map/cond/branch_1_fun/ppermute | solution.py:278
  16.4 0.0 copy-done.1
  16.4 0.0 copy-done.5
  16.4 0.9 %soft_own.3 = (f32[256,2048]{1,0:T(8,128)S(1)}, f32[256,1024]{1,0:T(8,128)S(1)}) custom-call(s32[256,128]{1,0:T(8,128)S(1)} %get-tuple-element.77.starts_ref, bf16[256,1024]{1,0:T(8,128)(2,1)S(1)} %copy-done.1, bf16[256,1024]{1,0:T(8,128)(2,1)S(1)} %copy-done.5, bf16[256,1024]{1,0:T(8,128)(2,1)S(1)} %copy-done.3), custom_call_target="tpu_custom_call" | custom-call | tf_op jit(solution)/shard_map/cond/branch_1_fun/soft_own/pallas_call | solution.py:244
  17.3 3.1 %collective-permute-done.13.k_ref.there_ref = bf16[256,1024]{1,0:T(8,128)(2,1)S(1)} collective-permute-done((bf16[256,1024]{1,0:T(8,128)(2,1)}, bf16[256,1024]{1,0:T(8,128)(2,1)S(1)}, u32[]{:S(2)}, u32[]{:S(2)}) %collective-permute-start.13) | collective-permute-done | bytes 524320 | tf_op jit(solution)/shard_map/cond/branch_1_fun/ppermute | solution.py:273
  20.5 0.0 copy-start.7
  20.5 0.0 copy-start.9
  20.5 0.0 copy-start.11
  20.5 0.0 copy-start.13
  20.5 0.0 copy-start.15
  20.5 1.6 %collective-permute-start.16 = (bf16[256,1024]{1,0:T(8,128)(2,1)S(1)}, bf16[256,1024]{1,0:T(8,128)(2,1)S(1)}, u32[]{:S(2)}, u32[]{:S(2)}) collective-permute-start(bf16[256,1024]{1,0:T(8,128)(2,1)S(1)} %pick_k.3), channel_id=1, source_target_pairs={{0,4},{4,0},{8,12},{12,8},{16,20},{20,16},{24,28},{28,24},{1,5},{5... | collective-permute-start | bytes 1572872 | tf_op jit(solution)/shard_map/cond/branch_1_fun/ppermute | solution.py:278
  22.1 2.7 %collective-permute-done.14.a_ref.other_ref = bf16[144,1024]{1,0:T(8,128)(2,1)S(1)} collective-permute-done((bf16[144,1024]{1,0:T(8,128)(2,1)S(1)}, bf16[144,1024]{1,0:T(8,128)(2,1)S(1)}, u32[]{:S(2)}, u32[]{:S(2)}) %collective-permute-start.14) | collective-permute-done | bytes 294944 | tf_op jit(solution)/shard_map/cond/branch_1_fun/ppermute | solution.py:278
  24.9 2.9 %collective-permute-start.15 = (bf16[128,1024]{1,0:T(8,128)(2,1)S(1)}, bf16[128,1024]{1,0:T(8,128)(2,1)S(1)}, u32[]{:S(2)}, u32[]{:S(2)}) collective-permute-start(bf16[128,1024]{1,0:T(8,128)(2,1)S(1)} %states.3), channel_id=1, source_target_pairs={{0,8},{8,16},{16,24},{1,9},{9,17},{17,25},{2,10},{10,18},{18,26},{... | collective-permute-start | bytes 786440 | tf_op jit(solution)/shard_map/cond/branch_1_fun/ppermute | solution.py:273
  27.7 3.8 %collective-permute-done.11.there_ref.v_ref = bf16[256,1024]{1,0:T(8,128)(2,1)S(1)} collective-permute-done((bf16[256,1024]{1,0:T(8,128)(2,1)S(1)}, bf16[256,1024]{1,0:T(8,128)(2,1)S(1)}, u32[]{:S(2)}, u32[]{:S(2)}) %collective-permute-start.11) | collective-permute-done | bytes 524320 | tf_op jit(solution)/shard_map/cond/branch_1_fun/ppermute | solution.py:273
  31.6 0.4 collective-permute-start.12
  32.0 4.0 %collective-permute-done.15.far_ref = bf16[128,1024]{1,0:T(8,128)(2,1)S(1)} collective-permute-done((bf16[128,1024]{1,0:T(8,128)(2,1)S(1)}, bf16[128,1024]{1,0:T(8,128)(2,1)S(1)}, u32[]{:S(2)}, u32[]{:S(2)}) %collective-permute-start.15) | collective-permute-done | bytes 262176 | tf_op jit(solution)/shard_map/cond/branch_1_fun/ppermute | solution.py:273
  36.0 0.0 collective-permute-done.16.k_ref
  36.1 0.2 pair.3
  36.3 4.6 %collective-permute-start.17 = (bf16[256,1024]{1,0:T(8,128)(2,1)S(1)}, bf16[256,1024]{1,0:T(8,128)(2,1)S(1)}, u32[]{:S(2)}, u32[]{:S(2)}) collective-permute-start(bf16[256,1024]{1,0:T(8,128)(2,1)S(1)} %pair.3), channel_id=1, source_target_pairs={{0,8},{4,12},{8,16},{12,20},{16,24},{20,28},{1,9},{5,13},{9,17},{1... | collective-permute-start | bytes 1572872 | tf_op jit(solution)/shard_map/cond/branch_1_fun/ppermute | solution.py:273
  40.8 0.0 copy-done.7
  40.9 0.0 copy-done.9
  40.9 0.0 copy-done.11
  40.9 1.0 %inner.3 = (f32[256,1024]{1,0:T(8,128)S(1)}, f32[256,1024]{1,0:T(8,128)S(1)}) custom-call(s32[256,128]{1,0:T(8,128)S(1)} %get-tuple-element.77.starts_ref, bf16[256,1024]{1,0:T(8,128)(2,1)S(1)} %copy-done.11, bf16[256,1024]{1,0:T(8,128)(2,1)S(1)} %copy-done.7, bf16[256,1024]{1,0:T(8,128)(2,1)S(1)} %copy-done.9, bf16[256,1024]{1,0:T(8,128)(2,1)S(1)} %copy-done.13, ...), custom_call_target="tpu_custom_call" | custom-call | tf_op jit(solution)/shard_map/cond/branch_1_fun/inner/pallas_call | solution.py:244
  41.9 1.1 %soft_2.3 = (f32[256,2048]{1,0:T(8,128)S(1)}, f32[256,1024]{1,0:T(8,128)S(1)}) custom-call(s32[256,128]{1,0:T(8,128)S(1)} %get-tuple-element.77.starts_ref, bf16[256,1024]{1,0:T(8,128)(2,1)S(1)} %copy-done.1, bf16[256,1024]{1,0:T(8,128)(2,1)S(1)} %collective-permute-done.13.k_ref.there_ref, bf16[256,1024]{1,0:T(8,128)(2,1)S(1)} %collective-permute-done.11.there_ref.v_ref, ...), custom_call_target="tpu_custom_call" | custom-call | tf_op jit(solution)/shard_map/cond/branch_1_fun/soft_2/pallas_call | solution.py:244
  43.0 2.5 %collective-permute-done.12.v_ref = bf16[256,1024]{1,0:T(8,128)(2,1)S(1)} collective-permute-done((bf16[256,1024]{1,0:T(8,128)(2,1)S(1)}, bf16[256,1024]{1,0:T(8,128)(2,1)S(1)}, u32[]{:S(2)}, u32[]{:S(2)}) %collective-permute-start.12) | collective-permute-done | bytes 524320 | tf_op jit(solution)/shard_map/cond/branch_1_fun/ppermute | solution.py:278
  45.6 3.5 %collective-permute-start.21 = (bf16[128,1024]{1,0:T(8,128)(2,1)S(1)}, bf16[128,1024]{1,0:T(8,128)(2,1)S(1)}, u32[]{:S(2)}, u32[]{:S(2)}) collective-permute-start(bf16[128,1024]{1,0:T(8,128)(2,1)S(1)} %nearest.3), channel_id=1, source_target_pairs={{0,8},{4,12},{8,16},{12,20},{16,24},{20,28},{1,9},{5,13},{9,17},{1... | collective-permute-start | bytes 786440 | tf_op jit(solution)/shard_map/cond/branch_1_fun/ppermute | solution.py:273
  49.0 1.1 %soft_1.3 = (f32[256,2048]{1,0:T(8,128)S(1)}, f32[256,1024]{1,0:T(8,128)S(1)}) custom-call(s32[256,128]{1,0:T(8,128)S(1)} %get-tuple-element.77.starts_ref, bf16[256,1024]{1,0:T(8,128)(2,1)S(1)} %copy-done.1, bf16[256,1024]{1,0:T(8,128)(2,1)S(1)} %collective-permute-done.16.k_ref, bf16[256,1024]{1,0:T(8,128)(2,1)S(1)} %collective-permute-done.12.v_ref, ...), custom_call_target="tpu_custom_call" | custom-call | tf_op jit(solution)/shard_map/cond/branch_1_fun/soft_1/pallas_call | solution.py:244
  50.2 2.8 %collective-permute-done.17.two_ref.k_ref = bf16[256,1024]{1,0:T(8,128)(2,1)S(1)} collective-permute-done((bf16[256,1024]{1,0:T(8,128)(2,1)S(1)}, bf16[256,1024]{1,0:T(8,128)(2,1)S(1)}, u32[]{:S(2)}, u32[]{:S(2)}) %collective-permute-start.17) | collective-permute-done | bytes 524320 | tf_op jit(solution)/shard_map/cond/branch_1_fun/ppermute | solution.py:273
  53.0 0.7 %cross.3 = (f32[256,1024]{1,0:T(8,128)S(1)}, f32[8,256]{1,0:T(8,128)S(1)}) custom-call(s32[256,128]{1,0:T(8,128)S(1)} %get-tuple-element.77.starts_ref, bf16[256,1024]{1,0:T(8,128)(2,1)S(1)} %copy-done.11, f32[256,1024]{1,0:T(8,128)S(1)} %get-tuple-element.79.cum_ref, f32[256,1024]{1,0:T(8,128)S(1)} %get-tuple-element.96.inner_ref, ...), custom_call_target="tpu_custom_call" | custom-call | tf_op jit(solution)/shard_map/cond/branch_1_fun/cross/pallas_call | solution.py:244
  53.7 0.0 collective-permute-start.18
  53.7 1.6 %collective-permute-start.19 = (f32[8,256]{1,0:T(8,128)S(1)}, f32[8,256]{1,0:T(8,128)S(1)}, u32[]{:S(2)}, u32[]{:S(2)}) collective-permute-start(f32[8,256]{1,0:T(8,128)S(1)} %get-tuple-element.107.refs_0_), channel_id=1, source_target_pairs={{0,2},{1,3},{2,0},{3,1},{4,6},{5,7},{6,4},{7,5},{8,10},{9,11},{10,... | collective-permute-start | bytes 24584 | tf_op jit(solution)/shard_map/cond/branch_1_fun/ppermute | solution.py:284
  55.3 0.3 collective-permute-start.20
  55.6 0.9 %collective-permute-done.21.v_ref = bf16[128,1024]{1,0:T(8,128)(2,1)S(1)} collective-permute-done((bf16[128,1024]{1,0:T(8,128)(2,1)S(1)}, bf16[128,1024]{1,0:T(8,128)(2,1)S(1)}, u32[]{:S(2)}, u32[]{:S(2)}) %collective-permute-start.21) | collective-permute-done | bytes 262176 | tf_op jit(solution)/shard_map/cond/branch_1_fun/ppermute | solution.py:273
  56.5 2.2 %soft_end.3 = bf16[256,1024]{1,0:T(8,128)(2,1)} custom-call(s32[256,128]{1,0:T(8,128)S(1)} %get-tuple-element.77.starts_ref, bf16[256,1024]{1,0:T(8,128)(2,1)S(1)} %copy-done.1, bf16[256,1024]{1,0:T(8,128)(2,1)S(1)} %collective-permute-done.17.two_ref.k_ref, bf16[128,1024]{1,0:T(8,128)(2,1)S(1)} %collective-permute-done.21.v_ref, ...), custom_call_target="tpu_custom_call" | custom-call | tf_op jit(solution)/shard_map/cond/branch_1_fun/soft_end/pallas_call | solution.py:244
  58.7 0.0 collective-permute-done.18.refs_1_
  58.7 0.0 collective-permute-done.19.refs_2_
  58.7 0.0 collective-permute-done.20.refs_3_
  58.7 1.1 %norm.3 = bf16[256,1024]{1,0:T(8,128)(2,1)} custom-call(f32[256,1024]{1,0:T(8,128)S(1)} %get-tuple-element.105.mixture_ref, f32[256,1024]{1,0:T(8,128)S(1)} %get-tuple-element.106.scale_ref, f32[8,256]{1,0:T(8,128)S(1)} %get-tuple-element.107.refs_0_, f32[8,256]{1,0:T(8,128)S(1)} %collective-permute-done.18.refs_1_, ...), custom_call_target="tpu_custom_call" | custom-call | tf_op jit(solution)/shard_map/cond/branch_1_fun/norm/pallas_call | solution.py:244
  (6 shorter events, 0.1 us)
Async XLA Ops:
  2.7 8.6 %copy-start.3 = (bf16[256,1024]{1,0:T(8,128)(2,1)S(1)}, bf16[256,1024]{1,0:T(8,128)(2,1)}, u32[]{:S(2)}) copy-start(bf16[256,1024]{1,0:T(8,128)(2,1)} %get-tuple-element.85.own_ref.v_ref) | copy-start | bytes 1572868 | tf_op jit(solution)/shard_map/cond
  2.7 13.7 %copy-start.1 = (bf16[256,1024]{1,0:T(8,128)(2,1)S(1)}, bf16[256,1024]{1,0:T(8,128)(2,1)}, u32[]{:S(2)}) copy-start(bf16[256,1024]{1,0:T(8,128)(2,1)} %get-tuple-element.86.q_ref) | copy-start | bytes 1572868 | tf_op jit(solution)/shard_map/cond
  2.7 13.7 %copy-start.5 = (bf16[256,1024]{1,0:T(8,128)(2,1)S(1)}, bf16[256,1024]{1,0:T(8,128)(2,1)}, u32[]{:S(2)}) copy-start(bf16[256,1024]{1,0:T(8,128)(2,1)} %get-tuple-element.99.k_ref.own_ref) | copy-start | bytes 1572868 | tf_op jit(solution)/shard_map/cond
  2.7 17.7 %collective-permute-start.13 = (bf16[256,1024]{1,0:T(8,128)(2,1)}, bf16[256,1024]{1,0:T(8,128)(2,1)S(1)}, u32[]{:S(2)}, u32[]{:S(2)}) collective-permute-start(bf16[256,1024]{1,0:T(8,128)(2,1)} %get-tuple-element.99.k_ref.own_ref), channel_id=1, source_target_pairs={{0,8},{4,12},{8,16},{12,20},{16,24},{20,28},{1,9},{5,13},{9,17},{1... | collective-permute-start | bytes 1572872 | tf_op jit(solution)/shard_map/cond/branch_1_fun/ppermute | solution.py:273
  11.3 20.2 %collective-permute-start.11 = (bf16[256,1024]{1,0:T(8,128)(2,1)S(1)}, bf16[256,1024]{1,0:T(8,128)(2,1)S(1)}, u32[]{:S(2)}, u32[]{:S(2)}) collective-permute-start(bf16[256,1024]{1,0:T(8,128)(2,1)S(1)} %copy-done.3), channel_id=1, source_target_pairs={{0,8},{4,12},{8,16},{12,20},{16,24},{20,28},{1,9},{5,13},{9,17},{1... | collective-permute-start | bytes 1572872 | tf_op jit(solution)/shard_map/cond/branch_1_fun/ppermute | solution.py:273
  14.8 10.0 %collective-permute-start.14 = (bf16[144,1024]{1,0:T(8,128)(2,1)S(1)}, bf16[144,1024]{1,0:T(8,128)(2,1)S(1)}, u32[]{:S(2)}, u32[]{:S(2)}) collective-permute-start(bf16[144,1024]{1,0:T(8,128)(2,1)S(1)} %get-tuple-element.84), channel_id=1, source_target_pairs={{0,4},{4,0},{8,12},{12,8},{16,20},{20,16},{24,28},{28,24},{1,5},{5... | collective-permute-start | bytes 884744 | tf_op jit(solution)/shard_map/cond/branch_1_fun/ppermute | solution.py:278
  20.5 20.4 %copy-start.7 = (bf16[256,1024]{1,0:T(8,128)(2,1)S(1)}, bf16[256,1024]{1,0:T(8,128)(2,1)}, u32[]{:S(2)}) copy-start(bf16[256,1024]{1,0:T(8,128)(2,1)} %get-tuple-element.82.k_ref) | copy-start | bytes 1572868 | tf_op jit(solution)/shard_map/cond
  20.5 20.4 %copy-start.9 = (bf16[256,1024]{1,0:T(8,128)(2,1)S(1)}, bf16[256,1024]{1,0:T(8,128)(2,1)}, u32[]{:S(2)}) copy-start(bf16[256,1024]{1,0:T(8,128)(2,1)} %get-tuple-element.83.v_ref) | copy-start | bytes 1572868 | tf_op jit(solution)/shard_map/cond
  20.5 20.4 %copy-start.11 = (bf16[256,1024]{1,0:T(8,128)(2,1)S(1)}, bf16[256,1024]{1,0:T(8,128)(2,1)}, u32[]{:S(2)}) copy-start(bf16[256,1024]{1,0:T(8,128)(2,1)} %get-tuple-element.78.q_ref) | copy-start | bytes 1572868 | tf_op jit(solution)/shard_map/cond
  20.5 20.4 %copy-start.13 = (bf16[256,1024]{1,0:T(8,128)(2,1)S(1)}, bf16[256,1024]{1,0:T(8,128)(2,1)}, u32[]{:S(2)}) copy-start(bf16[256,1024]{1,0:T(8,128)(2,1)} %get-tuple-element.92.gate_ref) | copy-start | bytes 1572868 | tf_op jit(solution)/shard_map/cond
  20.5 20.4 %copy-start.15 = (f32[1024]{0:T(1024)S(1)}, f32[1024]{0:T(1024)}, u32[]{:S(2)}) copy-start(f32[1024]{0:T(1024)} %get-tuple-element.93) | copy-start | bytes 12292 | tf_op jit(solution)/shard_map/cond
  20.5 15.5 %collective-permute-start.16 = (bf16[256,1024]{1,0:T(8,128)(2,1)S(1)}, bf16[256,1024]{1,0:T(8,128)(2,1)S(1)}, u32[]{:S(2)}, u32[]{:S(2)}) collective-permute-start(bf16[256,1024]{1,0:T(8,128)(2,1)S(1)} %pick_k.3), channel_id=1, source_target_pairs={{0,4},{4,0},{8,12},{12,8},{16,20},{20,16},{24,28},{28,24},{1,5},{5... | collective-permute-start | bytes 1572872 | tf_op jit(solution)/shard_map/cond/branch_1_fun/ppermute | solution.py:278
  24.9 11.2 %collective-permute-start.15 = (bf16[128,1024]{1,0:T(8,128)(2,1)S(1)}, bf16[128,1024]{1,0:T(8,128)(2,1)S(1)}, u32[]{:S(2)}, u32[]{:S(2)}) collective-permute-start(bf16[128,1024]{1,0:T(8,128)(2,1)S(1)} %states.3), channel_id=1, source_target_pairs={{0,8},{8,16},{16,24},{1,9},{9,17},{17,25},{2,10},{10,18},{18,26},{... | collective-permute-start | bytes 786440 | tf_op jit(solution)/shard_map/cond/branch_1_fun/ppermute | solution.py:273
  31.6 14.0 %collective-permute-start.12 = (bf16[256,1024]{1,0:T(8,128)(2,1)S(1)}, bf16[256,1024]{1,0:T(8,128)(2,1)S(1)}, u32[]{:S(2)}, u32[]{:S(2)}) collective-permute-start(bf16[256,1024]{1,0:T(8,128)(2,1)S(1)} %pick_v.3), channel_id=1, source_target_pairs={{0,4},{4,0},{8,12},{12,8},{16,20},{20,16},{24,28},{28,24},{1,5},{5... | collective-permute-start | bytes 1572872 | tf_op jit(solution)/shard_map/cond/branch_1_fun/ppermute | solution.py:278
  36.3 16.7 %collective-permute-start.17 = (bf16[256,1024]{1,0:T(8,128)(2,1)S(1)}, bf16[256,1024]{1,0:T(8,128)(2,1)S(1)}, u32[]{:S(2)}, u32[]{:S(2)}) collective-permute-start(bf16[256,1024]{1,0:T(8,128)(2,1)S(1)} %pair.3), channel_id=1, source_target_pairs={{0,8},{4,12},{8,16},{12,20},{16,24},{20,28},{1,9},{5,13},{9,17},{1... | collective-permute-start | bytes 1572872 | tf_op jit(solution)/shard_map/cond/branch_1_fun/ppermute | solution.py:273
  45.6 11.0 %collective-permute-start.21 = (bf16[128,1024]{1,0:T(8,128)(2,1)S(1)}, bf16[128,1024]{1,0:T(8,128)(2,1)S(1)}, u32[]{:S(2)}, u32[]{:S(2)}) collective-permute-start(bf16[128,1024]{1,0:T(8,128)(2,1)S(1)} %nearest.3), channel_id=1, source_target_pairs={{0,8},{4,12},{8,16},{12,20},{16,24},{20,28},{1,9},{5,13},{9,17},{1... | collective-permute-start | bytes 786440 | tf_op jit(solution)/shard_map/cond/branch_1_fun/ppermute | solution.py:273
  53.7 5.0 %collective-permute-start.18 = (f32[8,256]{1,0:T(8,128)S(1)}, f32[8,256]{1,0:T(8,128)S(1)}, u32[]{:S(2)}, u32[]{:S(2)}) collective-permute-start(f32[8,256]{1,0:T(8,128)S(1)} %get-tuple-element.107.refs_0_), channel_id=1, source_target_pairs={{0,1},{1,0},{2,3},{3,2},{4,5},{5,4},{6,7},{7,6},{8,9},{9,8},{10,11... | collective-permute-start | bytes 24584 | tf_op jit(solution)/shard_map/cond/branch_1_fun/ppermute | solution.py:284
  53.7 5.0 %collective-permute-start.19 = (f32[8,256]{1,0:T(8,128)S(1)}, f32[8,256]{1,0:T(8,128)S(1)}, u32[]{:S(2)}, u32[]{:S(2)}) collective-permute-start(f32[8,256]{1,0:T(8,128)S(1)} %get-tuple-element.107.refs_0_), channel_id=1, source_target_pairs={{0,2},{1,3},{2,0},{3,1},{4,6},{5,7},{6,4},{7,5},{8,10},{9,11},{10,... | collective-permute-start | bytes 24584 | tf_op jit(solution)/shard_map/cond/branch_1_fun/ppermute | solution.py:284
  55.3 3.4 %collective-permute-start.20 = (f32[8,256]{1,0:T(8,128)S(1)}, f32[8,256]{1,0:T(8,128)S(1)}, u32[]{:S(2)}, u32[]{:S(2)}) collective-permute-start(f32[8,256]{1,0:T(8,128)S(1)} %get-tuple-element.107.refs_0_), channel_id=1, source_target_pairs={{0,3},{1,2},{2,1},{3,0},{4,7},{5,6},{6,5},{7,4},{8,11},{9,10},{10,... | collective-permute-start | bytes 24584 | tf_op jit(solution)/shard_map/cond/branch_1_fun/ppermute | solution.py:284
